TPU v7x, 32 devices: a whole 2x2x4 slice. The times are simulated.
32 devices in a mesh: tm: 16 (over z, x, core), rows: 2 (over y).
Axes of the slice: x: 2, y: 2, z: 4, core: 2. Of those that a mesh axis runs over, the one named last changes fastest.
Arguments:
- frames: bfloat16 [32, 16, 128, 128], P('tm', 'rows'), may hold values from -6 to 6
- conv_fine: bfloat16 [3, 3, 384, 128], replicated, may hold values from -0.109375 to 0.109375
- conv_down: bfloat16 [3, 384, 256], replicated, may hold values from -0.1875 to 0.1875
- conv_coarse: bfloat16 [3, 3, 768, 256], replicated, may hold values from -0.078125 to 0.078125
Outputs:
- coarse_out: bfloat16 [16, 8, 64, 256], P('tm', 'rows')
All inputs are finite; a program needn't handle non-finite values.
Results may differ from a plain program's by a relative error of at most 0.014.
Values may be sent and summed in bfloat16 or wider, within the bound.
No kernel may reach another device: no remote copies, remote signals or barrier semaphores. Data moves between devices by JAX's collectives and lax.ppermute only.
A program may use at most 64 MiB of HBM per device.

v0:
```python
import functools

import jax
import jax.numpy as jnp
from jax import lax
from jax.experimental import pallas as pl
from jax.experimental.pallas import tpu as pltpu
from jax.sharding import PartitionSpec as P


F32 = jnp.float32
BF16 = jnp.bfloat16


def moved(value, steps, hop):
    tm, rows = lax.axis_size("tm"), lax.axis_size("rows")
    pairs = [
        (t * rows + r, (t + steps) * rows + r + hop)
        for t in range(tm - steps)
        for r in range(rows)
        if 0 <= r + hop < rows
    ]
    return lax.ppermute(value, ("tm", "rows"), pairs)


def ring(value, steps):
    tm = lax.axis_size("tm")
    return lax.ppermute(value, "tm", [(t, (t + steps) % tm) for t in range(tm)])


def swapped(value, steps):
    tm = lax.axis_size("tm")
    pairs = [(t * 2 + r, (t + steps) * 2 + 1 - r) for t in range(tm - steps) for r in range(2)]
    return lax.ppermute(value, ("tm", "rows"), pairs)


def paired(value):
    return lax.ppermute(value, "tm", [(t, t ^ 1) for t in range(lax.axis_size("tm"))])


def has_above():
    return lax.axis_index("rows") > 0


def has_below():
    return lax.axis_index("rows") < lax.axis_size("rows") - 1


def has_earlier(steps):
    return lax.axis_index("tm") >= steps


def pace_kernel(out):
    out[...] = jnp.zeros_like(out)


def edge_kernel(_, cells, out):
    width = out.shape[1]
    first = (1 - lax.axis_index("rows")) * (cells.shape[1] - width)
    out[...] = cells[:, pl.ds(first, width)]


def frame_rims(pace, frames):
    rows = frames.shape[1]
    if lax.axis_size("rows") == 2:
        sent = call(
            edge_kernel,
            jax.ShapeDtypeStruct((frames.shape[0], 2, *frames.shape[2:]), BF16),
            [],
            0,
            (pace, frames),
        )
        return [(both, both) for both in (swapped(sent, 0), swapped(sent, 1))]
    head, tail = frames[:, :2], frames[:, rows - 1 :]
    return [(moved(tail, steps, 1), moved(head, steps, -1)) for steps in (0, 1)]


def column_shift(value, cols, steps):
    size = value.shape[0]
    column = lax.broadcasted_iota(jnp.int32, value.shape, 0) % cols
    edge = 0 if steps > 0 else cols - 1
    return jnp.where(column == edge, 0.0, pltpu.roll(value, steps % size, 0))


def shifted_columns(flat, cols):
    wide = flat.astype(F32)
    return column_shift(wide, cols, 1).astype(BF16), column_shift(wide, cols, -1).astype(BF16)


def tap_matrix(weight, first_tap, row_taps, e, channels):
    zero = jnp.zeros((channels, channels), BF16)

    def pick(tap, b):
        return weight[tap, b, e * channels : (e + 1) * channels] if 0 <= tap <= 2 else zero

    return jnp.concatenate(
        [
            jnp.concatenate([pick(first_tap + f, b), pick(first_tap + f - 1, b)], axis=1)
            for f in range(2)
            for b in row_taps
        ],
        axis=0,
    )


def fine_rows(row, outs, row_taps, weight, first_tap):
    channels = weight.shape[-1]
    some = next(x for f in range(2) for r in outs for b in row_taps if (x := row(f, r - 1 + b)) is not None)
    cols = some.shape[0]
    zero = jnp.zeros((cols, channels), BF16)

    def cell(f, i):
        found = row(f, i)
        return zero if found is None else found

    left = jnp.concatenate(
        [
            jnp.concatenate([cell(f, r - 1 + b) for f in range(2) for b in row_taps], axis=1)
            for r in outs
        ],
        axis=0,
    )
    sums = [
        jnp.dot(
            left, tap_matrix(weight, first_tap, row_taps, e, channels), preferred_element_type=F32
        )
        for e in range(3)
    ]
    return sums[1] + column_shift(sums[0], cols, 1) + column_shift(sums[2], cols, -1)


def chunks_of(count):
    size = next(c for c in (3, 2, 1) if count % c == 0)
    return [range(i, i + size) for i in range(0, count, size)]


def fine_own_kernel(frames, weight, out):
    _, rows, cols, _ = frames.shape

    def row(f, i):
        return frames[f, i] if 0 <= i < rows else None

    for outs in chunks_of(rows + 1):
        out[outs[0] * cols : (outs[-1] + 1) * cols] = fine_rows(row, outs, range(3), weight, 2)


def halo_row(above, below, rows):
    def row(f, i):
        if i == -1:
            cells, have = above[f, above.shape[1] - 1], has_above()
        elif i >= rows:
            cells, have = below[f, i - rows], has_below()
        else:
            return None
        return jnp.where(have, cells, jnp.zeros_like(cells))

    return row


def halo_sum(above, below, weight, first_tap, rows):
    row = halo_row(above, below, rows)
    return jnp.concatenate(
        [
            fine_rows(row, [0], [0], weight, first_tap),
            fine_rows(row, [rows - 1, rows], [1, 2], weight, first_tap),
        ],
        axis=0,
    )


def fine_halo_kernel(above, below, weight, out, *, rows):
    out[...] = halo_sum(above, below, weight, 2, rows)


def silu(v):
    return v / (1.0 + jnp.exp(-v))


def fine_rest_kernel(frames, weight, own, halo, out):
    _, rows, cols, _ = frames.shape

    def row(f, i):
        return frames[f, i] if 0 <= i < rows else None

    for outs in chunks_of(rows + 1):
        total = jnp.where(has_earlier(1), fine_rows(row, outs, range(3), weight, 0), 0.0)
        for i, r in enumerate(outs):
            line = total[i * cols : (i + 1) * cols] + own[r * cols : (r + 1) * cols]
            for k, halo_r in enumerate((0, rows - 1, rows)):
                if r == halo_r:
                    line = line + halo[k * cols : (k + 1) * cols]
            out[r * cols : (r + 1) * cols] = line


def pool(sums):
    channels = sums.shape[1] // 2
    fine = silu(sums).astype(BF16).astype(F32)
    return ((fine[:, :channels] + fine[:, channels:]) * 0.5).astype(BF16).astype(F32)


def down_conv(pooled, half_rows, half_cols, down):
    strips = []
    for p in range(half_rows):
        pieces = [
            pooled[2 * p + b, pl.ds(e, half_cols, stride=2), :].astype(BF16)
            for b in range(3)
            for e in range(3)
        ]
        strips.append(jnp.concatenate(pieces, axis=1))
    left = jnp.concatenate(strips, axis=0)
    right = down[...].reshape(-1, down.shape[-1])
    return jnp.dot(left, right, preferred_element_type=F32).astype(BF16)


def ends_kernel(above, below, weight, sums, down, out, halo, pooled):
    cols = above.shape[2]
    rows = sums.shape[0] // cols - 1
    added = halo_sum(above, below, weight, 0, rows)
    halo[...] = added
    channels = pooled.shape[2]
    pooled[:, cols:] = jnp.zeros((3, pooled.shape[1] - cols, channels), F32)
    zero = jnp.zeros((cols, added.shape[1]), F32)
    if out.shape[0] == 1:
        starts = [(jnp.where(has_above(), 0, rows - 2), added)]
    else:
        first = jnp.concatenate([added[:cols], zero, zero], axis=0)
        last = jnp.concatenate([zero, added[cols:]], axis=0)
        starts = [(0, first), (rows - 2, last)]
    for side, (start, more) in enumerate(starts):
        begin = pl.multiple_of(start * cols, cols)
        mean = pool(sums[pl.ds(begin, 3 * cols), :] + more)
        for i in range(3):
            line = mean[i * cols : (i + 1) * cols]
            if side == 1 and i == 2:
                line = jnp.where(has_below(), line, 0.0)
            pooled[i, :cols] = line
        out[side] = down_conv(pooled, 1, cols // 2, down)


def reduce_kernel(sums, halo, down, out, pooled):
    _, half_rows, half_cols, _ = out.shape
    rows, cols = 2 * half_rows, 2 * half_cols
    channels = pooled.shape[2]
    pooled[:, cols:] = jnp.zeros((rows + 1, pooled.shape[1] - cols, channels), F32)
    for r in range(rows + 1):
        line = sums[r * cols : (r + 1) * cols]
        for k, halo_r in enumerate((0, rows - 1, rows)):
            if r == halo_r:
                line = line + halo[k * cols : (k + 1) * cols]
        mean = pool(line)
        if r == rows:
            mean = jnp.where(has_below(), mean, 0.0)
        pooled[r, :cols] = mean
    out[...] = down_conv(pooled, half_rows, half_cols, down).reshape(out.shape)


def coarse_sum(field, rim, weight, a):
    _, rows, cols, channels = field.shape
    zero = jnp.zeros((cols, channels), BF16)
    flat = jnp.concatenate(
        [
            jnp.where(has_above(), rim[0], zero),
            field.reshape(rows * cols, channels),
            jnp.where(has_below(), rim[rim.shape[0] - 1], zero),
        ],
        axis=0,
    )
    left, right = shifted_columns(flat, cols)
    taps = jnp.concatenate([left, flat, right], axis=1)
    total = None
    for b in range(3):
        part = jnp.dot(
            taps[b * cols : (b + rows) * cols], weight[a, b], preferred_element_type=F32
        )
        total = part if total is None else total + part
    return total


def coarse_first_kernel(field, rim, weight, out):
    out[...] = coarse_sum(field[...], rim[...], weight, 2)


def coarse_next_kernel(field, rim, weight, total, out):
    part = coarse_sum(field[...], rim[...], weight, 0)
    out[...] = total[...] + jnp.where(has_earlier(2), part, 0.0)


def coarse_last_kernel(direct, direct_rim, relayed, relayed_rim, weight, total, out):
    odd = lax.axis_index("tm") % 2 == 1
    field = jnp.where(odd, direct[...], relayed[...])
    rim = jnp.where(odd, direct_rim[...], relayed_rim[...])
    part = coarse_sum(field, rim, weight, 1)
    total = total[...] + jnp.where(has_earlier(1), part, 0.0)
    out[...] = silu(total).astype(BF16).reshape(out.shape)


def call(kernel, out_shape, scratch, flops, args):
    size = sum(a.size * a.dtype.itemsize for a in args)
    return pl.pallas_call(
        kernel,
        out_shape=out_shape,
        in_specs=[pl.BlockSpec(memory_space=pltpu.VMEM)] * len(args),
        out_specs=jax.tree.map(lambda _: pl.BlockSpec(memory_space=pltpu.VMEM), out_shape),
        scratch_shapes=scratch,
        cost_estimate=pl.CostEstimate(flops=flops, bytes_accessed=size, transcendentals=0),
        compiler_params=pltpu.CompilerParams(vmem_limit_bytes=20 * 1024 * 1024),
    )(*args)


def local(frames, conv_fine, conv_down, conv_coarse):
    _, rows, cols, channels = frames.shape
    wide = conv_down.shape[-1]
    strips, times = lax.axis_size("rows"), lax.axis_size("tm")
    pace = call(pace_kernel, jax.ShapeDtypeStruct((8, 128), F32), [], 4 * 10**9, ())

    earlier = ring(frames, 1)
    (above, below), (above_1, below_1) = frame_rims(pace, frames)
    size = (rows + 1) * cols
    pair = jax.ShapeDtypeStruct((size, 2 * channels), F32)
    flops = 2 * size * 18 * channels * 2 * channels
    own = call(fine_own_kernel, pair, [], flops, (frames, conv_fine))
    halo = call(
        functools.partial(fine_halo_kernel, rows=rows),
        jax.ShapeDtypeStruct((3 * cols, 2 * channels), F32),
        [],
        flops // 3,
        (above, below, conv_fine),
    )
    half_rows, half_cols = rows // 2, cols // 2
    shape = jax.ShapeDtypeStruct((1, half_rows, half_cols, wide), BF16)
    sides = 1 if strips == 2 else 2
    halo_sums = jax.ShapeDtypeStruct((3 * cols, 2 * channels), F32)
    fine_sums = call(fine_rest_kernel, pair, [], flops, (earlier, conv_fine, own, halo))
    above_1, below_1, fine_sums = lax.optimization_barrier((above_1, below_1, fine_sums))
    ends, halo_1 = call(
        ends_kernel,
        (jax.ShapeDtypeStruct((sides, half_cols, wide), BF16), halo_sums),
        [pltpu.VMEM((3, cols + 8, channels), F32)],
        flops // 3,
        (above_1, below_1, conv_fine, fine_sums, conv_down),
    )
    field = call(
        reduce_kernel,
        shape,
        [pltpu.VMEM((rows + 1, cols + 8, channels), F32)],
        flops // 3,
        (fine_sums, halo_1, conv_down),
    )
    field_2 = moved(field, 2, 0)
    if sides == 1:
        rim = swapped(ends, 0)
    else:
        rim = jnp.concatenate([moved(ends[1:], 0, 1), moved(ends[:1], 0, -1)], axis=0)
    rim_2 = moved(rim, 2, 0)
    sums = jax.ShapeDtypeStruct((half_rows * half_cols, wide), F32)
    flops = 2 * half_rows * half_cols * 9 * wide * wide
    total = call(coarse_first_kernel, sums, [], flops, (field, rim, conv_coarse))
    if times % 2 == 0:
        direct, direct_rim = paired(field), paired(rim)
    else:
        direct, direct_rim = ring(field, 1), ring(rim, 1)
    field_2, rim_2, total, direct, direct_rim = lax.optimization_barrier(
        (field_2, rim_2, total, direct, direct_rim)
    )
    if times % 2 == 0:
        relayed, relayed_rim = paired(field_2), paired(rim_2)
    else:
        relayed, relayed_rim = direct, direct_rim
    total = call(coarse_next_kernel, sums, [], flops, (field_2, rim_2, conv_coarse, total))
    return call(
        coarse_last_kernel,
        shape,
        [],
        flops,
        (direct, direct_rim, relayed, relayed_rim, conv_coarse, total),
    )


def solution(mesh):
    placed = (P("tm", "rows", None, None), P(), P(), P())
    return jax.shard_map(local, mesh=mesh, in_specs=placed, out_specs=P("tm", "rows", None, None), check_vma=False)
```

profile of v0, /device:TPU:0, one launch (start us, length us, event | category | flops | bytes accessed | tf_op | source)
XLA Modules:
  0.0 30.0 jit_solution(1912727164796850477)
XLA Ops:
  0.0 0.0 copy-start.3
  0.0 0.0 copy-start.2
  0.0 0.5 %collective-permute-start.1 = (bf16[2,8,128,128]{3,2,1,0:T(8,128)(2,1)}, bf16[2,8,128,128]{3,2,1,0:T(8,128)(2,1)S(1)}, u32[]{:S(2)}, u32[]{:S(2)}) collective-permute-start(bf16[2,8,128,128]{3,2,1,0:T(8,128)(2,1)} %frames.1), channel_id=1, source_target_pairs={{0,2},{2,4},{4,6},{6,8},{8,10},{10,12},{12,14},{14,16},{16,18},{18... | collective-permute-start | bytes 1572872 | tf_op jit(solution)/shard_map/ppermute | solution.py:28
  0.5 0.5 %copy-done.3 = bf16[2,8,128,128]{3,2,1,0:T(8,128)(2,1)S(1)} copy-done((bf16[2,8,128,128]{3,2,1,0:T(8,128)(2,1)S(1)}, bf16[2,8,128,128]{3,2,1,0:T(8,128)(2,1)}, u32[]{:S(2)}) %copy-start.3) | copy-done | bytes 524312
  1.1 3.1 %collective-permute-start.2 = (bf16[2,2,128,128]{3,2,1,0:T(8,128)(2,1)S(1)}, bf16[2,2,128,128]{3,2,1,0:T(8,128)(2,1)S(1)}, u32[]{:S(2)}, u32[]{:S(2)}) collective-permute-start(bf16[2,2,128,128]{3,2,1,0:T(8,128)(2,1)S(1)} %shard_map.47), channel_id=1, source_target_pairs={{0,1},{1,0},{2,3},{3,2},{4,5},{5,4},{6,7},{7,6},{8,9},{9,8},{10,11... | collective-permute-start | bytes 393224 | tf_op jit(solution)/shard_map/ppermute | solution.py:34
  4.1 2.3 %collective-permute-start = (bf16[2,2,128,128]{3,2,1,0:T(8,128)(2,1)S(1)}, bf16[2,2,128,128]{3,2,1,0:T(8,128)(2,1)S(1)}, u32[]{:S(2)}, u32[]{:S(2)}) collective-permute-start(bf16[2,2,128,128]{3,2,1,0:T(8,128)(2,1)S(1)} %shard_map.47), channel_id=1, source_target_pairs={{0,3},{1,2},{2,5},{3,4},{4,7},{5,6},{6,9},{7,8},{8,11},{9,10},{10,... | collective-permute-start | bytes 393224 | tf_op jit(solution)/shard_map/ppermute | solution.py:34
  6.4 0.0 copy-done.2
  6.4 1.5 %shard_map.48.own = f32[1152,256]{1,0:T(8,128)S(1)} custom-call(bf16[2,8,128,128]{3,2,1,0:T(8,128)(2,1)S(1)} %copy-done.3, bf16[3,3,384,128]{3,2,1,0:T(8,128)(2,1)S(1)} %copy-done.2), custom_call_target="tpu_custom_call" | custom-call | flops 1358954496 | bytes 1409024 | tf_op jit(solution)/shard_map/pallas_call | solution.py:299
  8.0 0.4 %collective-permute-done.2.above.below = bf16[2,2,128,128]{3,2,1,0:T(8,128)(2,1)S(1)} collective-permute-done((bf16[2,2,128,128]{3,2,1,0:T(8,128)(2,1)S(1)}, bf16[2,2,128,128]{3,2,1,0:T(8,128)(2,1)S(1)}, u32[]{:S(2)}, u32[]{:S(2)}) %collective-permute-start.2) | collective-permute-done | bytes 131104 | tf_op jit(solution)/shard_map/ppermute | solution.py:34
  8.4 0.4 %shard_map.49.halo = f32[384,256]{1,0:T(8,128)S(1)} custom-call(bf16[2,2,128,128]{3,2,1,0:T(8,128)(2,1)S(1)} %collective-permute-done.2.above.below, bf16[2,2,128,128]{3,2,1,0:T(8,128)(2,1)S(1)} %collective-permute-done.2.above.below, bf16[3,3,384,128]{3,2,1,0:T(8,128)(2,1)S(1)} %copy-done.2), custom_call_target="tpu_custom_call" | custom-call | flops 452984832 | bytes 1146880 | tf_op jit(solution)/shard_map/pallas_call | solution.py:299
  8.8 0.0 copy-start.1
  8.8 3.8 %collective-permute-done.1.frames = bf16[2,8,128,128]{3,2,1,0:T(8,128)(2,1)S(1)} collective-permute-done((bf16[2,8,128,128]{3,2,1,0:T(8,128)(2,1)}, bf16[2,8,128,128]{3,2,1,0:T(8,128)(2,1)S(1)}, u32[]{:S(2)}, u32[]{:S(2)}) %collective-permute-start.1) | collective-permute-done | bytes 524320 | tf_op jit(solution)/shard_map/ppermute | solution.py:28
  12.6 1.5 %shard_map.50.sums = f32[1152,256]{1,0:T(8,128)S(1)} custom-call(bf16[2,8,128,128]{3,2,1,0:T(8,128)(2,1)S(1)} %collective-permute-done.1.frames, bf16[3,3,384,128]{3,2,1,0:T(8,128)(2,1)S(1)} %copy-done.2, f32[1152,256]{1,0:T(8,128)S(1)} %shard_map.48.own, f32[384,256]{1,0:T(8,128)S(1)} %shard_map.49.halo), custom_call_target="tpu_custom_call" | custom-call | flops 1358954496 | bytes 2981888 | tf_op jit(solution)/shard_map/pallas_call | solution.py:299
  14.1 0.0 collective-permute-done.above.below
  14.2 0.0 copy-done.1
  14.2 0.0 copy-start
  14.2 0.7 %shard_map.51 = (bf16[1,64,256]{2,1,0:T(8,128)(2,1)S(1)}, f32[384,256]{1,0:T(8,128)S(1)}) custom-call(bf16[2,2,128,128]{3,2,1,0:T(8,128)(2,1)S(1)} %collective-permute-done.above.below, bf16[2,2,128,128]{3,2,1,0:T(8,128)(2,1)S(1)} %collective-permute-done.above.below, bf16[3,3,384,128]{3,2,1,0:T(8,128)(2,1)S(1)} %copy-done.2, ...), custom_call_target="tpu_custom_call" | custom-call | flops 452984832 | bytes 2916352 | tf_op jit(solution)/shard_map/pallas_call | solution.py:299
  14.9 0.6 %shard_map.52.field = bf16[1,4,64,256]{3,2,1,0:T(8,128)(2,1)S(1)} custom-call(f32[1152,256]{1,0:T(8,128)S(1)} %shard_map.50.sums, f32[384,256]{1,0:T(8,128)S(1)} %get-tuple-element.18.halo, bf16[3,384,256]{2,1,0:T(8,128)(2,1)S(1)} %copy-done.1), custom_call_target="tpu_custom_call" | custom-call | flops 452984832 | bytes 2162688 | tf_op jit(solution)/shard_map/pallas_call | solution.py:299
  15.5 0.1 collective-permute-start.6
  15.6 1.9 %collective-permute-start.3 = (bf16[1,4,64,256]{3,2,1,0:T(8,128)(2,1)S(1)}, bf16[1,4,64,256]{3,2,1,0:T(8,128)(2,1)S(1)}, u32[]{:S(2)}, u32[]{:S(2)}) collective-permute-start(bf16[1,4,64,256]{3,2,1,0:T(8,128)(2,1)S(1)} %shard_map.52.field), channel_id=1, source_target_pairs={{0,4},{1,5},{2,6},{3,7},{4,8},{5,9},{6,10},{7,11},{8,12},{9,13},{1... | collective-permute-start | bytes 393224 | tf_op jit(solution)/shard_map/ppermute | solution.py:23
  17.5 1.4 %collective-permute-start.4 = (bf16[1,64,256]{2,1,0:T(8,128)(2,1)S(1)}, bf16[1,64,256]{2,1,0:T(8,128)(2,1)S(1)}, u32[]{:S(2)}, u32[]{:S(2)}) collective-permute-start(bf16[1,64,256]{2,1,0:T(8,128)(2,1)S(1)} %get-tuple-element.19), channel_id=1, source_target_pairs={{0,1},{1,0},{2,3},{3,2},{4,5},{5,4},{6,7},{7,6},{8,9},{9,8},{10,11... | collective-permute-start | bytes 98312 | tf_op jit(solution)/shard_map/ppermute | solution.py:34
  18.9 2.6 %collective-permute-done.4.rim = bf16[1,64,256]{2,1,0:T(8,128)(2,1)S(1)} collective-permute-done((bf16[1,64,256]{2,1,0:T(8,128)(2,1)S(1)}, bf16[1,64,256]{2,1,0:T(8,128)(2,1)S(1)}, u32[]{:S(2)}, u32[]{:S(2)}) %collective-permute-start.4) | collective-permute-done | bytes 32800 | tf_op jit(solution)/shard_map/ppermute | solution.py:34
  21.5 0.0 collective-permute-start.7
  21.5 4.3 %collective-permute-start.5 = (bf16[1,64,256]{2,1,0:T(8,128)(2,1)S(1)}, bf16[1,64,256]{2,1,0:T(8,128)(2,1)S(1)}, u32[]{:S(2)}, u32[]{:S(2)}) collective-permute-start(bf16[1,64,256]{2,1,0:T(8,128)(2,1)S(1)} %collective-permute-done.4.rim), channel_id=1, source_target_pairs={{0,4},{1,5},{2,6},{3,7},{4,8},{5,9},{6,10},{7,11},{8,12},{9,13},{1... | collective-permute-start | bytes 98312 | tf_op jit(solution)/shard_map/ppermute | solution.py:23
  25.8 0.0 copy-done
  25.8 0.5 %shard_map.53.total = f32[256,256]{1,0:T(8,128)S(1)} custom-call(bf16[1,4,64,256]{3,2,1,0:T(8,128)(2,1)S(1)} %shard_map.52.field, bf16[1,64,256]{2,1,0:T(8,128)(2,1)S(1)} %collective-permute-done.4.rim, bf16[3,3,768,256]{3,2,1,0:T(8,128)(2,1)S(1)} %copy-done), custom_call_target="tpu_custom_call" | custom-call | flops 301989888 | bytes 3702784 | tf_op jit(solution)/shard_map/pallas_call | solution.py:299
  26.3 0.0 collective-permute-done.7.direct_rim
  26.3 1.1 %collective-permute-done.5.rim = bf16[1,64,256]{2,1,0:T(8,128)(2,1)S(1)} collective-permute-done((bf16[1,64,256]{2,1,0:T(8,128)(2,1)S(1)}, bf16[1,64,256]{2,1,0:T(8,128)(2,1)S(1)}, u32[]{:S(2)}, u32[]{:S(2)}) %collective-permute-start.5) | collective-permute-done | bytes 32800 | tf_op jit(solution)/shard_map/ppermute | solution.py:23
  27.4 0.0 collective-permute-done.6.direct
  27.4 0.0 collective-permute-done.3.field
  27.4 0.0 collective-permute-start.8
  27.4 0.5 %collective-permute-start.9 = (bf16[1,64,256]{2,1,0:T(8,128)(2,1)S(1)}, bf16[1,64,256]{2,1,0:T(8,128)(2,1)S(1)}, u32[]{:S(2)}, u32[]{:S(2)}) collective-permute-start(bf16[1,64,256]{2,1,0:T(8,128)(2,1)S(1)} %collective-permute-done.5.rim), channel_id=1, source_target_pairs={{0,2},{2,0},{4,6},{6,4},{8,10},{10,8},{12,14},{14,12},{16,18},{18,... | collective-permute-start | bytes 98312 | tf_op jit(solution)/shard_map/ppermute | solution.py:38
  27.9 0.5 %shard_map.54.total = f32[256,256]{1,0:T(8,128)S(1)} custom-call(bf16[1,4,64,256]{3,2,1,0:T(8,128)(2,1)S(1)} %collective-permute-done.3.field, bf16[1,64,256]{2,1,0:T(8,128)(2,1)S(1)} %collective-permute-done.5.rim, bf16[3,3,768,256]{3,2,1,0:T(8,128)(2,1)S(1)} %copy-done, f32[256,256]{1,0:T(8,128)S(1)} %shard_map.53.total), custom_call_target="tpu_custom_call" | custom-call | flops 301989888 | bytes 3964928 | tf_op jit(solution)/shard_map/pallas_call | solution.py:299
  28.4 0.4 %collective-permute-done.9.relayed_rim = bf16[1,64,256]{2,1,0:T(8,128)(2,1)S(1)} collective-permute-done((bf16[1,64,256]{2,1,0:T(8,128)(2,1)S(1)}, bf16[1,64,256]{2,1,0:T(8,128)(2,1)S(1)}, u32[]{:S(2)}, u32[]{:S(2)}) %collective-permute-start.9) | collective-permute-done | bytes 32800 | tf_op jit(solution)/shard_map/ppermute | solution.py:38
  28.8 0.0 collective-permute-done.8.relayed
  28.8 1.2 %shard_map.55 = bf16[1,4,64,256]{3,2,1,0:T(8,128)(2,1)} custom-call(bf16[1,4,64,256]{3,2,1,0:T(8,128)(2,1)S(1)} %collective-permute-done.6.direct, bf16[1,64,256]{2,1,0:T(8,128)(2,1)S(1)} %collective-permute-done.7.direct_rim, bf16[1,4,64,256]{3,2,1,0:T(8,128)(2,1)S(1)} %collective-permute-done.8.relayed, ...), custom_call_target="tpu_custom_call" | custom-call | flops 301989888 | bytes 4128768 | tf_op jit(solution)/shard_map/pallas_call | solution.py:299
  (2 shorter events, 0.0 us)
Async XLA Ops:
  0.0 1.0 %copy-start.3 = (bf16[2,8,128,128]{3,2,1,0:T(8,128)(2,1)S(1)}, bf16[2,8,128,128]{3,2,1,0:T(8,128)(2,1)}, u32[]{:S(2)}) copy-start(bf16[2,8,128,128]{3,2,1,0:T(8,128)(2,1)} %frames.1) | copy-start | bytes 1572868
  0.0 6.4 %copy-start.2 = (bf16[3,3,384,128]{3,2,1,0:T(8,128)(2,1)S(1)}, bf16[3,3,384,128]{3,2,1,0:T(8,128)(2,1)}, u32[]{:S(2)}) copy-start(bf16[3,3,384,128]{3,2,1,0:T(8,128)(2,1)} %weight.10) | copy-start | bytes 2654212
  0.0 12.6 %collective-permute-start.1 = (bf16[2,8,128,128]{3,2,1,0:T(8,128)(2,1)}, bf16[2,8,128,128]{3,2,1,0:T(8,128)(2,1)S(1)}, u32[]{:S(2)}, u32[]{:S(2)}) collective-permute-start(bf16[2,8,128,128]{3,2,1,0:T(8,128)(2,1)} %frames.1), channel_id=1, source_target_pairs={{0,2},{2,4},{4,6},{6,8},{8,10},{10,12},{12,14},{14,16},{16,18},{18... | collective-permute-start | bytes 1572872 | tf_op jit(solution)/shard_map/ppermute | solution.py:28
  1.1 7.3 %collective-permute-start.2 = (bf16[2,2,128,128]{3,2,1,0:T(8,128)(2,1)S(1)}, bf16[2,2,128,128]{3,2,1,0:T(8,128)(2,1)S(1)}, u32[]{:S(2)}, u32[]{:S(2)}) collective-permute-start(bf16[2,2,128,128]{3,2,1,0:T(8,128)(2,1)S(1)} %shard_map.47), channel_id=1, source_target_pairs={{0,1},{1,0},{2,3},{3,2},{4,5},{5,4},{6,7},{7,6},{8,9},{9,8},{10,11... | collective-permute-start | bytes 393224 | tf_op jit(solution)/shard_map/ppermute | solution.py:34
  4.1 10.0 %collective-permute-start = (bf16[2,2,128,128]{3,2,1,0:T(8,128)(2,1)S(1)}, bf16[2,2,128,128]{3,2,1,0:T(8,128)(2,1)S(1)}, u32[]{:S(2)}, u32[]{:S(2)}) collective-permute-start(bf16[2,2,128,128]{3,2,1,0:T(8,128)(2,1)S(1)} %shard_map.47), channel_id=1, source_target_pairs={{0,3},{1,2},{2,5},{3,4},{4,7},{5,6},{6,9},{7,8},{8,11},{9,10},{10,... | collective-permute-start | bytes 393224 | tf_op jit(solution)/shard_map/ppermute | solution.py:34
  8.8 5.4 %copy-start.1 = (bf16[3,384,256]{2,1,0:T(8,128)(2,1)S(1)}, bf16[3,384,256]{2,1,0:T(8,128)(2,1)}, u32[]{:S(2)}) copy-start(bf16[3,384,256]{2,1,0:T(8,128)(2,1)} %down.3) | copy-start | bytes 1769476
  14.2 11.7 %copy-start = (bf16[3,3,768,256]{3,2,1,0:T(8,128)(2,1)S(1)}, bf16[3,3,768,256]{3,2,1,0:T(8,128)(2,1)}, u32[]{:S(2)}) copy-start(bf16[3,3,768,256]{3,2,1,0:T(8,128)(2,1)} %weight.13) | copy-start | bytes 10616836
  15.5 11.9 %collective-permute-start.6 = (bf16[1,4,64,256]{3,2,1,0:T(8,128)(2,1)S(1)}, bf16[1,4,64,256]{3,2,1,0:T(8,128)(2,1)S(1)}, u32[]{:S(2)}, u32[]{:S(2)}) collective-permute-start(bf16[1,4,64,256]{3,2,1,0:T(8,128)(2,1)S(1)} %shard_map.52.field), channel_id=1, source_target_pairs={{0,2},{2,0},{4,6},{6,4},{8,10},{10,8},{12,14},{14,12},{16,18},{18,... | collective-permute-start | bytes 393224 | tf_op jit(solution)/shard_map/ppermute | solution.py:38
  15.6 11.8 %collective-permute-start.3 = (bf16[1,4,64,256]{3,2,1,0:T(8,128)(2,1)S(1)}, bf16[1,4,64,256]{3,2,1,0:T(8,128)(2,1)S(1)}, u32[]{:S(2)}, u32[]{:S(2)}) collective-permute-start(bf16[1,4,64,256]{3,2,1,0:T(8,128)(2,1)S(1)} %shard_map.52.field), channel_id=1, source_target_pairs={{0,4},{1,5},{2,6},{3,7},{4,8},{5,9},{6,10},{7,11},{8,12},{9,13},{1... | collective-permute-start | bytes 393224 | tf_op jit(solution)/shard_map/ppermute | solution.py:23
  17.5 4.0 %collective-permute-start.4 = (bf16[1,64,256]{2,1,0:T(8,128)(2,1)S(1)}, bf16[1,64,256]{2,1,0:T(8,128)(2,1)S(1)}, u32[]{:S(2)}, u32[]{:S(2)}) collective-permute-start(bf16[1,64,256]{2,1,0:T(8,128)(2,1)S(1)} %get-tuple-element.19), channel_id=1, source_target_pairs={{0,1},{1,0},{2,3},{3,2},{4,5},{5,4},{6,7},{7,6},{8,9},{9,8},{10,11... | collective-permute-start | bytes 98312 | tf_op jit(solution)/shard_map/ppermute | solution.py:34
  21.5 4.8 %collective-permute-start.7 = (bf16[1,64,256]{2,1,0:T(8,128)(2,1)S(1)}, bf16[1,64,256]{2,1,0:T(8,128)(2,1)S(1)}, u32[]{:S(2)}, u32[]{:S(2)}) collective-permute-start(bf16[1,64,256]{2,1,0:T(8,128)(2,1)S(1)} %collective-permute-done.4.rim), channel_id=1, source_target_pairs={{0,2},{2,0},{4,6},{6,4},{8,10},{10,8},{12,14},{14,12},{16,18},{18,... | collective-permute-start | bytes 98312 | tf_op jit(solution)/shard_map/ppermute | solution.py:38
  21.5 5.9 %collective-permute-start.5 = (bf16[1,64,256]{2,1,0:T(8,128)(2,1)S(1)}, bf16[1,64,256]{2,1,0:T(8,128)(2,1)S(1)}, u32[]{:S(2)}, u32[]{:S(2)}) collective-permute-start(bf16[1,64,256]{2,1,0:T(8,128)(2,1)S(1)} %collective-permute-done.4.rim), channel_id=1, source_target_pairs={{0,4},{1,5},{2,6},{3,7},{4,8},{5,9},{6,10},{7,11},{8,12},{9,13},{1... | collective-permute-start | bytes 98312 | tf_op jit(solution)/shard_map/ppermute | solution.py:23
  27.4 1.4 %collective-permute-start.8 = (bf16[1,4,64,256]{3,2,1,0:T(8,128)(2,1)S(1)}, bf16[1,4,64,256]{3,2,1,0:T(8,128)(2,1)S(1)}, u32[]{:S(2)}, u32[]{:S(2)}) collective-permute-start(bf16[1,4,64,256]{3,2,1,0:T(8,128)(2,1)S(1)} %collective-permute-done.3.field), channel_id=1, source_target_pairs={{0,2},{2,0},{4,6},{6,4},{8,10},{10,8},{12,14},{14,12},{16,18},{18,... | collective-permute-start | bytes 393224 | tf_op jit(solution)/shard_map/ppermute | solution.py:38
  27.4 1.4 %collective-permute-start.9 = (bf16[1,64,256]{2,1,0:T(8,128)(2,1)S(1)}, bf16[1,64,256]{2,1,0:T(8,128)(2,1)S(1)}, u32[]{:S(2)}, u32[]{:S(2)}) collective-permute-start(bf16[1,64,256]{2,1,0:T(8,128)(2,1)S(1)} %collective-permute-done.5.rim), channel_id=1, source_target_pairs={{0,2},{2,0},{4,6},{6,4},{8,10},{10,8},{12,14},{14,12},{16,18},{18,... | collective-permute-start | bytes 98312 | tf_op jit(solution)/shard_map/ppermute | solution.py:38
where the time goes:
time: 30.1 us; the launch traced here: 30 us
  starting transfers between devices  14.1 us (47%)
  waiting for transfers between devices  8.21 us (27%)
  Pallas kernels  6.97 us (23%)
  local copies, waits for them, and re-layouts  0.56 us (2%)
    pallas_call x10, Pallas kernels, call(): pl.pallas_call(kernel, out_shape=out_shape, in_specs=[pl.BlockSpec(memory...  6.97 us
    ppermute x3, starting transfers between devices, swapped(): return lax.ppermute(value, ('tm', 'rows'), pairs)  6.77 us
    ppermute x2, starting transfers between devices, moved(): return lax.ppermute(value, ('tm', 'rows'), pairs)  6.22 us
    ppermute x1, waiting for transfers between devices, ring(): return lax.ppermute(value, 'tm', [(t, (t + steps) % tm) for t in range(tm)])  3.78 us
    ppermute x3, waiting for transfers between devices, swapped(): return lax.ppermute(value, ('tm', 'rows'), pairs)  2.94 us
    ppermute x2, waiting for transfers between devices, moved(): return lax.ppermute(value, ('tm', 'rows'), pairs)  1.08 us
  transfers between devices with their start and end apart: 10, of which 5 were waited for; matrix products, arithmetic and copies ran while one was open for 0% of the time, Pallas kernels for 15%

commit v1 on v0

--- a/solution.py
+++ b/solution.py
@@ -254,14 +254,20 @@
     out[...] = down_conv(pooled, half_rows, half_cols, down).reshape(out.shape)
 
 
-def coarse_sum(field, rim, weight, a):
-    _, rows, cols, channels = field.shape
+def join_kernel(field, rim, out):
+    rows = field.shape[1]
+    out[0, :rows] = field[0]
+    out[0, rows:] = rim[...]
+
+
+def coarse_sum(joined, rows, weight, a):
+    _, count, cols, channels = joined.shape
     zero = jnp.zeros((cols, channels), BF16)
     flat = jnp.concatenate(
         [
-            jnp.where(has_above(), rim[0], zero),
-            field.reshape(rows * cols, channels),
-            jnp.where(has_below(), rim[rim.shape[0] - 1], zero),
+            jnp.where(has_above(), joined[0, rows], zero),
+            joined[0, :rows].reshape(rows * cols, channels),
+            jnp.where(has_below(), joined[0, count - 1], zero),
         ],
         axis=0,
     )
@@ -276,20 +282,18 @@
     return total
 
 
-def coarse_first_kernel(field, rim, weight, out):
-    out[...] = coarse_sum(field[...], rim[...], weight, 2)
-
-
-def coarse_next_kernel(field, rim, weight, total, out):
-    part = coarse_sum(field[...], rim[...], weight, 0)
+def coarse_first_kernel(joined, weight, out):
+    out[...] = coarse_sum(joined[...], out.shape[0] // joined.shape[2], weight, 2)
+
+
+def coarse_next_kernel(joined, weight, total, out):
+    part = coarse_sum(joined[...], out.shape[0] // joined.shape[2], weight, 0)
     out[...] = total[...] + jnp.where(has_earlier(2), part, 0.0)
 
 
-def coarse_last_kernel(direct, direct_rim, relayed, relayed_rim, weight, total, out):
+def coarse_last_kernel(direct, relayed, weight, total, out):
     odd = lax.axis_index("tm") % 2 == 1
-    field = jnp.where(odd, direct[...], relayed[...])
-    rim = jnp.where(odd, direct_rim[...], relayed_rim[...])
-    part = coarse_sum(field, rim, weight, 1)
+    part = coarse_sum(jnp.where(odd, direct[...], relayed[...]), out.shape[1], weight, 1)
     total = total[...] + jnp.where(has_earlier(1), part, 0.0)
     out[...] = silu(total).astype(BF16).reshape(out.shape)
 
@@ -346,34 +350,21 @@
         flops // 3,
         (fine_sums, halo_1, conv_down),
     )
-    field_2 = moved(field, 2, 0)
     if sides == 1:
         rim = swapped(ends, 0)
     else:
         rim = jnp.concatenate([moved(ends[1:], 0, 1), moved(ends[:1], 0, -1)], axis=0)
-    rim_2 = moved(rim, 2, 0)
+    joined_shape = jax.ShapeDtypeStruct((1, half_rows + sides, half_cols, wide), BF16)
+    joined = call(join_kernel, joined_shape, [], 0, (field, rim))
     sums = jax.ShapeDtypeStruct((half_rows * half_cols, wide), F32)
     flops = 2 * half_rows * half_cols * 9 * wide * wide
-    total = call(coarse_first_kernel, sums, [], flops, (field, rim, conv_coarse))
-    if times % 2 == 0:
-        direct, direct_rim = paired(field), paired(rim)
-    else:
-        direct, direct_rim = ring(field, 1), ring(rim, 1)
-    field_2, rim_2, total, direct, direct_rim = lax.optimization_barrier(
-        (field_2, rim_2, total, direct, direct_rim)
-    )
-    if times % 2 == 0:
-        relayed, relayed_rim = paired(field_2), paired(rim_2)
-    else:
-        relayed, relayed_rim = direct, direct_rim
-    total = call(coarse_next_kernel, sums, [], flops, (field_2, rim_2, conv_coarse, total))
-    return call(
-        coarse_last_kernel,
-        shape,
-        [],
-        flops,
-        (direct, direct_rim, relayed, relayed_rim, conv_coarse, total),
-    )
+    joined_2 = moved(joined, 2, 0)
+    total = call(coarse_first_kernel, sums, [], flops, (joined, conv_coarse))
+    direct = paired(joined) if times % 2 == 0 else ring(joined, 1)
+    joined_2, total, direct = lax.optimization_barrier((joined_2, total, direct))
+    relayed = paired(joined_2) if times % 2 == 0 else direct
+    total = call(coarse_next_kernel, sums, [], flops, (joined_2, conv_coarse, total))
+    return call(coarse_last_kernel, shape, [], flops, (direct, relayed, conv_coarse, total))
 
 
 def solution(mesh):

time: 30.1 us -> 29.3 us (0.973)
  the two profiles are of different devices: /device:TPU:0 before, /device:TPU:16 now
where the time goes in v1:
time: 29.3 us; the launch traced here: 28.8 us
  waiting for transfers between devices  13.4 us (46%)
  starting transfers between devices  7.28 us (25%)
  Pallas kernels  6.96 us (24%)
  local copies, waits for them, and re-layouts  1.03 us (4%)
    pallas_call x11, Pallas kernels, call(): pl.pallas_call(kernel, out_shape=out_shape, in_specs=[pl.BlockSpec(memory...  6.96 us
    ppermute x1, waiting for transfers between devices, moved(): return lax.ppermute(value, ('tm', 'rows'), pairs)  6.37 us
    ppermute x3, starting transfers between devices, swapped(): return lax.ppermute(value, ('tm', 'rows'), pairs)  4.7 us
    ppermute x3, waiting for transfers between devices, swapped(): return lax.ppermute(value, ('tm', 'rows'), pairs)  3.91 us
    ppermute x1, starting transfers between devices, moved(): return lax.ppermute(value, ('tm', 'rows'), pairs)  2.5 us
    ppermute x1, waiting for transfers between devices, ring(): return lax.ppermute(value, 'tm', [(t, (t + steps) % tm) for t in range(tm)])  2.17 us
    unnamed x8, local copies, waits for them, and re-layouts  1.03 us
    ppermute x2, waiting for transfers between devices, paired(): lax.ppermute(value, 'tm', [(t, t ^ 1) for t in range(lax.axis_size('tm'))])  0.91 us
  transfers between devices with their start and end apart: 7, of which 6 were waited for; matrix products, arithmetic and copies ran while one was open for 0% of the time, Pallas kernels for 18%

profile of v1, /device:TPU:16, one launch (start us, length us, event | category | flops | bytes accessed | tf_op | source)
XLA Modules:
  0.0 28.8 jit_solution(15615656817703629571)
XLA Ops:
  0.0 0.0 copy-start.3
  0.0 0.0 copy-start.2
  0.0 0.0 collective-permute-start.1
  0.0 1.0 %copy-done.3 = bf16[2,8,128,128]{3,2,1,0:T(8,128)(2,1)S(1)} copy-done((bf16[2,8,128,128]{3,2,1,0:T(8,128)(2,1)S(1)}, bf16[2,8,128,128]{3,2,1,0:T(8,128)(2,1)}, u32[]{:S(2)}) %copy-start.3) | copy-done | bytes 524312
  1.1 1.6 %collective-permute-start.2 = (bf16[2,2,128,128]{3,2,1,0:T(8,128)(2,1)S(1)}, bf16[2,2,128,128]{3,2,1,0:T(8,128)(2,1)S(1)}, u32[]{:S(2)}, u32[]{:S(2)}) collective-permute-start(bf16[2,2,128,128]{3,2,1,0:T(8,128)(2,1)S(1)} %shard_map.47), channel_id=1, source_target_pairs={{0,1},{1,0},{2,3},{3,2},{4,5},{5,4},{6,7},{7,6},{8,9},{9,8},{10,11... | collective-permute-start | bytes 393224 | tf_op jit(solution)/shard_map/ppermute | solution.py:34
  2.6 2.3 %collective-permute-start = (bf16[2,2,128,128]{3,2,1,0:T(8,128)(2,1)S(1)}, bf16[2,2,128,128]{3,2,1,0:T(8,128)(2,1)S(1)}, u32[]{:S(2)}, u32[]{:S(2)}) collective-permute-start(bf16[2,2,128,128]{3,2,1,0:T(8,128)(2,1)S(1)} %shard_map.47), channel_id=1, source_target_pairs={{0,3},{1,2},{2,5},{3,4},{4,7},{5,6},{6,9},{7,8},{8,11},{9,10},{10,... | collective-permute-start | bytes 393224 | tf_op jit(solution)/shard_map/ppermute | solution.py:34
  5.0 0.0 copy-done.2
  5.0 1.5 %shard_map.48.own = f32[1152,256]{1,0:T(8,128)S(1)} custom-call(bf16[2,8,128,128]{3,2,1,0:T(8,128)(2,1)S(1)} %copy-done.3, bf16[3,3,384,128]{3,2,1,0:T(8,128)(2,1)S(1)} %copy-done.2), custom_call_target="tpu_custom_call" | custom-call | flops 1358954496 | bytes 1409024 | tf_op jit(solution)/shard_map/pallas_call | solution.py:303
  6.5 0.6 %collective-permute-done.2.above.below = bf16[2,2,128,128]{3,2,1,0:T(8,128)(2,1)S(1)} collective-permute-done((bf16[2,2,128,128]{3,2,1,0:T(8,128)(2,1)S(1)}, bf16[2,2,128,128]{3,2,1,0:T(8,128)(2,1)S(1)}, u32[]{:S(2)}, u32[]{:S(2)}) %collective-permute-start.2) | collective-permute-done | bytes 131104 | tf_op jit(solution)/shard_map/ppermute | solution.py:34
  7.1 0.4 %shard_map.49.halo = f32[384,256]{1,0:T(8,128)S(1)} custom-call(bf16[2,2,128,128]{3,2,1,0:T(8,128)(2,1)S(1)} %collective-permute-done.2.above.below, bf16[2,2,128,128]{3,2,1,0:T(8,128)(2,1)S(1)} %collective-permute-done.2.above.below, bf16[3,3,384,128]{3,2,1,0:T(8,128)(2,1)S(1)} %copy-done.2), custom_call_target="tpu_custom_call" | custom-call | flops 452984832 | bytes 1146880 | tf_op jit(solution)/shard_map/pallas_call | solution.py:303
  7.5 0.0 copy-start.1
  7.5 2.2 %collective-permute-done.1.frames = bf16[2,8,128,128]{3,2,1,0:T(8,128)(2,1)S(1)} collective-permute-done((bf16[2,8,128,128]{3,2,1,0:T(8,128)(2,1)}, bf16[2,8,128,128]{3,2,1,0:T(8,128)(2,1)S(1)}, u32[]{:S(2)}, u32[]{:S(2)}) %collective-permute-start.1) | collective-permute-done | bytes 524320 | tf_op jit(solution)/shard_map/ppermute | solution.py:28
  9.7 1.5 %shard_map.50.sums = f32[1152,256]{1,0:T(8,128)S(1)} custom-call(bf16[2,8,128,128]{3,2,1,0:T(8,128)(2,1)S(1)} %collective-permute-done.1.frames, bf16[3,3,384,128]{3,2,1,0:T(8,128)(2,1)S(1)} %copy-done.2, f32[1152,256]{1,0:T(8,128)S(1)} %shard_map.48.own, f32[384,256]{1,0:T(8,128)S(1)} %shard_map.49.halo), custom_call_target="tpu_custom_call" | custom-call | flops 1358954496 | bytes 2981888 | tf_op jit(solution)/shard_map/pallas_call | solution.py:303
  11.3 0.8 %collective-permute-done.above.below = bf16[2,2,128,128]{3,2,1,0:T(8,128)(2,1)S(1)} collective-permute-done((bf16[2,2,128,128]{3,2,1,0:T(8,128)(2,1)S(1)}, bf16[2,2,128,128]{3,2,1,0:T(8,128)(2,1)S(1)}, u32[]{:S(2)}, u32[]{:S(2)}) %collective-permute-start) | collective-permute-done | bytes 131104 | tf_op jit(solution)/shard_map/ppermute | solution.py:34
  12.1 0.0 copy-done.1
  12.1 0.0 copy-start
  12.1 0.7 %shard_map.51 = (bf16[1,64,256]{2,1,0:T(8,128)(2,1)S(1)}, f32[384,256]{1,0:T(8,128)S(1)}) custom-call(bf16[2,2,128,128]{3,2,1,0:T(8,128)(2,1)S(1)} %collective-permute-done.above.below, bf16[2,2,128,128]{3,2,1,0:T(8,128)(2,1)S(1)} %collective-permute-done.above.below, bf16[3,3,384,128]{3,2,1,0:T(8,128)(2,1)S(1)} %copy-done.2, ...), custom_call_target="tpu_custom_call" | custom-call | flops 452984832 | bytes 2916352 | tf_op jit(solution)/shard_map/pallas_call | solution.py:303
  12.8 0.8 %collective-permute-start.3 = (bf16[1,64,256]{2,1,0:T(8,128)(2,1)S(1)}, bf16[1,64,256]{2,1,0:T(8,128)(2,1)S(1)}, u32[]{:S(2)}, u32[]{:S(2)}) collective-permute-start(bf16[1,64,256]{2,1,0:T(8,128)(2,1)S(1)} %get-tuple-element.17), channel_id=1, source_target_pairs={{0,1},{1,0},{2,3},{3,2},{4,5},{5,4},{6,7},{7,6},{8,9},{9,8},{10,11... | collective-permute-start | bytes 98312 | tf_op jit(solution)/shard_map/ppermute | solution.py:34
  13.6 0.6 %shard_map.52.field = bf16[1,4,64,256]{3,2,1,0:T(8,128)(2,1)S(1)} custom-call(f32[1152,256]{1,0:T(8,128)S(1)} %shard_map.50.sums, f32[384,256]{1,0:T(8,128)S(1)} %get-tuple-element.16.halo, bf16[3,384,256]{2,1,0:T(8,128)(2,1)S(1)} %copy-done.1), custom_call_target="tpu_custom_call" | custom-call | flops 452984832 | bytes 2162688 | tf_op jit(solution)/shard_map/pallas_call | solution.py:303
  14.2 2.5 %collective-permute-done.3.rim = bf16[1,64,256]{2,1,0:T(8,128)(2,1)S(1)} collective-permute-done((bf16[1,64,256]{2,1,0:T(8,128)(2,1)S(1)}, bf16[1,64,256]{2,1,0:T(8,128)(2,1)S(1)}, u32[]{:S(2)}, u32[]{:S(2)}) %collective-permute-start.3) | collective-permute-done | bytes 32800 | tf_op jit(solution)/shard_map/ppermute | solution.py:34
  16.8 0.1 collective-permute-start.5
  16.8 2.5 %collective-permute-start.4 = (bf16[1,5,64,256]{3,2,1,0:T(8,128)(2,1)S(1)}, bf16[1,5,64,256]{3,2,1,0:T(8,128)(2,1)S(1)}, u32[]{:S(2)}, u32[]{:S(2)}) collective-permute-start(bf16[1,5,64,256]{3,2,1,0:T(8,128)(2,1)S(1)} %shard_map.53.joined), channel_id=1, source_target_pairs={{0,4},{1,5},{2,6},{3,7},{4,8},{5,9},{6,10},{7,11},{8,12},{9,13},{1... | collective-permute-start | bytes 491528 | tf_op jit(solution)/shard_map/ppermute | solution.py:23
  19.3 0.0 copy-done
  19.4 0.5 %shard_map.54.total = f32[256,256]{1,0:T(8,128)S(1)} custom-call(bf16[1,5,64,256]{3,2,1,0:T(8,128)(2,1)S(1)} %shard_map.53.joined, bf16[3,3,768,256]{3,2,1,0:T(8,128)(2,1)S(1)} %copy-done), custom_call_target="tpu_custom_call" | custom-call | flops 301989888 | bytes 3702784 | tf_op jit(solution)/shard_map/pallas_call | solution.py:303
  19.8 0.0 collective-permute-done.5.direct
  19.9 6.4 %collective-permute-done.4.joined = bf16[1,5,64,256]{3,2,1,0:T(8,128)(2,1)S(1)} collective-permute-done((bf16[1,5,64,256]{3,2,1,0:T(8,128)(2,1)S(1)}, bf16[1,5,64,256]{3,2,1,0:T(8,128)(2,1)S(1)}, u32[]{:S(2)}, u32[]{:S(2)}) %collective-permute-start.4) | collective-permute-done | bytes 163872 | tf_op jit(solution)/shard_map/ppermute | solution.py:23
  26.2 0.0 collective-permute-start.6
  26.2 0.5 %shard_map.55.total = f32[256,256]{1,0:T(8,128)S(1)} custom-call(bf16[1,5,64,256]{3,2,1,0:T(8,128)(2,1)S(1)} %collective-permute-done.4.joined, bf16[3,3,768,256]{3,2,1,0:T(8,128)(2,1)S(1)} %copy-done, f32[256,256]{1,0:T(8,128)S(1)} %shard_map.54.total), custom_call_target="tpu_custom_call" | custom-call | flops 301989888 | bytes 3964928 | tf_op jit(solution)/shard_map/pallas_call | solution.py:303
  26.7 0.9 %collective-permute-done.6.relayed = bf16[1,5,64,256]{3,2,1,0:T(8,128)(2,1)S(1)} collective-permute-done((bf16[1,5,64,256]{3,2,1,0:T(8,128)(2,1)S(1)}, bf16[1,5,64,256]{3,2,1,0:T(8,128)(2,1)S(1)}, u32[]{:S(2)}, u32[]{:S(2)}) %collective-permute-start.6) | collective-permute-done | bytes 163872 | tf_op jit(solution)/shard_map/ppermute | solution.py:38
  27.6 1.2 %shard_map.56 = bf16[1,4,64,256]{3,2,1,0:T(8,128)(2,1)} custom-call(bf16[1,5,64,256]{3,2,1,0:T(8,128)(2,1)S(1)} %collective-permute-done.5.direct, bf16[1,5,64,256]{3,2,1,0:T(8,128)(2,1)S(1)} %collective-permute-done.6.relayed, bf16[3,3,768,256]{3,2,1,0:T(8,128)(2,1)S(1)} %copy-done, f32[256,256]{1,0:T(8,128)S(1)} %shard_map.55.total), custom_call_target="tpu_custom_call" | custom-call | flops 301989888 | bytes 4128768 | tf_op jit(solution)/shard_map/pallas_call | solution.py:303
  (3 shorter events, 0.0 us)
Async XLA Ops:
  0.0 1.0 %copy-start.3 = (bf16[2,8,128,128]{3,2,1,0:T(8,128)(2,1)S(1)}, bf16[2,8,128,128]{3,2,1,0:T(8,128)(2,1)}, u32[]{:S(2)}) copy-start(bf16[2,8,128,128]{3,2,1,0:T(8,128)(2,1)} %frames.1) | copy-start | bytes 1572868
  0.0 4.9 %copy-start.2 = (bf16[3,3,384,128]{3,2,1,0:T(8,128)(2,1)S(1)}, bf16[3,3,384,128]{3,2,1,0:T(8,128)(2,1)}, u32[]{:S(2)}) copy-start(bf16[3,3,384,128]{3,2,1,0:T(8,128)(2,1)} %weight.10) | copy-start | bytes 2654212
  0.0 9.7 %collective-permute-start.1 = (bf16[2,8,128,128]{3,2,1,0:T(8,128)(2,1)}, bf16[2,8,128,128]{3,2,1,0:T(8,128)(2,1)S(1)}, u32[]{:S(2)}, u32[]{:S(2)}) collective-permute-start(bf16[2,8,128,128]{3,2,1,0:T(8,128)(2,1)} %frames.1), channel_id=1, source_target_pairs={{0,2},{2,4},{4,6},{6,8},{8,10},{10,12},{12,14},{14,16},{16,18},{18... | collective-permute-start | bytes 1572872 | tf_op jit(solution)/shard_map/ppermute | solution.py:28
  1.1 6.0 %collective-permute-start.2 = (bf16[2,2,128,128]{3,2,1,0:T(8,128)(2,1)S(1)}, bf16[2,2,128,128]{3,2,1,0:T(8,128)(2,1)S(1)}, u32[]{:S(2)}, u32[]{:S(2)}) collective-permute-start(bf16[2,2,128,128]{3,2,1,0:T(8,128)(2,1)S(1)} %shard_map.47), channel_id=1, source_target_pairs={{0,1},{1,0},{2,3},{3,2},{4,5},{5,4},{6,7},{7,6},{8,9},{9,8},{10,11... | collective-permute-start | bytes 393224 | tf_op jit(solution)/shard_map/ppermute | solution.py:34
  2.6 9.4 %collective-permute-start = (bf16[2,2,128,128]{3,2,1,0:T(8,128)(2,1)S(1)}, bf16[2,2,128,128]{3,2,1,0:T(8,128)(2,1)S(1)}, u32[]{:S(2)}, u32[]{:S(2)}) collective-permute-start(bf16[2,2,128,128]{3,2,1,0:T(8,128)(2,1)S(1)} %shard_map.47), channel_id=1, source_target_pairs={{0,3},{1,2},{2,5},{3,4},{4,7},{5,6},{6,9},{7,8},{8,11},{9,10},{10,... | collective-permute-start | bytes 393224 | tf_op jit(solution)/shard_map/ppermute | solution.py:34
  7.5 4.5 %copy-start.1 = (bf16[3,384,256]{2,1,0:T(8,128)(2,1)S(1)}, bf16[3,384,256]{2,1,0:T(8,128)(2,1)}, u32[]{:S(2)}) copy-start(bf16[3,384,256]{2,1,0:T(8,128)(2,1)} %down.3) | copy-start | bytes 1769476
  12.1 7.3 %copy-start = (bf16[3,3,768,256]{3,2,1,0:T(8,128)(2,1)S(1)}, bf16[3,3,768,256]{3,2,1,0:T(8,128)(2,1)}, u32[]{:S(2)}) copy-start(bf16[3,3,768,256]{3,2,1,0:T(8,128)(2,1)} %weight.13) | copy-start | bytes 10616836
  12.8 4.0 %collective-permute-start.3 = (bf16[1,64,256]{2,1,0:T(8,128)(2,1)S(1)}, bf16[1,64,256]{2,1,0:T(8,128)(2,1)S(1)}, u32[]{:S(2)}, u32[]{:S(2)}) collective-permute-start(bf16[1,64,256]{2,1,0:T(8,128)(2,1)S(1)} %get-tuple-element.17), channel_id=1, source_target_pairs={{0,1},{1,0},{2,3},{3,2},{4,5},{5,4},{6,7},{7,6},{8,9},{9,8},{10,11... | collective-permute-start | bytes 98312 | tf_op jit(solution)/shard_map/ppermute | solution.py:34
  16.8 3.1 %collective-permute-start.5 = (bf16[1,5,64,256]{3,2,1,0:T(8,128)(2,1)S(1)}, bf16[1,5,64,256]{3,2,1,0:T(8,128)(2,1)S(1)}, u32[]{:S(2)}, u32[]{:S(2)}) collective-permute-start(bf16[1,5,64,256]{3,2,1,0:T(8,128)(2,1)S(1)} %shard_map.53.joined), channel_id=1, source_target_pairs={{0,2},{2,0},{4,6},{6,4},{8,10},{10,8},{12,14},{14,12},{16,18},{18,... | collective-permute-start | bytes 491528 | tf_op jit(solution)/shard_map/ppermute | solution.py:38
  16.8 9.4 %collective-permute-start.4 = (bf16[1,5,64,256]{3,2,1,0:T(8,128)(2,1)S(1)}, bf16[1,5,64,256]{3,2,1,0:T(8,128)(2,1)S(1)}, u32[]{:S(2)}, u32[]{:S(2)}) collective-permute-start(bf16[1,5,64,256]{3,2,1,0:T(8,128)(2,1)S(1)} %shard_map.53.joined), channel_id=1, source_target_pairs={{0,4},{1,5},{2,6},{3,7},{4,8},{5,9},{6,10},{7,11},{8,12},{9,13},{1... | collective-permute-start | bytes 491528 | tf_op jit(solution)/shard_map/ppermute | solution.py:23
  26.2 1.4 %collective-permute-start.6 = (bf16[1,5,64,256]{3,2,1,0:T(8,128)(2,1)S(1)}, bf16[1,5,64,256]{3,2,1,0:T(8,128)(2,1)S(1)}, u32[]{:S(2)}, u32[]{:S(2)}) collective-permute-start(bf16[1,5,64,256]{3,2,1,0:T(8,128)(2,1)S(1)} %collective-permute-done.4.joined), channel_id=1, source_target_pairs={{0,2},{2,0},{4,6},{6,4},{8,10},{10,8},{12,14},{14,12},{16,18},{18,... | collective-permute-start | bytes 491528 | tf_op jit(solution)/shard_map/ppermute | solution.py:38

commit v2 on v0

--- a/solution.py
+++ b/solution.py
@@ -355,10 +355,9 @@
     sums = jax.ShapeDtypeStruct((half_rows * half_cols, wide), F32)
     flops = 2 * half_rows * half_cols * 9 * wide * wide
     total = call(coarse_first_kernel, sums, [], flops, (field, rim, conv_coarse))
-    if times % 2 == 0:
-        direct, direct_rim = paired(field), paired(rim)
-    else:
-        direct, direct_rim = ring(field, 1), ring(rim, 1)
+    near = paired if times % 2 == 0 else functools.partial(ring, steps=1)
+    direct = near(field)
+    direct_rim = near(rim)
     field_2, rim_2, total, direct, direct_rim = lax.optimization_barrier(
         (field_2, rim_2, total, direct, direct_rim)
     )

time: 30.1 us -> 30.1 us (level)
  no operation moved by 1% of the time
where the time goes in v2:
time: 30.1 us; the launch traced here: 30 us
  starting transfers between devices  14.1 us (47%)
  waiting for transfers between devices  8.21 us (27%)
  Pallas kernels  6.97 us (23%)
  local copies, waits for them, and re-layouts  0.56 us (2%)
    pallas_call x10, Pallas kernels, call(): pl.pallas_call(kernel, out_shape=out_shape, in_specs=[pl.BlockSpec(memory...  6.97 us
    ppermute x3, starting transfers between devices, swapped(): return lax.ppermute(value, ('tm', 'rows'), pairs)  6.77 us
    ppermute x2, starting transfers between devices, moved(): return lax.ppermute(value, ('tm', 'rows'), pairs)  6.22 us
    ppermute x1, waiting for transfers between devices, ring(): return lax.ppermute(value, 'tm', [(t, (t + steps) % tm) for t in range(tm)])  3.78 us
    ppermute x3, waiting for transfers between devices, swapped(): return lax.ppermute(value, ('tm', 'rows'), pairs)  2.94 us
    ppermute x2, waiting for transfers between devices, moved(): return lax.ppermute(value, ('tm', 'rows'), pairs)  1.08 us
  transfers between devices with their start and end apart: 10, of which 5 were waited for; matrix products, arithmetic and copies ran while one was open for 0% of the time, Pallas kernels for 15%

profile of v2, /device:TPU:0, one launch (start us, length us, event | category | flops | bytes accessed | tf_op | source)
XLA Modules:
  0.0 30.0 jit_solution(1912727164796850477)
XLA Ops:
  0.0 0.0 copy-start.3
  0.0 0.0 copy-start.2
  0.0 0.5 %collective-permute-start.1 = (bf16[2,8,128,128]{3,2,1,0:T(8,128)(2,1)}, bf16[2,8,128,128]{3,2,1,0:T(8,128)(2,1)S(1)}, u32[]{:S(2)}, u32[]{:S(2)}) collective-permute-start(bf16[2,8,128,128]{3,2,1,0:T(8,128)(2,1)} %frames.1), channel_id=1, source_target_pairs={{0,2},{2,4},{4,6},{6,8},{8,10},{10,12},{12,14},{14,16},{16,18},{18... | collective-permute-start | bytes 1572872 | tf_op jit(solution)/shard_map/ppermute | solution.py:28
  0.5 0.5 %copy-done.3 = bf16[2,8,128,128]{3,2,1,0:T(8,128)(2,1)S(1)} copy-done((bf16[2,8,128,128]{3,2,1,0:T(8,128)(2,1)S(1)}, bf16[2,8,128,128]{3,2,1,0:T(8,128)(2,1)}, u32[]{:S(2)}) %copy-start.3) | copy-done | bytes 524312
  1.1 3.1 %collective-permute-start.2 = (bf16[2,2,128,128]{3,2,1,0:T(8,128)(2,1)S(1)}, bf16[2,2,128,128]{3,2,1,0:T(8,128)(2,1)S(1)}, u32[]{:S(2)}, u32[]{:S(2)}) collective-permute-start(bf16[2,2,128,128]{3,2,1,0:T(8,128)(2,1)S(1)} %shard_map.47), channel_id=1, source_target_pairs={{0,1},{1,0},{2,3},{3,2},{4,5},{5,4},{6,7},{7,6},{8,9},{9,8},{10,11... | collective-permute-start | bytes 393224 | tf_op jit(solution)/shard_map/ppermute | solution.py:34
  4.1 2.3 %collective-permute-start = (bf16[2,2,128,128]{3,2,1,0:T(8,128)(2,1)S(1)}, bf16[2,2,128,128]{3,2,1,0:T(8,128)(2,1)S(1)}, u32[]{:S(2)}, u32[]{:S(2)}) collective-permute-start(bf16[2,2,128,128]{3,2,1,0:T(8,128)(2,1)S(1)} %shard_map.47), channel_id=1, source_target_pairs={{0,3},{1,2},{2,5},{3,4},{4,7},{5,6},{6,9},{7,8},{8,11},{9,10},{10,... | collective-permute-start | bytes 393224 | tf_op jit(solution)/shard_map/ppermute | solution.py:34
  6.4 0.0 copy-done.2
  6.4 1.5 %shard_map.48.own = f32[1152,256]{1,0:T(8,128)S(1)} custom-call(bf16[2,8,128,128]{3,2,1,0:T(8,128)(2,1)S(1)} %copy-done.3, bf16[3,3,384,128]{3,2,1,0:T(8,128)(2,1)S(1)} %copy-done.2), custom_call_target="tpu_custom_call" | custom-call | flops 1358954496 | bytes 1409024 | tf_op jit(solution)/shard_map/pallas_call | solution.py:299
  8.0 0.4 %collective-permute-done.2.above.below = bf16[2,2,128,128]{3,2,1,0:T(8,128)(2,1)S(1)} collective-permute-done((bf16[2,2,128,128]{3,2,1,0:T(8,128)(2,1)S(1)}, bf16[2,2,128,128]{3,2,1,0:T(8,128)(2,1)S(1)}, u32[]{:S(2)}, u32[]{:S(2)}) %collective-permute-start.2) | collective-permute-done | bytes 131104 | tf_op jit(solution)/shard_map/ppermute | solution.py:34
  8.4 0.4 %shard_map.49.halo = f32[384,256]{1,0:T(8,128)S(1)} custom-call(bf16[2,2,128,128]{3,2,1,0:T(8,128)(2,1)S(1)} %collective-permute-done.2.above.below, bf16[2,2,128,128]{3,2,1,0:T(8,128)(2,1)S(1)} %collective-permute-done.2.above.below, bf16[3,3,384,128]{3,2,1,0:T(8,128)(2,1)S(1)} %copy-done.2), custom_call_target="tpu_custom_call" | custom-call | flops 452984832 | bytes 1146880 | tf_op jit(solution)/shard_map/pallas_call | solution.py:299
  8.8 0.0 copy-start.1
  8.8 3.8 %collective-permute-done.1.frames = bf16[2,8,128,128]{3,2,1,0:T(8,128)(2,1)S(1)} collective-permute-done((bf16[2,8,128,128]{3,2,1,0:T(8,128)(2,1)}, bf16[2,8,128,128]{3,2,1,0:T(8,128)(2,1)S(1)}, u32[]{:S(2)}, u32[]{:S(2)}) %collective-permute-start.1) | collective-permute-done | bytes 524320 | tf_op jit(solution)/shard_map/ppermute | solution.py:28
  12.6 1.5 %shard_map.50.sums = f32[1152,256]{1,0:T(8,128)S(1)} custom-call(bf16[2,8,128,128]{3,2,1,0:T(8,128)(2,1)S(1)} %collective-permute-done.1.frames, bf16[3,3,384,128]{3,2,1,0:T(8,128)(2,1)S(1)} %copy-done.2, f32[1152,256]{1,0:T(8,128)S(1)} %shard_map.48.own, f32[384,256]{1,0:T(8,128)S(1)} %shard_map.49.halo), custom_call_target="tpu_custom_call" | custom-call | flops 1358954496 | bytes 2981888 | tf_op jit(solution)/shard_map/pallas_call | solution.py:299
  14.1 0.0 collective-permute-done.above.below
  14.2 0.0 copy-done.1
  14.2 0.0 copy-start
  14.2 0.7 %shard_map.51 = (bf16[1,64,256]{2,1,0:T(8,128)(2,1)S(1)}, f32[384,256]{1,0:T(8,128)S(1)}) custom-call(bf16[2,2,128,128]{3,2,1,0:T(8,128)(2,1)S(1)} %collective-permute-done.above.below, bf16[2,2,128,128]{3,2,1,0:T(8,128)(2,1)S(1)} %collective-permute-done.above.below, bf16[3,3,384,128]{3,2,1,0:T(8,128)(2,1)S(1)} %copy-done.2, ...), custom_call_target="tpu_custom_call" | custom-call | flops 452984832 | bytes 2916352 | tf_op jit(solution)/shard_map/pallas_call | solution.py:299
  14.9 0.6 %shard_map.52.field = bf16[1,4,64,256]{3,2,1,0:T(8,128)(2,1)S(1)} custom-call(f32[1152,256]{1,0:T(8,128)S(1)} %shard_map.50.sums, f32[384,256]{1,0:T(8,128)S(1)} %get-tuple-element.18.halo, bf16[3,384,256]{2,1,0:T(8,128)(2,1)S(1)} %copy-done.1), custom_call_target="tpu_custom_call" | custom-call | flops 452984832 | bytes 2162688 | tf_op jit(solution)/shard_map/pallas_call | solution.py:299
  15.5 0.1 collective-permute-start.6
  15.6 1.9 %collective-permute-start.3 = (bf16[1,4,64,256]{3,2,1,0:T(8,128)(2,1)S(1)}, bf16[1,4,64,256]{3,2,1,0:T(8,128)(2,1)S(1)}, u32[]{:S(2)}, u32[]{:S(2)}) collective-permute-start(bf16[1,4,64,256]{3,2,1,0:T(8,128)(2,1)S(1)} %shard_map.52.field), channel_id=1, source_target_pairs={{0,4},{1,5},{2,6},{3,7},{4,8},{5,9},{6,10},{7,11},{8,12},{9,13},{1... | collective-permute-start | bytes 393224 | tf_op jit(solution)/shard_map/ppermute | solution.py:23
  17.5 1.4 %collective-permute-start.4 = (bf16[1,64,256]{2,1,0:T(8,128)(2,1)S(1)}, bf16[1,64,256]{2,1,0:T(8,128)(2,1)S(1)}, u32[]{:S(2)}, u32[]{:S(2)}) collective-permute-start(bf16[1,64,256]{2,1,0:T(8,128)(2,1)S(1)} %get-tuple-element.19), channel_id=1, source_target_pairs={{0,1},{1,0},{2,3},{3,2},{4,5},{5,4},{6,7},{7,6},{8,9},{9,8},{10,11... | collective-permute-start | bytes 98312 | tf_op jit(solution)/shard_map/ppermute | solution.py:34
  18.9 2.6 %collective-permute-done.4.rim = bf16[1,64,256]{2,1,0:T(8,128)(2,1)S(1)} collective-permute-done((bf16[1,64,256]{2,1,0:T(8,128)(2,1)S(1)}, bf16[1,64,256]{2,1,0:T(8,128)(2,1)S(1)}, u32[]{:S(2)}, u32[]{:S(2)}) %collective-permute-start.4) | collective-permute-done | bytes 32800 | tf_op jit(solution)/shard_map/ppermute | solution.py:34
  21.5 0.0 collective-permute-start.7
  21.5 4.3 %collective-permute-start.5 = (bf16[1,64,256]{2,1,0:T(8,128)(2,1)S(1)}, bf16[1,64,256]{2,1,0:T(8,128)(2,1)S(1)}, u32[]{:S(2)}, u32[]{:S(2)}) collective-permute-start(bf16[1,64,256]{2,1,0:T(8,128)(2,1)S(1)} %collective-permute-done.4.rim), channel_id=1, source_target_pairs={{0,4},{1,5},{2,6},{3,7},{4,8},{5,9},{6,10},{7,11},{8,12},{9,13},{1... | collective-permute-start | bytes 98312 | tf_op jit(solution)/shard_map/ppermute | solution.py:23
  25.8 0.0 copy-done
  25.8 0.5 %shard_map.53.total = f32[256,256]{1,0:T(8,128)S(1)} custom-call(bf16[1,4,64,256]{3,2,1,0:T(8,128)(2,1)S(1)} %shard_map.52.field, bf16[1,64,256]{2,1,0:T(8,128)(2,1)S(1)} %collective-permute-done.4.rim, bf16[3,3,768,256]{3,2,1,0:T(8,128)(2,1)S(1)} %copy-done), custom_call_target="tpu_custom_call" | custom-call | flops 301989888 | bytes 3702784 | tf_op jit(solution)/shard_map/pallas_call | solution.py:299
  26.3 0.0 collective-permute-done.7.direct_rim
  26.3 1.1 %collective-permute-done.5.rim = bf16[1,64,256]{2,1,0:T(8,128)(2,1)S(1)} collective-permute-done((bf16[1,64,256]{2,1,0:T(8,128)(2,1)S(1)}, bf16[1,64,256]{2,1,0:T(8,128)(2,1)S(1)}, u32[]{:S(2)}, u32[]{:S(2)}) %collective-permute-start.5) | collective-permute-done | bytes 32800 | tf_op jit(solution)/shard_map/ppermute | solution.py:23
  27.4 0.0 collective-permute-done.6.direct
  27.4 0.0 collective-permute-done.3.field
  27.4 0.0 collective-permute-start.8
  27.4 0.5 %collective-permute-start.9 = (bf16[1,64,256]{2,1,0:T(8,128)(2,1)S(1)}, bf16[1,64,256]{2,1,0:T(8,128)(2,1)S(1)}, u32[]{:S(2)}, u32[]{:S(2)}) collective-permute-start(bf16[1,64,256]{2,1,0:T(8,128)(2,1)S(1)} %collective-permute-done.5.rim), channel_id=1, source_target_pairs={{0,2},{2,0},{4,6},{6,4},{8,10},{10,8},{12,14},{14,12},{16,18},{18,... | collective-permute-start | bytes 98312 | tf_op jit(solution)/shard_map/ppermute | solution.py:38
  27.9 0.5 %shard_map.54.total = f32[256,256]{1,0:T(8,128)S(1)} custom-call(bf16[1,4,64,256]{3,2,1,0:T(8,128)(2,1)S(1)} %collective-permute-done.3.field, bf16[1,64,256]{2,1,0:T(8,128)(2,1)S(1)} %collective-permute-done.5.rim, bf16[3,3,768,256]{3,2,1,0:T(8,128)(2,1)S(1)} %copy-done, f32[256,256]{1,0:T(8,128)S(1)} %shard_map.53.total), custom_call_target="tpu_custom_call" | custom-call | flops 301989888 | bytes 3964928 | tf_op jit(solution)/shard_map/pallas_call | solution.py:299
  28.4 0.4 %collective-permute-done.9.relayed_rim = bf16[1,64,256]{2,1,0:T(8,128)(2,1)S(1)} collective-permute-done((bf16[1,64,256]{2,1,0:T(8,128)(2,1)S(1)}, bf16[1,64,256]{2,1,0:T(8,128)(2,1)S(1)}, u32[]{:S(2)}, u32[]{:S(2)}) %collective-permute-start.9) | collective-permute-done | bytes 32800 | tf_op jit(solution)/shard_map/ppermute | solution.py:38
  28.8 0.0 collective-permute-done.8.relayed
  28.8 1.2 %shard_map.55 = bf16[1,4,64,256]{3,2,1,0:T(8,128)(2,1)} custom-call(bf16[1,4,64,256]{3,2,1,0:T(8,128)(2,1)S(1)} %collective-permute-done.6.direct, bf16[1,64,256]{2,1,0:T(8,128)(2,1)S(1)} %collective-permute-done.7.direct_rim, bf16[1,4,64,256]{3,2,1,0:T(8,128)(2,1)S(1)} %collective-permute-done.8.relayed, ...), custom_call_target="tpu_custom_call" | custom-call | flops 301989888 | bytes 4128768 | tf_op jit(solution)/shard_map/pallas_call | solution.py:299
  (2 shorter events, 0.0 us)
Async XLA Ops:
  0.0 1.0 %copy-start.3 = (bf16[2,8,128,128]{3,2,1,0:T(8,128)(2,1)S(1)}, bf16[2,8,128,128]{3,2,1,0:T(8,128)(2,1)}, u32[]{:S(2)}) copy-start(bf16[2,8,128,128]{3,2,1,0:T(8,128)(2,1)} %frames.1) | copy-start | bytes 1572868
  0.0 6.4 %copy-start.2 = (bf16[3,3,384,128]{3,2,1,0:T(8,128)(2,1)S(1)}, bf16[3,3,384,128]{3,2,1,0:T(8,128)(2,1)}, u32[]{:S(2)}) copy-start(bf16[3,3,384,128]{3,2,1,0:T(8,128)(2,1)} %weight.10) | copy-start | bytes 2654212
  0.0 12.6 %collective-permute-start.1 = (bf16[2,8,128,128]{3,2,1,0:T(8,128)(2,1)}, bf16[2,8,128,128]{3,2,1,0:T(8,128)(2,1)S(1)}, u32[]{:S(2)}, u32[]{:S(2)}) collective-permute-start(bf16[2,8,128,128]{3,2,1,0:T(8,128)(2,1)} %frames.1), channel_id=1, source_target_pairs={{0,2},{2,4},{4,6},{6,8},{8,10},{10,12},{12,14},{14,16},{16,18},{18... | collective-permute-start | bytes 1572872 | tf_op jit(solution)/shard_map/ppermute | solution.py:28
  1.1 7.3 %collective-permute-start.2 = (bf16[2,2,128,128]{3,2,1,0:T(8,128)(2,1)S(1)}, bf16[2,2,128,128]{3,2,1,0:T(8,128)(2,1)S(1)}, u32[]{:S(2)}, u32[]{:S(2)}) collective-permute-start(bf16[2,2,128,128]{3,2,1,0:T(8,128)(2,1)S(1)} %shard_map.47), channel_id=1, source_target_pairs={{0,1},{1,0},{2,3},{3,2},{4,5},{5,4},{6,7},{7,6},{8,9},{9,8},{10,11... | collective-permute-start | bytes 393224 | tf_op jit(solution)/shard_map/ppermute | solution.py:34
  4.1 10.0 %collective-permute-start = (bf16[2,2,128,128]{3,2,1,0:T(8,128)(2,1)S(1)}, bf16[2,2,128,128]{3,2,1,0:T(8,128)(2,1)S(1)}, u32[]{:S(2)}, u32[]{:S(2)}) collective-permute-start(bf16[2,2,128,128]{3,2,1,0:T(8,128)(2,1)S(1)} %shard_map.47), channel_id=1, source_target_pairs={{0,3},{1,2},{2,5},{3,4},{4,7},{5,6},{6,9},{7,8},{8,11},{9,10},{10,... | collective-permute-start | bytes 393224 | tf_op jit(solution)/shard_map/ppermute | solution.py:34
  8.8 5.4 %copy-start.1 = (bf16[3,384,256]{2,1,0:T(8,128)(2,1)S(1)}, bf16[3,384,256]{2,1,0:T(8,128)(2,1)}, u32[]{:S(2)}) copy-start(bf16[3,384,256]{2,1,0:T(8,128)(2,1)} %down.3) | copy-start | bytes 1769476
  14.2 11.7 %copy-start = (bf16[3,3,768,256]{3,2,1,0:T(8,128)(2,1)S(1)}, bf16[3,3,768,256]{3,2,1,0:T(8,128)(2,1)}, u32[]{:S(2)}) copy-start(bf16[3,3,768,256]{3,2,1,0:T(8,128)(2,1)} %weight.13) | copy-start | bytes 10616836
  15.5 11.9 %collective-permute-start.6 = (bf16[1,4,64,256]{3,2,1,0:T(8,128)(2,1)S(1)}, bf16[1,4,64,256]{3,2,1,0:T(8,128)(2,1)S(1)}, u32[]{:S(2)}, u32[]{:S(2)}) collective-permute-start(bf16[1,4,64,256]{3,2,1,0:T(8,128)(2,1)S(1)} %shard_map.52.field), channel_id=1, source_target_pairs={{0,2},{2,0},{4,6},{6,4},{8,10},{10,8},{12,14},{14,12},{16,18},{18,... | collective-permute-start | bytes 393224 | tf_op jit(solution)/shard_map/ppermute | solution.py:38
  15.6 11.8 %collective-permute-start.3 = (bf16[1,4,64,256]{3,2,1,0:T(8,128)(2,1)S(1)}, bf16[1,4,64,256]{3,2,1,0:T(8,128)(2,1)S(1)}, u32[]{:S(2)}, u32[]{:S(2)}) collective-permute-start(bf16[1,4,64,256]{3,2,1,0:T(8,128)(2,1)S(1)} %shard_map.52.field), channel_id=1, source_target_pairs={{0,4},{1,5},{2,6},{3,7},{4,8},{5,9},{6,10},{7,11},{8,12},{9,13},{1... | collective-permute-start | bytes 393224 | tf_op jit(solution)/shard_map/ppermute | solution.py:23
  17.5 4.0 %collective-permute-start.4 = (bf16[1,64,256]{2,1,0:T(8,128)(2,1)S(1)}, bf16[1,64,256]{2,1,0:T(8,128)(2,1)S(1)}, u32[]{:S(2)}, u32[]{:S(2)}) collective-permute-start(bf16[1,64,256]{2,1,0:T(8,128)(2,1)S(1)} %get-tuple-element.19), channel_id=1, source_target_pairs={{0,1},{1,0},{2,3},{3,2},{4,5},{5,4},{6,7},{7,6},{8,9},{9,8},{10,11... | collective-permute-start | bytes 98312 | tf_op jit(solution)/shard_map/ppermute | solution.py:34
  21.5 4.8 %collective-permute-start.7 = (bf16[1,64,256]{2,1,0:T(8,128)(2,1)S(1)}, bf16[1,64,256]{2,1,0:T(8,128)(2,1)S(1)}, u32[]{:S(2)}, u32[]{:S(2)}) collective-permute-start(bf16[1,64,256]{2,1,0:T(8,128)(2,1)S(1)} %collective-permute-done.4.rim), channel_id=1, source_target_pairs={{0,2},{2,0},{4,6},{6,4},{8,10},{10,8},{12,14},{14,12},{16,18},{18,... | collective-permute-start | bytes 98312 | tf_op jit(solution)/shard_map/ppermute | solution.py:38
  21.5 5.9 %collective-permute-start.5 = (bf16[1,64,256]{2,1,0:T(8,128)(2,1)S(1)}, bf16[1,64,256]{2,1,0:T(8,128)(2,1)S(1)}, u32[]{:S(2)}, u32[]{:S(2)}) collective-permute-start(bf16[1,64,256]{2,1,0:T(8,128)(2,1)S(1)} %collective-permute-done.4.rim), channel_id=1, source_target_pairs={{0,4},{1,5},{2,6},{3,7},{4,8},{5,9},{6,10},{7,11},{8,12},{9,13},{1... | collective-permute-start | bytes 98312 | tf_op jit(solution)/shard_map/ppermute | solution.py:23
  27.4 1.4 %collective-permute-start.8 = (bf16[1,4,64,256]{3,2,1,0:T(8,128)(2,1)S(1)}, bf16[1,4,64,256]{3,2,1,0:T(8,128)(2,1)S(1)}, u32[]{:S(2)}, u32[]{:S(2)}) collective-permute-start(bf16[1,4,64,256]{3,2,1,0:T(8,128)(2,1)S(1)} %collective-permute-done.3.field), channel_id=1, source_target_pairs={{0,2},{2,0},{4,6},{6,4},{8,10},{10,8},{12,14},{14,12},{16,18},{18,... | collective-permute-start | bytes 393224 | tf_op jit(solution)/shard_map/ppermute | solution.py:38
  27.4 1.4 %collective-permute-start.9 = (bf16[1,64,256]{2,1,0:T(8,128)(2,1)S(1)}, bf16[1,64,256]{2,1,0:T(8,128)(2,1)S(1)}, u32[]{:S(2)}, u32[]{:S(2)}) collective-permute-start(bf16[1,64,256]{2,1,0:T(8,128)(2,1)S(1)} %collective-permute-done.5.rim), channel_id=1, source_target_pairs={{0,2},{2,0},{4,6},{6,4},{8,10},{10,8},{12,14},{14,12},{16,18},{18,... | collective-permute-start | bytes 98312 | tf_op jit(solution)/shard_map/ppermute | solution.py:38

commit v3 on v2

--- a/solution.py
+++ b/solution.py
@@ -254,19 +254,16 @@
     out[...] = down_conv(pooled, half_rows, half_cols, down).reshape(out.shape)
 
 
-def coarse_sum(field, rim, weight, a):
+def column_taps(flat, cols):
+    left, right = shifted_columns(flat, cols)
+    return jnp.concatenate([left, flat, right], axis=1)
+
+
+def coarse_sum(field, weight, a):
     _, rows, cols, channels = field.shape
-    zero = jnp.zeros((cols, channels), BF16)
-    flat = jnp.concatenate(
-        [
-            jnp.where(has_above(), rim[0], zero),
-            field.reshape(rows * cols, channels),
-            jnp.where(has_below(), rim[rim.shape[0] - 1], zero),
-        ],
-        axis=0,
-    )
-    left, right = shifted_columns(flat, cols)
-    taps = jnp.concatenate([left, flat, right], axis=1)
+    zero = jnp.zeros((cols, 3 * channels), BF16)
+    taps = column_taps(field.reshape(rows * cols, channels), cols)
+    taps = jnp.concatenate([zero, taps, zero], axis=0)
     total = None
     for b in range(3):
         part = jnp.dot(
@@ -276,31 +273,67 @@
     return total
 
 
-def coarse_first_kernel(field, rim, weight, out):
-    out[...] = coarse_sum(field[...], rim[...], weight, 2)
-
-
-def coarse_next_kernel(field, rim, weight, total, out):
-    part = coarse_sum(field[...], rim[...], weight, 0)
+def coarse_first_kernel(field, weight, out):
+    out[...] = coarse_sum(field[...], weight, 2)
+
+
+def coarse_next_kernel(field, weight, total, out):
+    part = coarse_sum(field[...], weight, 0)
     out[...] = total[...] + jnp.where(has_earlier(2), part, 0.0)
 
 
-def coarse_last_kernel(direct, direct_rim, relayed, relayed_rim, weight, total, out):
-    odd = lax.axis_index("tm") % 2 == 1
-    field = jnp.where(odd, direct[...], relayed[...])
-    rim = jnp.where(odd, direct_rim[...], relayed_rim[...])
-    part = coarse_sum(field, rim, weight, 1)
-    total = total[...] + jnp.where(has_earlier(1), part, 0.0)
-    out[...] = silu(total).astype(BF16).reshape(out.shape)
-
-
-def call(kernel, out_shape, scratch, flops, args):
+def from_pair(direct, relayed):
+    return jnp.where(lax.axis_index("tm") % 2 == 1, direct[...], relayed[...])
+
+
+def coarse_body_kernel(direct, relayed, weight, total, out, ends):
+    _, rows, cols, _ = out.shape
+    part = coarse_sum(from_pair(direct, relayed), weight, 1)
+    sums = total[...] + jnp.where(has_earlier(1), part, 0.0)
+    out[...] = silu(sums).astype(BF16).reshape(out.shape)
+    head, tail = sums[:cols], sums[(rows - 1) * cols :]
+    if ends.shape[0] == 1:
+        ends[0] = jnp.where(has_above(), head, tail)
+    else:
+        ends[0], ends[1] = head, tail
+
+
+def coarse_ends_kernel(rim_0, direct, relayed, rim_2, weight, sums, _, out, row, sem):
+    rows, cols = out.shape[1:3]
+    sides = sums.shape[0]
+    rims = [
+        jnp.where(has_earlier(2), rim_0[...], jnp.zeros_like(rim_0[...])),
+        jnp.where(has_earlier(1), from_pair(direct, relayed), jnp.zeros_like(direct[...])),
+        rim_2[...],
+    ]
+    strip = lax.axis_index("rows")
+    copies = []
+    for side in range(sides):
+        taps = jnp.concatenate([column_taps(rim[side], cols) for rim in rims], axis=1)
+        if sides == 1:
+            b, p = 2 * (1 - strip), (rows - 1) * (1 - strip)
+        else:
+            b, p = 2 * side, (rows - 1) * side
+            taps = jnp.where((has_above(), has_below())[side], taps, jnp.zeros_like(taps))
+        kernel = weight[:, b].reshape(taps.shape[1], -1)
+        total = sums[side] + jnp.dot(taps, kernel, preferred_element_type=F32)
+        row[side] = silu(total).astype(BF16)
+        copies.append(pltpu.make_async_copy(row.at[side], out.at[0, p], sem.at[side]))
+        copies[-1].start()
+    for copy in copies:
+        copy.wait()
+
+
+def call(kernel, out_shape, scratch, flops, args, in_place=False):
     size = sum(a.size * a.dtype.itemsize for a in args)
+    vmem = pl.BlockSpec(memory_space=pltpu.VMEM)
+    last = pl.BlockSpec(memory_space=pl.ANY) if in_place else vmem
     return pl.pallas_call(
         kernel,
         out_shape=out_shape,
-        in_specs=[pl.BlockSpec(memory_space=pltpu.VMEM)] * len(args),
-        out_specs=jax.tree.map(lambda _: pl.BlockSpec(memory_space=pltpu.VMEM), out_shape),
+        in_specs=[vmem] * (len(args) - 1) + [last] if args else [],
+        out_specs=last if in_place else jax.tree.map(lambda _: vmem, out_shape),
+        input_output_aliases={len(args) - 1: 0} if in_place else {},
         scratch_shapes=scratch,
         cost_estimate=pl.CostEstimate(flops=flops, bytes_accessed=size, transcendentals=0),
         compiler_params=pltpu.CompilerParams(vmem_limit_bytes=20 * 1024 * 1024),
@@ -354,24 +387,28 @@
     rim_2 = moved(rim, 2, 0)
     sums = jax.ShapeDtypeStruct((half_rows * half_cols, wide), F32)
     flops = 2 * half_rows * half_cols * 9 * wide * wide
-    total = call(coarse_first_kernel, sums, [], flops, (field, rim, conv_coarse))
+    total = call(coarse_first_kernel, sums, [], flops, (field, conv_coarse))
     near = paired if times % 2 == 0 else functools.partial(ring, steps=1)
     direct = near(field)
     direct_rim = near(rim)
-    field_2, rim_2, total, direct, direct_rim = lax.optimization_barrier(
-        (field_2, rim_2, total, direct, direct_rim)
-    )
-    if times % 2 == 0:
-        relayed, relayed_rim = paired(field_2), paired(rim_2)
-    else:
-        relayed, relayed_rim = direct, direct_rim
-    total = call(coarse_next_kernel, sums, [], flops, (field_2, rim_2, conv_coarse, total))
+    field_2, total, direct, direct_rim = lax.optimization_barrier(
+        (field_2, total, direct, direct_rim)
+    )
+    relayed = paired(field_2) if times % 2 == 0 else direct
+    total = call(coarse_next_kernel, sums, [], flops, (field_2, conv_coarse, total))
+    rims = jax.ShapeDtypeStruct((sides, half_cols, wide), F32)
+    body, body_ends = call(
+        coarse_body_kernel, (shape, rims), [], flops, (direct, relayed, conv_coarse, total)
+    )
+    rim_2, body, body_ends = lax.optimization_barrier((rim_2, body, body_ends))
+    relayed_rim = paired(rim_2) if times % 2 == 0 else direct_rim
     return call(
-        coarse_last_kernel,
+        coarse_ends_kernel,
         shape,
-        [],
-        flops,
-        (direct, direct_rim, relayed, relayed_rim, conv_coarse, total),
+        [pltpu.VMEM(ends.shape, BF16), pltpu.SemaphoreType.DMA((sides,))],
+        flops // 4,
+        (rim_2, direct_rim, relayed_rim, rim, conv_coarse, body_ends, body),
+        in_place=True,
     )
 
 

time: 30.1 us -> 31.6 us (1.050)
  the two profiles are of different devices: /device:TPU:0 before, /device:TPU:16 now
where the time goes in v3:
time: 31.6 us; the launch traced here: 31.1 us
  waiting for transfers between devices  11.1 us (35%)
  starting transfers between devices  10.8 us (34%)
  Pallas kernels  7.95 us (25%)
  local copies, waits for them, and re-layouts  1.03 us (3%)
    pallas_call x11, Pallas kernels, call(): pl.pallas_call(kernel, out_shape=out_shape, in_specs=[vmem] * (len(args)...  7.95 us
    ppermute x2, starting transfers between devices, moved(): return lax.ppermute(value, ('tm', 'rows'), pairs)  6.03 us
    ppermute x3, starting transfers between devices, swapped(): return lax.ppermute(value, ('tm', 'rows'), pairs)  4.7 us
    ppermute x3, waiting for transfers between devices, swapped(): return lax.ppermute(value, ('tm', 'rows'), pairs)  4.56 us
    ppermute x2, waiting for transfers between devices, moved(): return lax.ppermute(value, ('tm', 'rows'), pairs)  2.48 us
    ppermute x1, waiting for transfers between devices, ring(): return lax.ppermute(value, 'tm', [(t, (t + steps) % tm) for t in range(tm)])  2.17 us
    ppermute x4, waiting for transfers between devices, paired(): lax.ppermute(value, 'tm', [(t, t ^ 1) for t in range(lax.axis_size('tm'))])  1.93 us
    unnamed x8, local copies, waits for them, and re-layouts  1.03 us
  transfers between devices with their start and end apart: 10, of which 8 were waited for; matrix products, arithmetic and copies ran while one was open for 0% of the time, Pallas kernels for 18%

profile of v3, /device:TPU:16, one launch (start us, length us, event | category | flops | bytes accessed | tf_op | source)
XLA Modules:
  0.0 31.1 jit_solution(13690333839427388329)
XLA Ops:
  0.0 0.0 copy-start.3
  0.0 0.0 copy-start.2
  0.0 0.0 collective-permute-start.1
  0.0 1.0 %copy-done.3 = bf16[2,8,128,128]{3,2,1,0:T(8,128)(2,1)S(1)} copy-done((bf16[2,8,128,128]{3,2,1,0:T(8,128)(2,1)S(1)}, bf16[2,8,128,128]{3,2,1,0:T(8,128)(2,1)}, u32[]{:S(2)}) %copy-start.3) | copy-done | bytes 524312
  1.1 1.6 %collective-permute-start.2 = (bf16[2,2,128,128]{3,2,1,0:T(8,128)(2,1)S(1)}, bf16[2,2,128,128]{3,2,1,0:T(8,128)(2,1)S(1)}, u32[]{:S(2)}, u32[]{:S(2)}) collective-permute-start(bf16[2,2,128,128]{3,2,1,0:T(8,128)(2,1)S(1)} %shard_map.47), channel_id=1, source_target_pairs={{0,1},{1,0},{2,3},{3,2},{4,5},{5,4},{6,7},{7,6},{8,9},{9,8},{10,11... | collective-permute-start | bytes 393224 | tf_op jit(solution)/shard_map/ppermute | solution.py:34
  2.6 2.3 %collective-permute-start = (bf16[2,2,128,128]{3,2,1,0:T(8,128)(2,1)S(1)}, bf16[2,2,128,128]{3,2,1,0:T(8,128)(2,1)S(1)}, u32[]{:S(2)}, u32[]{:S(2)}) collective-permute-start(bf16[2,2,128,128]{3,2,1,0:T(8,128)(2,1)S(1)} %shard_map.47), channel_id=1, source_target_pairs={{0,3},{1,2},{2,5},{3,4},{4,7},{5,6},{6,9},{7,8},{8,11},{9,10},{10,... | collective-permute-start | bytes 393224 | tf_op jit(solution)/shard_map/ppermute | solution.py:34
  5.0 0.0 copy-done.2
  5.0 1.5 %shard_map.48.own = f32[1152,256]{1,0:T(8,128)S(1)} custom-call(bf16[2,8,128,128]{3,2,1,0:T(8,128)(2,1)S(1)} %copy-done.3, bf16[3,3,384,128]{3,2,1,0:T(8,128)(2,1)S(1)} %copy-done.2), custom_call_target="tpu_custom_call" | custom-call | flops 1358954496 | bytes 1409024 | tf_op jit(solution)/shard_map/pallas_call | solution.py:331
  6.5 0.6 %collective-permute-done.2.above.below = bf16[2,2,128,128]{3,2,1,0:T(8,128)(2,1)S(1)} collective-permute-done((bf16[2,2,128,128]{3,2,1,0:T(8,128)(2,1)S(1)}, bf16[2,2,128,128]{3,2,1,0:T(8,128)(2,1)S(1)}, u32[]{:S(2)}, u32[]{:S(2)}) %collective-permute-start.2) | collective-permute-done | bytes 131104 | tf_op jit(solution)/shard_map/ppermute | solution.py:34
  7.1 0.4 %shard_map.49.halo = f32[384,256]{1,0:T(8,128)S(1)} custom-call(bf16[2,2,128,128]{3,2,1,0:T(8,128)(2,1)S(1)} %collective-permute-done.2.above.below, bf16[2,2,128,128]{3,2,1,0:T(8,128)(2,1)S(1)} %collective-permute-done.2.above.below, bf16[3,3,384,128]{3,2,1,0:T(8,128)(2,1)S(1)} %copy-done.2), custom_call_target="tpu_custom_call" | custom-call | flops 452984832 | bytes 1146880 | tf_op jit(solution)/shard_map/pallas_call | solution.py:331
  7.5 0.0 copy-start.1
  7.5 2.2 %collective-permute-done.1.frames = bf16[2,8,128,128]{3,2,1,0:T(8,128)(2,1)S(1)} collective-permute-done((bf16[2,8,128,128]{3,2,1,0:T(8,128)(2,1)}, bf16[2,8,128,128]{3,2,1,0:T(8,128)(2,1)S(1)}, u32[]{:S(2)}, u32[]{:S(2)}) %collective-permute-start.1) | collective-permute-done | bytes 524320 | tf_op jit(solution)/shard_map/ppermute | solution.py:28
  9.7 1.5 %shard_map.50.sums = f32[1152,256]{1,0:T(8,128)S(1)} custom-call(bf16[2,8,128,128]{3,2,1,0:T(8,128)(2,1)S(1)} %collective-permute-done.1.frames, bf16[3,3,384,128]{3,2,1,0:T(8,128)(2,1)S(1)} %copy-done.2, f32[1152,256]{1,0:T(8,128)S(1)} %shard_map.48.own, f32[384,256]{1,0:T(8,128)S(1)} %shard_map.49.halo), custom_call_target="tpu_custom_call" | custom-call | flops 1358954496 | bytes 2981888 | tf_op jit(solution)/shard_map/pallas_call | solution.py:331
  11.3 0.8 %collective-permute-done.above.below = bf16[2,2,128,128]{3,2,1,0:T(8,128)(2,1)S(1)} collective-permute-done((bf16[2,2,128,128]{3,2,1,0:T(8,128)(2,1)S(1)}, bf16[2,2,128,128]{3,2,1,0:T(8,128)(2,1)S(1)}, u32[]{:S(2)}, u32[]{:S(2)}) %collective-permute-start) | collective-permute-done | bytes 131104 | tf_op jit(solution)/shard_map/ppermute | solution.py:34
  12.1 0.0 copy-done.1
  12.1 0.0 copy-start
  12.1 0.7 %shard_map.51 = (bf16[1,64,256]{2,1,0:T(8,128)(2,1)S(1)}, f32[384,256]{1,0:T(8,128)S(1)}) custom-call(bf16[2,2,128,128]{3,2,1,0:T(8,128)(2,1)S(1)} %collective-permute-done.above.below, bf16[2,2,128,128]{3,2,1,0:T(8,128)(2,1)S(1)} %collective-permute-done.above.below, bf16[3,3,384,128]{3,2,1,0:T(8,128)(2,1)S(1)} %copy-done.2, ...), custom_call_target="tpu_custom_call" | custom-call | flops 452984832 | bytes 2916352 | tf_op jit(solution)/shard_map/pallas_call | solution.py:331
  12.8 0.6 %shard_map.52.field = bf16[1,4,64,256]{3,2,1,0:T(8,128)(2,1)S(1)} custom-call(f32[1152,256]{1,0:T(8,128)S(1)} %shard_map.50.sums, f32[384,256]{1,0:T(8,128)S(1)} %get-tuple-element.23.halo, bf16[3,384,256]{2,1,0:T(8,128)(2,1)S(1)} %copy-done.1), custom_call_target="tpu_custom_call" | custom-call | flops 452984832 | bytes 2162688 | tf_op jit(solution)/shard_map/pallas_call | solution.py:331
  13.4 0.1 collective-permute-start.6
  13.5 2.5 %collective-permute-start.5 = (bf16[1,4,64,256]{3,2,1,0:T(8,128)(2,1)S(1)}, bf16[1,4,64,256]{3,2,1,0:T(8,128)(2,1)S(1)}, u32[]{:S(2)}, u32[]{:S(2)}) collective-permute-start(bf16[1,4,64,256]{3,2,1,0:T(8,128)(2,1)S(1)} %shard_map.52.field), channel_id=1, source_target_pairs={{0,4},{1,5},{2,6},{3,7},{4,8},{5,9},{6,10},{7,11},{8,12},{9,13},{1... | collective-permute-start | bytes 393224 | tf_op jit(solution)/shard_map/ppermute | solution.py:23
  16.0 0.8 %collective-permute-start.3 = (bf16[1,64,256]{2,1,0:T(8,128)(2,1)S(1)}, bf16[1,64,256]{2,1,0:T(8,128)(2,1)S(1)}, u32[]{:S(2)}, u32[]{:S(2)}) collective-permute-start(bf16[1,64,256]{2,1,0:T(8,128)(2,1)S(1)} %get-tuple-element.22), channel_id=1, source_target_pairs={{0,1},{1,0},{2,3},{3,2},{4,5},{5,4},{6,7},{7,6},{8,9},{9,8},{10,11... | collective-permute-start | bytes 98312 | tf_op jit(solution)/shard_map/ppermute | solution.py:34
  16.8 3.2 %collective-permute-done.3.rim_2 = bf16[1,64,256]{2,1,0:T(8,128)(2,1)S(1)} collective-permute-done((bf16[1,64,256]{2,1,0:T(8,128)(2,1)S(1)}, bf16[1,64,256]{2,1,0:T(8,128)(2,1)S(1)}, u32[]{:S(2)}, u32[]{:S(2)}) %collective-permute-start.3) | collective-permute-done | bytes 32800 | tf_op jit(solution)/shard_map/ppermute | solution.py:34
  20.0 0.0 collective-permute-start.7
  20.0 0.0 copy-done
  20.0 0.5 %shard_map.53.total = f32[256,256]{1,0:T(8,128)S(1)} custom-call(bf16[1,4,64,256]{3,2,1,0:T(8,128)(2,1)S(1)} %shard_map.52.field, bf16[3,3,768,256]{3,2,1,0:T(8,128)(2,1)S(1)} %copy-done), custom_call_target="tpu_custom_call" | custom-call | flops 301989888 | bytes 3670016 | tf_op jit(solution)/shard_map/pallas_call | solution.py:331
  20.5 0.7 %collective-permute-done.7.direct = bf16[1,64,256]{2,1,0:T(8,128)(2,1)S(1)} collective-permute-done((bf16[1,64,256]{2,1,0:T(8,128)(2,1)S(1)}, bf16[1,64,256]{2,1,0:T(8,128)(2,1)S(1)}, u32[]{:S(2)}, u32[]{:S(2)}) %collective-permute-start.7) | collective-permute-done | bytes 32800 | tf_op jit(solution)/shard_map/ppermute | solution.py:38
  21.2 0.0 collective-permute-done.6.direct
  21.2 1.0 %collective-permute-done.5.field = bf16[1,4,64,256]{3,2,1,0:T(8,128)(2,1)S(1)} collective-permute-done((bf16[1,4,64,256]{3,2,1,0:T(8,128)(2,1)S(1)}, bf16[1,4,64,256]{3,2,1,0:T(8,128)(2,1)S(1)}, u32[]{:S(2)}, u32[]{:S(2)}) %collective-permute-start.5) | collective-permute-done | bytes 131104 | tf_op jit(solution)/shard_map/ppermute | solution.py:23
  22.2 0.0 collective-permute-start.8
  22.2 3.5 %collective-permute-start.4 = (bf16[1,64,256]{2,1,0:T(8,128)(2,1)S(1)}, bf16[1,64,256]{2,1,0:T(8,128)(2,1)S(1)}, u32[]{:S(2)}, u32[]{:S(2)}) collective-permute-start(bf16[1,64,256]{2,1,0:T(8,128)(2,1)S(1)} %collective-permute-done.3.rim_2), channel_id=1, source_target_pairs={{0,4},{1,5},{2,6},{3,7},{4,8},{5,9},{6,10},{7,11},{8,12},{9,13},{1... | collective-permute-start | bytes 98312 | tf_op jit(solution)/shard_map/ppermute | solution.py:23
  25.7 0.5 %shard_map.54.total = f32[256,256]{1,0:T(8,128)S(1)} custom-call(bf16[1,4,64,256]{3,2,1,0:T(8,128)(2,1)S(1)} %collective-permute-done.5.field, bf16[3,3,768,256]{3,2,1,0:T(8,128)(2,1)S(1)} %copy-done, f32[256,256]{1,0:T(8,128)S(1)} %shard_map.53.total), custom_call_target="tpu_custom_call" | custom-call | flops 301989888 | bytes 3932160 | tf_op jit(solution)/shard_map/pallas_call | solution.py:331
  26.2 0.0 collective-permute-done.8.relayed
  26.2 1.2 %shard_map.55 = (bf16[1,4,64,256]{3,2,1,0:T(8,128)(2,1)}, f32[1,64,256]{2,1,0:T(8,128)S(1)}) custom-call(bf16[1,4,64,256]{3,2,1,0:T(8,128)(2,1)S(1)} %collective-permute-done.6.direct, bf16[1,4,64,256]{3,2,1,0:T(8,128)(2,1)S(1)} %collective-permute-done.8.relayed, bf16[3,3,768,256]{3,2,1,0:T(8,128)(2,1)S(1)} %copy-done, f32[256,256]{1,0:T(8,128)S(1)} %shard_map.54.total), custom_call_target="tpu_custom_call" | custom-call | flops 301989888 | bytes 4063232 | tf_op jit(solution)/shard_map/pallas_call | solution.py:331
  27.4 1.5 %collective-permute-done.4.rim_0 = bf16[1,64,256]{2,1,0:T(8,128)(2,1)S(1)} collective-permute-done((bf16[1,64,256]{2,1,0:T(8,128)(2,1)S(1)}, bf16[1,64,256]{2,1,0:T(8,128)(2,1)S(1)}, u32[]{:S(2)}, u32[]{:S(2)}) %collective-permute-start.4) | collective-permute-done | bytes 32800 | tf_op jit(solution)/shard_map/ppermute | solution.py:23
  28.9 0.0 collective-permute-start.9
  28.9 1.2 %collective-permute-done.9.relayed = bf16[1,64,256]{2,1,0:T(8,128)(2,1)S(1)} collective-permute-done((bf16[1,64,256]{2,1,0:T(8,128)(2,1)S(1)}, bf16[1,64,256]{2,1,0:T(8,128)(2,1)S(1)}, u32[]{:S(2)}, u32[]{:S(2)}) %collective-permute-start.9) | collective-permute-done | bytes 32800 | tf_op jit(solution)/shard_map/ppermute | solution.py:38
  30.1 1.0 %shard_map.56 = bf16[1,4,64,256]{3,2,1,0:T(8,128)(2,1)} custom-call(bf16[1,64,256]{2,1,0:T(8,128)(2,1)S(1)} %collective-permute-done.4.rim_0, bf16[1,64,256]{2,1,0:T(8,128)(2,1)S(1)} %collective-permute-done.7.direct, bf16[1,64,256]{2,1,0:T(8,128)(2,1)S(1)} %collective-permute-done.9.relayed, ...), custom_call_target="tpu_custom_call", output_to_operand_aliasing={{}: (6, {})} | custom-call | flops 75497472 | bytes 3866624 | tf_op jit(solution)/shard_map/pallas_call | solution.py:331
  (2 shorter events, 0.0 us)
Async XLA Ops:
  0.0 1.0 %copy-start.3 = (bf16[2,8,128,128]{3,2,1,0:T(8,128)(2,1)S(1)}, bf16[2,8,128,128]{3,2,1,0:T(8,128)(2,1)}, u32[]{:S(2)}) copy-start(bf16[2,8,128,128]{3,2,1,0:T(8,128)(2,1)} %frames.1) | copy-start | bytes 1572868
  0.0 4.9 %copy-start.2 = (bf16[3,3,384,128]{3,2,1,0:T(8,128)(2,1)S(1)}, bf16[3,3,384,128]{3,2,1,0:T(8,128)(2,1)}, u32[]{:S(2)}) copy-start(bf16[3,3,384,128]{3,2,1,0:T(8,128)(2,1)} %weight.11) | copy-start | bytes 2654212
  0.0 9.7 %collective-permute-start.1 = (bf16[2,8,128,128]{3,2,1,0:T(8,128)(2,1)}, bf16[2,8,128,128]{3,2,1,0:T(8,128)(2,1)S(1)}, u32[]{:S(2)}, u32[]{:S(2)}) collective-permute-start(bf16[2,8,128,128]{3,2,1,0:T(8,128)(2,1)} %frames.1), channel_id=1, source_target_pairs={{0,2},{2,4},{4,6},{6,8},{8,10},{10,12},{12,14},{14,16},{16,18},{18... | collective-permute-start | bytes 1572872 | tf_op jit(solution)/shard_map/ppermute | solution.py:28
  1.1 6.0 %collective-permute-start.2 = (bf16[2,2,128,128]{3,2,1,0:T(8,128)(2,1)S(1)}, bf16[2,2,128,128]{3,2,1,0:T(8,128)(2,1)S(1)}, u32[]{:S(2)}, u32[]{:S(2)}) collective-permute-start(bf16[2,2,128,128]{3,2,1,0:T(8,128)(2,1)S(1)} %shard_map.47), channel_id=1, source_target_pairs={{0,1},{1,0},{2,3},{3,2},{4,5},{5,4},{6,7},{7,6},{8,9},{9,8},{10,11... | collective-permute-start | bytes 393224 | tf_op jit(solution)/shard_map/ppermute | solution.py:34
  2.6 9.4 %collective-permute-start = (bf16[2,2,128,128]{3,2,1,0:T(8,128)(2,1)S(1)}, bf16[2,2,128,128]{3,2,1,0:T(8,128)(2,1)S(1)}, u32[]{:S(2)}, u32[]{:S(2)}) collective-permute-start(bf16[2,2,128,128]{3,2,1,0:T(8,128)(2,1)S(1)} %shard_map.47), channel_id=1, source_target_pairs={{0,3},{1,2},{2,5},{3,4},{4,7},{5,6},{6,9},{7,8},{8,11},{9,10},{10,... | collective-permute-start | bytes 393224 | tf_op jit(solution)/shard_map/ppermute | solution.py:34
  7.5 4.5 %copy-start.1 = (bf16[3,384,256]{2,1,0:T(8,128)(2,1)S(1)}, bf16[3,384,256]{2,1,0:T(8,128)(2,1)}, u32[]{:S(2)}) copy-start(bf16[3,384,256]{2,1,0:T(8,128)(2,1)} %down.3) | copy-start | bytes 1769476
  12.1 7.9 %copy-start = (bf16[3,3,768,256]{3,2,1,0:T(8,128)(2,1)S(1)}, bf16[3,3,768,256]{3,2,1,0:T(8,128)(2,1)}, u32[]{:S(2)}) copy-start(bf16[3,3,768,256]{3,2,1,0:T(8,128)(2,1)} %weight.15) | copy-start | bytes 10616836
  13.4 7.8 %collective-permute-start.6 = (bf16[1,4,64,256]{3,2,1,0:T(8,128)(2,1)S(1)}, bf16[1,4,64,256]{3,2,1,0:T(8,128)(2,1)S(1)}, u32[]{:S(2)}, u32[]{:S(2)}) collective-permute-start(bf16[1,4,64,256]{3,2,1,0:T(8,128)(2,1)S(1)} %shard_map.52.field), channel_id=1, source_target_pairs={{0,2},{2,0},{4,6},{6,4},{8,10},{10,8},{12,14},{14,12},{16,18},{18,... | collective-permute-start | bytes 393224 | tf_op jit(solution)/shard_map/ppermute | solution.py:38
  13.5 8.7 %collective-permute-start.5 = (bf16[1,4,64,256]{3,2,1,0:T(8,128)(2,1)S(1)}, bf16[1,4,64,256]{3,2,1,0:T(8,128)(2,1)S(1)}, u32[]{:S(2)}, u32[]{:S(2)}) collective-permute-start(bf16[1,4,64,256]{3,2,1,0:T(8,128)(2,1)S(1)} %shard_map.52.field), channel_id=1, source_target_pairs={{0,4},{1,5},{2,6},{3,7},{4,8},{5,9},{6,10},{7,11},{8,12},{9,13},{1... | collective-permute-start | bytes 393224 | tf_op jit(solution)/shard_map/ppermute | solution.py:23
  16.0 4.0 %collective-permute-start.3 = (bf16[1,64,256]{2,1,0:T(8,128)(2,1)S(1)}, bf16[1,64,256]{2,1,0:T(8,128)(2,1)S(1)}, u32[]{:S(2)}, u32[]{:S(2)}) collective-permute-start(bf16[1,64,256]{2,1,0:T(8,128)(2,1)S(1)} %get-tuple-element.22), channel_id=1, source_target_pairs={{0,1},{1,0},{2,3},{3,2},{4,5},{5,4},{6,7},{7,6},{8,9},{9,8},{10,11... | collective-permute-start | bytes 98312 | tf_op jit(solution)/shard_map/ppermute | solution.py:34
  20.0 1.2 %collective-permute-start.7 = (bf16[1,64,256]{2,1,0:T(8,128)(2,1)S(1)}, bf16[1,64,256]{2,1,0:T(8,128)(2,1)S(1)}, u32[]{:S(2)}, u32[]{:S(2)}) collective-permute-start(bf16[1,64,256]{2,1,0:T(8,128)(2,1)S(1)} %collective-permute-done.3.rim_2), channel_id=1, source_target_pairs={{0,2},{2,0},{4,6},{6,4},{8,10},{10,8},{12,14},{14,12},{16,18},{18,... | collective-permute-start | bytes 98312 | tf_op jit(solution)/shard_map/ppermute | solution.py:38
  22.2 4.0 %collective-permute-start.8 = (bf16[1,4,64,256]{3,2,1,0:T(8,128)(2,1)S(1)}, bf16[1,4,64,256]{3,2,1,0:T(8,128)(2,1)S(1)}, u32[]{:S(2)}, u32[]{:S(2)}) collective-permute-start(bf16[1,4,64,256]{3,2,1,0:T(8,128)(2,1)S(1)} %collective-permute-done.5.field), channel_id=1, source_target_pairs={{0,2},{2,0},{4,6},{6,4},{8,10},{10,8},{12,14},{14,12},{16,18},{18,... | collective-permute-start | bytes 393224 | tf_op jit(solution)/shard_map/ppermute | solution.py:38
  22.2 6.7 %collective-permute-start.4 = (bf16[1,64,256]{2,1,0:T(8,128)(2,1)S(1)}, bf16[1,64,256]{2,1,0:T(8,128)(2,1)S(1)}, u32[]{:S(2)}, u32[]{:S(2)}) collective-permute-start(bf16[1,64,256]{2,1,0:T(8,128)(2,1)S(1)} %collective-permute-done.3.rim_2), channel_id=1, source_target_pairs={{0,4},{1,5},{2,6},{3,7},{4,8},{5,9},{6,10},{7,11},{8,12},{9,13},{1... | collective-permute-start | bytes 98312 | tf_op jit(solution)/shard_map/ppermute | solution.py:23
  28.9 1.2 %collective-permute-start.9 = (bf16[1,64,256]{2,1,0:T(8,128)(2,1)S(1)}, bf16[1,64,256]{2,1,0:T(8,128)(2,1)S(1)}, u32[]{:S(2)}, u32[]{:S(2)}) collective-permute-start(bf16[1,64,256]{2,1,0:T(8,128)(2,1)S(1)} %collective-permute-done.4.rim_0), channel_id=1, source_target_pairs={{0,2},{2,0},{4,6},{6,4},{8,10},{10,8},{12,14},{14,12},{16,18},{18,... | collective-permute-start | bytes 98312 | tf_op jit(solution)/shard_map/ppermute | solution.py:38

commit v4 on v2

--- a/solution.py
+++ b/solution.py
@@ -65,13 +65,13 @@
     if lax.axis_size("rows") == 2:
         sent = call(
             edge_kernel,
-            jax.ShapeDtypeStruct((frames.shape[0], 2, *frames.shape[2:]), BF16),
+            jax.ShapeDtypeStruct((frames.shape[0], 1, *frames.shape[2:]), BF16),
             [],
             0,
             (pace, frames),
         )
         return [(both, both) for both in (swapped(sent, 0), swapped(sent, 1))]
-    head, tail = frames[:, :2], frames[:, rows - 1 :]
+    head, tail = frames[:, :1], frames[:, rows - 1 :]
     return [(moved(tail, steps, 1), moved(head, steps, -1)) for steps in (0, 1)]
 
 
@@ -130,7 +130,7 @@
 
 
 def chunks_of(count):
-    size = next(c for c in (3, 2, 1) if count % c == 0)
+    size = next(c for c in (4, 3, 2, 1) if count % c == 0)
     return [range(i, i + size) for i in range(0, count, size)]
 
 
@@ -140,36 +140,26 @@
     def row(f, i):
         return frames[f, i] if 0 <= i < rows else None
 
-    for outs in chunks_of(rows + 1):
+    for outs in chunks_of(rows):
         out[outs[0] * cols : (outs[-1] + 1) * cols] = fine_rows(row, outs, range(3), weight, 2)
 
 
-def halo_row(above, below, rows):
+def halo_sums(above, below, weight, first_tap, rows):
     def row(f, i):
         if i == -1:
-            cells, have = above[f, above.shape[1] - 1], has_above()
-        elif i >= rows:
-            cells, have = below[f, i - rows], has_below()
+            cells, have = above[f, 0], has_above()
         else:
-            return None
+            cells, have = below[f, 0], has_below()
         return jnp.where(have, cells, jnp.zeros_like(cells))
 
-    return row
-
-
-def halo_sum(above, below, weight, first_tap, rows):
-    row = halo_row(above, below, rows)
-    return jnp.concatenate(
-        [
-            fine_rows(row, [0], [0], weight, first_tap),
-            fine_rows(row, [rows - 1, rows], [1, 2], weight, first_tap),
-        ],
-        axis=0,
+    return (
+        fine_rows(row, [0], [0], weight, first_tap),
+        fine_rows(row, [rows - 1], [2], weight, first_tap),
     )
 
 
 def fine_halo_kernel(above, below, weight, out, *, rows):
-    out[...] = halo_sum(above, below, weight, 2, rows)
+    out[0], out[1] = halo_sums(above, below, weight, 2, rows)
 
 
 def silu(v):
@@ -182,13 +172,13 @@
     def row(f, i):
         return frames[f, i] if 0 <= i < rows else None
 
-    for outs in chunks_of(rows + 1):
+    for outs in chunks_of(rows):
         total = jnp.where(has_earlier(1), fine_rows(row, outs, range(3), weight, 0), 0.0)
         for i, r in enumerate(outs):
             line = total[i * cols : (i + 1) * cols] + own[r * cols : (r + 1) * cols]
-            for k, halo_r in enumerate((0, rows - 1, rows)):
+            for k, halo_r in enumerate((0, rows - 1)):
                 if r == halo_r:
-                    line = line + halo[k * cols : (k + 1) * cols]
+                    line = line + halo[k]
             out[r * cols : (r + 1) * cols] = line
 
 
@@ -198,70 +188,84 @@
     return ((fine[:, :channels] + fine[:, channels:]) * 0.5).astype(BF16).astype(F32)
 
 
-def down_conv(pooled, half_rows, half_cols, down):
-    strips = []
-    for p in range(half_rows):
-        pieces = [
-            pooled[2 * p + b, pl.ds(e, half_cols, stride=2), :].astype(BF16)
-            for b in range(3)
-            for e in range(3)
-        ]
-        strips.append(jnp.concatenate(pieces, axis=1))
-    left = jnp.concatenate(strips, axis=0)
-    right = down[...].reshape(-1, down.shape[-1])
-    return jnp.dot(left, right, preferred_element_type=F32).astype(BF16)
-
-
-def ends_kernel(above, below, weight, sums, down, out, halo, pooled):
+def down_taps(pooled, first, row_taps, half_cols):
+    pieces = [
+        pooled[first + i, pl.ds(e, half_cols, stride=2), :].astype(BF16)
+        for i in range(row_taps)
+        for e in range(3)
+    ]
+    return jnp.concatenate(pieces, axis=1)
+
+
+def put_pooled(pooled, lines):
+    cols = lines[0].shape[0]
+    pad = pooled.shape[1] - cols
+    pooled[:, cols:] = jnp.zeros((pooled.shape[0], pad, pooled.shape[2]), F32)
+    for i, line in enumerate(lines):
+        pooled[i, :cols] = line
+
+
+def ends_kernel(above, below, weight, sums, down, sent, kept, first, pooled):
     cols = above.shape[2]
-    rows = sums.shape[0] // cols - 1
-    added = halo_sum(above, below, weight, 0, rows)
-    halo[...] = added
-    channels = pooled.shape[2]
-    pooled[:, cols:] = jnp.zeros((3, pooled.shape[1] - cols, channels), F32)
-    zero = jnp.zeros((cols, added.shape[1]), F32)
-    if out.shape[0] == 1:
-        starts = [(jnp.where(has_above(), 0, rows - 2), added)]
+    rows = sums.shape[0] // cols
+    half_cols = cols // 2
+    top, bottom = halo_sums(above, below, weight, 0, rows)
+    lines = []
+    for r in (0, 1, 2, rows - 2, rows - 1):
+        line = sums[r * cols : (r + 1) * cols]
+        if r == 0:
+            line = line + top
+        if r == rows - 1:
+            line = line + bottom
+        lines.append(pool(line))
+    put_pooled(pooled, lines)
+    dot = functools.partial(jnp.dot, preferred_element_type=F32)
+    flat = down[...].reshape(-1, down.shape[-1])
+    third = down.shape[1]
+    head = dot(down_taps(pooled, 0, 3, half_cols), flat).astype(BF16)
+    added = dot(down_taps(pooled, 0, 1, half_cols), down[2])
+    tail = dot(down_taps(pooled, 3, 2, half_cols), flat[: 2 * third])
+    first[...] = head
+    kept[0], kept[1] = added, tail
+    if sent.shape[0] == 2:
+        sent[0] = jnp.where(has_above(), head, tail.astype(BF16))
+        sent[1] = added.astype(BF16)
     else:
-        first = jnp.concatenate([added[:cols], zero, zero], axis=0)
-        last = jnp.concatenate([zero, added[cols:]], axis=0)
-        starts = [(0, first), (rows - 2, last)]
-    for side, (start, more) in enumerate(starts):
-        begin = pl.multiple_of(start * cols, cols)
-        mean = pool(sums[pl.ds(begin, 3 * cols), :] + more)
-        for i in range(3):
-            line = mean[i * cols : (i + 1) * cols]
-            if side == 1 and i == 2:
-                line = jnp.where(has_below(), line, 0.0)
-            pooled[i, :cols] = line
-        out[side] = down_conv(pooled, 1, cols // 2, down)
-
-
-def reduce_kernel(sums, halo, down, out, pooled):
-    _, half_rows, half_cols, _ = out.shape
-    rows, cols = 2 * half_rows, 2 * half_cols
-    channels = pooled.shape[2]
-    pooled[:, cols:] = jnp.zeros((rows + 1, pooled.shape[1] - cols, channels), F32)
-    for r in range(rows + 1):
-        line = sums[r * cols : (r + 1) * cols]
-        for k, halo_r in enumerate((0, rows - 1, rows)):
-            if r == halo_r:
-                line = line + halo[k * cols : (k + 1) * cols]
-        mean = pool(line)
-        if r == rows:
-            mean = jnp.where(has_below(), mean, 0.0)
-        pooled[r, :cols] = mean
-    out[...] = down_conv(pooled, half_rows, half_cols, down).reshape(out.shape)
-
-
-def coarse_sum(field, rim, weight, a):
-    _, rows, cols, channels = field.shape
+        sent[0], sent[1], sent[2] = head, added.astype(BF16), tail.astype(BF16)
+
+
+def reduce_kernel(sums, first, down, out, pooled):
+    _, count, half_cols, _ = out.shape
+    cols = 2 * half_cols
+    put_pooled(pooled, [pool(sums[r * cols : (r + 1) * cols]) for r in range(2, 2 * count + 1)])
+    left = [down_taps(pooled, 2 * p, 3, half_cols) for p in range(count - 1)]
+    flat = down[...].reshape(-1, down.shape[-1])
+    rest = jnp.dot(jnp.concatenate(left, axis=0), flat, preferred_element_type=F32)
+    out[0, 0] = first[...]
+    out[0, 1:] = rest.astype(BF16).reshape(count - 1, half_cols, -1)
+
+
+def edge_rows_kernel(above, below, kept, out):
+    added, tail = kept[0], kept[1]
+    more = jnp.where(has_below(), below[1].astype(F32), 0.0)
+    out[0, 0] = (tail + more).astype(BF16)
+    upper = (above[0].astype(F32) + added).astype(BF16)
+    if out.shape[1] == 2:
+        out[0, 1] = jnp.where(has_above(), upper, below[0])
+    else:
+        out[0, 1], out[0, 2] = upper, below[0]
+
+
+def coarse_sum(main, edge, weight, a):
+    _, count, cols, channels = main.shape
+    rows = count + 1
     zero = jnp.zeros((cols, channels), BF16)
     flat = jnp.concatenate(
         [
-            jnp.where(has_above(), rim[0], zero),
-            field.reshape(rows * cols, channels),
-            jnp.where(has_below(), rim[rim.shape[0] - 1], zero),
+            jnp.where(has_above(), edge[0, 1], zero),
+            main[0].reshape(count * cols, channels),
+            edge[0, 0],
+            jnp.where(has_below(), edge[0, edge.shape[1] - 1], zero),
         ],
         axis=0,
     )
@@ -276,12 +280,12 @@
     return total
 
 
-def coarse_first_kernel(field, rim, weight, out):
-    out[...] = coarse_sum(field[...], rim[...], weight, 2)
-
-
-def coarse_next_kernel(field, rim, weight, total, out):
-    part = coarse_sum(field[...], rim[...], weight, 0)
+def coarse_first_kernel(main, edge, weight, out):
+    out[...] = coarse_sum(main[...], edge[...], weight, 2)
+
+
+def coarse_next_kernel(main, edge, weight, total, out):
+    part = coarse_sum(main[...], edge[...], weight, 0)
     out[...] = total[...] + jnp.where(has_earlier(2), part, 0.0)
 
 
@@ -315,42 +319,52 @@
 
     earlier = ring(frames, 1)
     (above, below), (above_1, below_1) = frame_rims(pace, frames)
-    size = (rows + 1) * cols
+    size = rows * cols
     pair = jax.ShapeDtypeStruct((size, 2 * channels), F32)
     flops = 2 * size * 18 * channels * 2 * channels
     own = call(fine_own_kernel, pair, [], flops, (frames, conv_fine))
     halo = call(
         functools.partial(fine_halo_kernel, rows=rows),
-        jax.ShapeDtypeStruct((3 * cols, 2 * channels), F32),
+        jax.ShapeDtypeStruct((2, cols, 2 * channels), F32),
         [],
         flops // 3,
         (above, below, conv_fine),
     )
     half_rows, half_cols = rows // 2, cols // 2
     shape = jax.ShapeDtypeStruct((1, half_rows, half_cols, wide), BF16)
-    sides = 1 if strips == 2 else 2
-    halo_sums = jax.ShapeDtypeStruct((3 * cols, 2 * channels), F32)
+    two = strips == 2
     fine_sums = call(fine_rest_kernel, pair, [], flops, (earlier, conv_fine, own, halo))
     above_1, below_1, fine_sums = lax.optimization_barrier((above_1, below_1, fine_sums))
-    ends, halo_1 = call(
+    sent, kept, first = call(
         ends_kernel,
-        (jax.ShapeDtypeStruct((sides, half_cols, wide), BF16), halo_sums),
-        [pltpu.VMEM((3, cols + 8, channels), F32)],
+        (
+            jax.ShapeDtypeStruct((2 if two else 3, half_cols, wide), BF16),
+            jax.ShapeDtypeStruct((2, half_cols, wide), F32),
+            jax.ShapeDtypeStruct((half_cols, wide), BF16),
+        ),
+        [pltpu.VMEM((5, cols + 8, channels), F32)],
         flops // 3,
         (above_1, below_1, conv_fine, fine_sums, conv_down),
     )
     field = call(
         reduce_kernel,
-        shape,
-        [pltpu.VMEM((rows + 1, cols + 8, channels), F32)],
+        jax.ShapeDtypeStruct((1, half_rows - 1, half_cols, wide), BF16),
+        [pltpu.VMEM((rows - 3, cols + 8, channels), F32)],
         flops // 3,
-        (fine_sums, halo_1, conv_down),
+        (fine_sums, first, conv_down),
     )
     field_2 = moved(field, 2, 0)
-    if sides == 1:
-        rim = swapped(ends, 0)
+    if two:
+        from_above = from_below = swapped(sent, 0)
     else:
-        rim = jnp.concatenate([moved(ends[1:], 0, 1), moved(ends[:1], 0, -1)], axis=0)
+        from_above, from_below = moved(sent[2:], 0, 1), moved(sent[:2], 0, -1)
+    rim = call(
+        edge_rows_kernel,
+        jax.ShapeDtypeStruct((1, 2 if two else 3, half_cols, wide), BF16),
+        [],
+        0,
+        (from_above, from_below, kept),
+    )
     rim_2 = moved(rim, 2, 0)
     sums = jax.ShapeDtypeStruct((half_rows * half_cols, wide), F32)
     flops = 2 * half_rows * half_cols * 9 * wide * wide

time: 30.1 us -> 27.2 us (0.904)
  waiting for transfers between devices: 8.21 us -> 6.79 us
  starting transfers between devices: 14.1 us -> 13.2 us
  Pallas kernels: 6.97 us -> 6.27 us
    ppermute x3, waiting for transfers between devices: 2.94 us -> 0.55 us  [swapped(): return lax.ppermute(value, ('tm', 'rows'), pairs)]
    ppermute x2, starting transfers between devices: 6.22 us -> 4.71 us  [moved(): return lax.ppermute(value, ('tm', 'rows'), pairs)]
    pallas_call x10 -> x11, Pallas kernels: 6.97 us -> 6.27 us  [call(): pl.pallas_call(kernel, out_shape=out_shape, in_specs=[pl.BlockSpec(memory...]
    ppermute x1, waiting for transfers between devices: 3.78 us -> 4.45 us  [ring(): return lax.ppermute(value, 'tm', [(t, (t + steps) % tm) for t in range(tm)])]
    ppermute x3, starting transfers between devices: 6.77 us -> 7.34 us  [swapped(): return lax.ppermute(value, ('tm', 'rows'), pairs)]
  transfers between devices with their start and end apart: 10 -> 10, of which waited for: 5 -> 4; matrix products, arithmetic and copies ran while one was open for 0% -> 0% of each run, Pallas kernels for 15% -> 16%
where the time goes in v4:
time: 27.2 us; the launch traced here: 27 us
  starting transfers between devices  13.2 us (49%)
  waiting for transfers between devices  6.79 us (25%)
  Pallas kernels  6.27 us (23%)
  local copies, waits for them, and re-layouts  0.56 us (2%)
    ppermute x3, starting transfers between devices, swapped(): return lax.ppermute(value, ('tm', 'rows'), pairs)  7.34 us
    pallas_call x11, Pallas kernels, call(): pl.pallas_call(kernel, out_shape=out_shape, in_specs=[pl.BlockSpec(memory...  6.27 us
    ppermute x2, starting transfers between devices, moved(): return lax.ppermute(value, ('tm', 'rows'), pairs)  4.71 us
    ppermute x1, waiting for transfers between devices, ring(): return lax.ppermute(value, 'tm', [(t, (t + steps) % tm) for t in range(tm)])  4.45 us
    ppermute x2, waiting for transfers between devices, moved(): return lax.ppermute(value, ('tm', 'rows'), pairs)  1.36 us
    ppermute x4, starting transfers between devices, paired(): lax.ppermute(value, 'tm', [(t, t ^ 1) for t in range(lax.axis_size('tm'))])  0.65 us
    unnamed x8, local copies, waits for them, and re-layouts  0.56 us
    ppermute x3, waiting for transfers between devices, swapped(): return lax.ppermute(value, ('tm', 'rows'), pairs)  0.55 us
  transfers between devices with their start and end apart: 10, of which 4 were waited for; matrix products, arithmetic and copies ran while one was open for 0% of the time, Pallas kernels for 16%

profile of v4, /device:TPU:0, one launch (start us, length us, event | category | flops | bytes accessed | tf_op | source)
XLA Modules:
  0.0 27.0 jit_solution(12511641986561675840)
XLA Ops:
  0.0 0.0 copy-start.3
  0.0 0.0 copy-start.2
  0.0 0.5 %collective-permute-start.1 = (bf16[2,8,128,128]{3,2,1,0:T(8,128)(2,1)}, bf16[2,8,128,128]{3,2,1,0:T(8,128)(2,1)S(1)}, u32[]{:S(2)}, u32[]{:S(2)}) collective-permute-start(bf16[2,8,128,128]{3,2,1,0:T(8,128)(2,1)} %frames.1), channel_id=1, source_target_pairs={{0,2},{2,4},{4,6},{6,8},{8,10},{10,12},{12,14},{14,16},{16,18},{18... | collective-permute-start | bytes 1572872 | tf_op jit(solution)/shard_map/ppermute | solution.py:28
  0.5 0.5 %copy-done.3 = bf16[2,8,128,128]{3,2,1,0:T(8,128)(2,1)S(1)} copy-done((bf16[2,8,128,128]{3,2,1,0:T(8,128)(2,1)S(1)}, bf16[2,8,128,128]{3,2,1,0:T(8,128)(2,1)}, u32[]{:S(2)}) %copy-start.3) | copy-done | bytes 524312
  1.0 3.0 %collective-permute-start.2 = (bf16[2,1,128,128]{3,2,1,0:T(8,128)(2,1)S(1)}, bf16[2,1,128,128]{3,2,1,0:T(8,128)(2,1)S(1)}, u32[]{:S(2)}, u32[]{:S(2)}) collective-permute-start(bf16[2,1,128,128]{3,2,1,0:T(8,128)(2,1)S(1)} %shard_map.47), channel_id=1, source_target_pairs={{0,1},{1,0},{2,3},{3,2},{4,5},{5,4},{6,7},{7,6},{8,9},{9,8},{10,11... | collective-permute-start | bytes 196616 | tf_op jit(solution)/shard_map/ppermute | solution.py:34
  4.0 2.4 %collective-permute-start = (bf16[2,1,128,128]{3,2,1,0:T(8,128)(2,1)S(1)}, bf16[2,1,128,128]{3,2,1,0:T(8,128)(2,1)S(1)}, u32[]{:S(2)}, u32[]{:S(2)}) collective-permute-start(bf16[2,1,128,128]{3,2,1,0:T(8,128)(2,1)S(1)} %shard_map.47), channel_id=1, source_target_pairs={{0,3},{1,2},{2,5},{3,4},{4,7},{5,6},{6,9},{7,8},{8,11},{9,10},{10,... | collective-permute-start | bytes 196616 | tf_op jit(solution)/shard_map/ppermute | solution.py:34
  6.4 0.0 copy-done.2
  6.4 1.4 %shard_map.48.own = f32[1024,256]{1,0:T(8,128)S(1)} custom-call(bf16[2,8,128,128]{3,2,1,0:T(8,128)(2,1)S(1)} %copy-done.3, bf16[3,3,384,128]{3,2,1,0:T(8,128)(2,1)S(1)} %copy-done.2), custom_call_target="tpu_custom_call" | custom-call | flops 1207959552 | bytes 1409024 | tf_op jit(solution)/shard_map/pallas_call | solution.py:303
  7.8 0.0 copy-start.1
  7.8 0.0 collective-permute-done.2.above.below
  7.9 0.3 %shard_map.49.halo = f32[2,128,256]{2,1,0:T(8,128)S(1)} custom-call(bf16[2,1,128,128]{3,2,1,0:T(8,128)(2,1)S(1)} %collective-permute-done.2.above.below, bf16[2,1,128,128]{3,2,1,0:T(8,128)(2,1)S(1)} %collective-permute-done.2.above.below, bf16[3,3,384,128]{3,2,1,0:T(8,128)(2,1)S(1)} %copy-done.2), custom_call_target="tpu_custom_call" | custom-call | flops 402653184 | bytes 1015808 | tf_op jit(solution)/shard_map/pallas_call | solution.py:303
  8.1 0.0 copy-start
  8.1 4.4 %collective-permute-done.1.frames = bf16[2,8,128,128]{3,2,1,0:T(8,128)(2,1)S(1)} collective-permute-done((bf16[2,8,128,128]{3,2,1,0:T(8,128)(2,1)}, bf16[2,8,128,128]{3,2,1,0:T(8,128)(2,1)S(1)}, u32[]{:S(2)}, u32[]{:S(2)}) %collective-permute-start.1) | collective-permute-done | bytes 524320 | tf_op jit(solution)/shard_map/ppermute | solution.py:28
  12.6 1.4 %shard_map.50.sums = f32[1024,256]{1,0:T(8,128)S(1)} custom-call(bf16[2,8,128,128]{3,2,1,0:T(8,128)(2,1)S(1)} %collective-permute-done.1.frames, bf16[3,3,384,128]{3,2,1,0:T(8,128)(2,1)S(1)} %copy-done.2, f32[1024,256]{1,0:T(8,128)S(1)} %shard_map.48.own, f32[2,128,256]{2,1,0:T(8,128)S(1)} %shard_map.49.halo), custom_call_target="tpu_custom_call" | custom-call | flops 1207959552 | bytes 2719744 | tf_op jit(solution)/shard_map/pallas_call | solution.py:303
  14.0 0.0 collective-permute-done.above.below
  14.0 0.0 copy-done.1
  14.0 0.7 %shard_map.51 = (bf16[2,64,256]{2,1,0:T(8,128)(2,1)S(1)}, f32[2,64,256]{2,1,0:T(8,128)S(1)}, bf16[64,256]{1,0:T(8,128)(2,1)S(1)}) custom-call(bf16[2,1,128,128]{3,2,1,0:T(8,128)(2,1)S(1)} %collective-permute-done.above.below, bf16[2,1,128,128]{3,2,1,0:T(8,128)(2,1)S(1)} %collective-permute-done.above.below, bf16[3,3,384,128]{3,2,1,0:T(8,128)(2,1)S(1)} %copy-done.2, ...), custom_call_target="tpu_custom_call" | custom-call | flops 402653184 | bytes 2654208 | tf_op jit(solution)/shard_map/pallas_call | solution.py:303
  14.7 2.0 %collective-permute-start.4 = (bf16[2,64,256]{2,1,0:T(8,128)(2,1)S(1)}, bf16[2,64,256]{2,1,0:T(8,128)(2,1)S(1)}, u32[]{:S(2)}, u32[]{:S(2)}) collective-permute-start(bf16[2,64,256]{2,1,0:T(8,128)(2,1)S(1)} %get-tuple-element.20), channel_id=1, source_target_pairs={{0,1},{1,0},{2,3},{3,2},{4,5},{5,4},{6,7},{7,6},{8,9},{9,8},{10,11... | collective-permute-start | bytes 196616 | tf_op jit(solution)/shard_map/ppermute | solution.py:34
  16.7 0.4 %shard_map.52.main = bf16[1,3,64,256]{3,2,1,0:T(8,128)(2,1)S(1)} custom-call(f32[1024,256]{1,0:T(8,128)S(1)} %shard_map.50.sums, bf16[64,256]{1,0:T(8,128)(2,1)S(1)} %get-tuple-element.19.first, bf16[3,384,256]{2,1,0:T(8,128)(2,1)S(1)} %copy-done.1), custom_call_target="tpu_custom_call" | custom-call | flops 402653184 | bytes 1671168 | tf_op jit(solution)/shard_map/pallas_call | solution.py:303
  17.1 0.1 collective-permute-start.6
  17.2 1.3 %collective-permute-start.3 = (bf16[1,3,64,256]{3,2,1,0:T(8,128)(2,1)S(1)}, bf16[1,3,64,256]{3,2,1,0:T(8,128)(2,1)S(1)}, u32[]{:S(2)}, u32[]{:S(2)}) collective-permute-start(bf16[1,3,64,256]{3,2,1,0:T(8,128)(2,1)S(1)} %shard_map.52.main), channel_id=1, source_target_pairs={{0,4},{1,5},{2,6},{3,7},{4,8},{5,9},{6,10},{7,11},{8,12},{9,13},{1... | collective-permute-start | bytes 294920 | tf_op jit(solution)/shard_map/ppermute | solution.py:23
  18.5 0.5 %collective-permute-done.4.above.below = bf16[2,64,256]{2,1,0:T(8,128)(2,1)S(1)} collective-permute-done((bf16[2,64,256]{2,1,0:T(8,128)(2,1)S(1)}, bf16[2,64,256]{2,1,0:T(8,128)(2,1)S(1)}, u32[]{:S(2)}, u32[]{:S(2)}) %collective-permute-start.4) | collective-permute-done | bytes 65568 | tf_op jit(solution)/shard_map/ppermute | solution.py:34
  19.0 0.1 collective-permute-start.7
  19.1 3.4 %collective-permute-start.5 = (bf16[1,2,64,256]{3,2,1,0:T(8,128)(2,1)S(1)}, bf16[1,2,64,256]{3,2,1,0:T(8,128)(2,1)S(1)}, u32[]{:S(2)}, u32[]{:S(2)}) collective-permute-start(bf16[1,2,64,256]{3,2,1,0:T(8,128)(2,1)S(1)} %shard_map.53.edge), channel_id=1, source_target_pairs={{0,4},{1,5},{2,6},{3,7},{4,8},{5,9},{6,10},{7,11},{8,12},{9,13},{1... | collective-permute-start | bytes 196616 | tf_op jit(solution)/shard_map/ppermute | solution.py:23
  22.5 0.0 copy-done
  22.5 0.5 %shard_map.54.total = f32[256,256]{1,0:T(8,128)S(1)} custom-call(bf16[1,3,64,256]{3,2,1,0:T(8,128)(2,1)S(1)} %shard_map.52.main, bf16[1,2,64,256]{3,2,1,0:T(8,128)(2,1)S(1)} %shard_map.53.edge, bf16[3,3,768,256]{3,2,1,0:T(8,128)(2,1)S(1)} %copy-done), custom_call_target="tpu_custom_call" | custom-call | flops 301989888 | bytes 3702784 | tf_op jit(solution)/shard_map/pallas_call | solution.py:303
  23.0 0.0 collective-permute-done.6.direct
  23.0 0.0 collective-permute-done.3.main
  23.0 0.0 collective-permute-done.7.direct_rim
  23.1 1.4 %collective-permute-done.5.edge = bf16[1,2,64,256]{3,2,1,0:T(8,128)(2,1)S(1)} collective-permute-done((bf16[1,2,64,256]{3,2,1,0:T(8,128)(2,1)S(1)}, bf16[1,2,64,256]{3,2,1,0:T(8,128)(2,1)S(1)}, u32[]{:S(2)}, u32[]{:S(2)}) %collective-permute-start.5) | collective-permute-done | bytes 65568 | tf_op jit(solution)/shard_map/ppermute | solution.py:23
  24.4 0.0 collective-permute-start.8
  24.4 0.5 %collective-permute-start.9 = (bf16[1,2,64,256]{3,2,1,0:T(8,128)(2,1)S(1)}, bf16[1,2,64,256]{3,2,1,0:T(8,128)(2,1)S(1)}, u32[]{:S(2)}, u32[]{:S(2)}) collective-permute-start(bf16[1,2,64,256]{3,2,1,0:T(8,128)(2,1)S(1)} %collective-permute-done.5.edge), channel_id=1, source_target_pairs={{0,2},{2,0},{4,6},{6,4},{8,10},{10,8},{12,14},{14,12},{16,18},{18,... | collective-permute-start | bytes 196616 | tf_op jit(solution)/shard_map/ppermute | solution.py:38
  24.9 0.5 %shard_map.55.total = f32[256,256]{1,0:T(8,128)S(1)} custom-call(bf16[1,3,64,256]{3,2,1,0:T(8,128)(2,1)S(1)} %collective-permute-done.3.main, bf16[1,2,64,256]{3,2,1,0:T(8,128)(2,1)S(1)} %collective-permute-done.5.edge, bf16[3,3,768,256]{3,2,1,0:T(8,128)(2,1)S(1)} %copy-done, f32[256,256]{1,0:T(8,128)S(1)} %shard_map.54.total), custom_call_target="tpu_custom_call" | custom-call | flops 301989888 | bytes 3964928 | tf_op jit(solution)/shard_map/pallas_call | solution.py:303
  25.4 0.4 %collective-permute-done.9.relayed_rim = bf16[1,2,64,256]{3,2,1,0:T(8,128)(2,1)S(1)} collective-permute-done((bf16[1,2,64,256]{3,2,1,0:T(8,128)(2,1)S(1)}, bf16[1,2,64,256]{3,2,1,0:T(8,128)(2,1)S(1)}, u32[]{:S(2)}, u32[]{:S(2)}) %collective-permute-start.9) | collective-permute-done | bytes 65568 | tf_op jit(solution)/shard_map/ppermute | solution.py:38
  25.8 0.0 collective-permute-done.8.relayed
  25.8 1.2 %shard_map.56 = bf16[1,4,64,256]{3,2,1,0:T(8,128)(2,1)} custom-call(bf16[1,3,64,256]{3,2,1,0:T(8,128)(2,1)S(1)} %collective-permute-done.6.direct, bf16[1,2,64,256]{3,2,1,0:T(8,128)(2,1)S(1)} %collective-permute-done.7.direct_rim, bf16[1,3,64,256]{3,2,1,0:T(8,128)(2,1)S(1)} %collective-permute-done.8.relayed, ...), custom_call_target="tpu_custom_call" | custom-call | flops 301989888 | bytes 4128768 | tf_op jit(solution)/shard_map/pallas_call | solution.py:303
  (3 shorter events, 0.0 us)
Async XLA Ops:
  0.0 1.0 %copy-start.3 = (bf16[2,8,128,128]{3,2,1,0:T(8,128)(2,1)S(1)}, bf16[2,8,128,128]{3,2,1,0:T(8,128)(2,1)}, u32[]{:S(2)}) copy-start(bf16[2,8,128,128]{3,2,1,0:T(8,128)(2,1)} %frames.1) | copy-start | bytes 1572868
  0.0 6.4 %copy-start.2 = (bf16[3,3,384,128]{3,2,1,0:T(8,128)(2,1)S(1)}, bf16[3,3,384,128]{3,2,1,0:T(8,128)(2,1)}, u32[]{:S(2)}) copy-start(bf16[3,3,384,128]{3,2,1,0:T(8,128)(2,1)} %weight.10) | copy-start | bytes 2654212
  0.0 12.6 %collective-permute-start.1 = (bf16[2,8,128,128]{3,2,1,0:T(8,128)(2,1)}, bf16[2,8,128,128]{3,2,1,0:T(8,128)(2,1)S(1)}, u32[]{:S(2)}, u32[]{:S(2)}) collective-permute-start(bf16[2,8,128,128]{3,2,1,0:T(8,128)(2,1)} %frames.1), channel_id=1, source_target_pairs={{0,2},{2,4},{4,6},{6,8},{8,10},{10,12},{12,14},{14,16},{16,18},{18... | collective-permute-start | bytes 1572872 | tf_op jit(solution)/shard_map/ppermute | solution.py:28
  1.0 6.8 %collective-permute-start.2 = (bf16[2,1,128,128]{3,2,1,0:T(8,128)(2,1)S(1)}, bf16[2,1,128,128]{3,2,1,0:T(8,128)(2,1)S(1)}, u32[]{:S(2)}, u32[]{:S(2)}) collective-permute-start(bf16[2,1,128,128]{3,2,1,0:T(8,128)(2,1)S(1)} %shard_map.47), channel_id=1, source_target_pairs={{0,1},{1,0},{2,3},{3,2},{4,5},{5,4},{6,7},{7,6},{8,9},{9,8},{10,11... | collective-permute-start | bytes 196616 | tf_op jit(solution)/shard_map/ppermute | solution.py:34
  4.0 10.0 %collective-permute-start = (bf16[2,1,128,128]{3,2,1,0:T(8,128)(2,1)S(1)}, bf16[2,1,128,128]{3,2,1,0:T(8,128)(2,1)S(1)}, u32[]{:S(2)}, u32[]{:S(2)}) collective-permute-start(bf16[2,1,128,128]{3,2,1,0:T(8,128)(2,1)S(1)} %shard_map.47), channel_id=1, source_target_pairs={{0,3},{1,2},{2,5},{3,4},{4,7},{5,6},{6,9},{7,8},{8,11},{9,10},{10,... | collective-permute-start | bytes 196616 | tf_op jit(solution)/shard_map/ppermute | solution.py:34
  7.8 6.2 %copy-start.1 = (bf16[3,384,256]{2,1,0:T(8,128)(2,1)S(1)}, bf16[3,384,256]{2,1,0:T(8,128)(2,1)}, u32[]{:S(2)}) copy-start(bf16[3,384,256]{2,1,0:T(8,128)(2,1)} %down.3) | copy-start | bytes 1769476
  8.1 14.4 %copy-start = (bf16[3,3,768,256]{3,2,1,0:T(8,128)(2,1)S(1)}, bf16[3,3,768,256]{3,2,1,0:T(8,128)(2,1)}, u32[]{:S(2)}) copy-start(bf16[3,3,768,256]{3,2,1,0:T(8,128)(2,1)} %weight.13) | copy-start | bytes 10616836
  14.7 4.3 %collective-permute-start.4 = (bf16[2,64,256]{2,1,0:T(8,128)(2,1)S(1)}, bf16[2,64,256]{2,1,0:T(8,128)(2,1)S(1)}, u32[]{:S(2)}, u32[]{:S(2)}) collective-permute-start(bf16[2,64,256]{2,1,0:T(8,128)(2,1)S(1)} %get-tuple-element.20), channel_id=1, source_target_pairs={{0,1},{1,0},{2,3},{3,2},{4,5},{5,4},{6,7},{7,6},{8,9},{9,8},{10,11... | collective-permute-start | bytes 196616 | tf_op jit(solution)/shard_map/ppermute | solution.py:34
  17.1 6.0 %collective-permute-start.6 = (bf16[1,3,64,256]{3,2,1,0:T(8,128)(2,1)S(1)}, bf16[1,3,64,256]{3,2,1,0:T(8,128)(2,1)S(1)}, u32[]{:S(2)}, u32[]{:S(2)}) collective-permute-start(bf16[1,3,64,256]{3,2,1,0:T(8,128)(2,1)S(1)} %shard_map.52.main), channel_id=1, source_target_pairs={{0,2},{2,0},{4,6},{6,4},{8,10},{10,8},{12,14},{14,12},{16,18},{18,... | collective-permute-start | bytes 294920 | tf_op jit(solution)/shard_map/ppermute | solution.py:38
  17.2 5.9 %collective-permute-start.3 = (bf16[1,3,64,256]{3,2,1,0:T(8,128)(2,1)S(1)}, bf16[1,3,64,256]{3,2,1,0:T(8,128)(2,1)S(1)}, u32[]{:S(2)}, u32[]{:S(2)}) collective-permute-start(bf16[1,3,64,256]{3,2,1,0:T(8,128)(2,1)S(1)} %shard_map.52.main), channel_id=1, source_target_pairs={{0,4},{1,5},{2,6},{3,7},{4,8},{5,9},{6,10},{7,11},{8,12},{9,13},{1... | collective-permute-start | bytes 294920 | tf_op jit(solution)/shard_map/ppermute | solution.py:23
  19.0 4.0 %collective-permute-start.7 = (bf16[1,2,64,256]{3,2,1,0:T(8,128)(2,1)S(1)}, bf16[1,2,64,256]{3,2,1,0:T(8,128)(2,1)S(1)}, u32[]{:S(2)}, u32[]{:S(2)}) collective-permute-start(bf16[1,2,64,256]{3,2,1,0:T(8,128)(2,1)S(1)} %shard_map.53.edge), channel_id=1, source_target_pairs={{0,2},{2,0},{4,6},{6,4},{8,10},{10,8},{12,14},{14,12},{16,18},{18,... | collective-permute-start | bytes 196616 | tf_op jit(solution)/shard_map/ppermute | solution.py:38
  19.1 5.3 %collective-permute-start.5 = (bf16[1,2,64,256]{3,2,1,0:T(8,128)(2,1)S(1)}, bf16[1,2,64,256]{3,2,1,0:T(8,128)(2,1)S(1)}, u32[]{:S(2)}, u32[]{:S(2)}) collective-permute-start(bf16[1,2,64,256]{3,2,1,0:T(8,128)(2,1)S(1)} %shard_map.53.edge), channel_id=1, source_target_pairs={{0,4},{1,5},{2,6},{3,7},{4,8},{5,9},{6,10},{7,11},{8,12},{9,13},{1... | collective-permute-start | bytes 196616 | tf_op jit(solution)/shard_map/ppermute | solution.py:23
  24.4 1.4 %collective-permute-start.8 = (bf16[1,3,64,256]{3,2,1,0:T(8,128)(2,1)S(1)}, bf16[1,3,64,256]{3,2,1,0:T(8,128)(2,1)S(1)}, u32[]{:S(2)}, u32[]{:S(2)}) collective-permute-start(bf16[1,3,64,256]{3,2,1,0:T(8,128)(2,1)S(1)} %collective-permute-done.3.main), channel_id=1, source_target_pairs={{0,2},{2,0},{4,6},{6,4},{8,10},{10,8},{12,14},{14,12},{16,18},{18,... | collective-permute-start | bytes 294920 | tf_op jit(solution)/shard_map/ppermute | solution.py:38
  24.4 1.4 %collective-permute-start.9 = (bf16[1,2,64,256]{3,2,1,0:T(8,128)(2,1)S(1)}, bf16[1,2,64,256]{3,2,1,0:T(8,128)(2,1)S(1)}, u32[]{:S(2)}, u32[]{:S(2)}) collective-permute-start(bf16[1,2,64,256]{3,2,1,0:T(8,128)(2,1)S(1)} %collective-permute-done.5.edge), channel_id=1, source_target_pairs={{0,2},{2,0},{4,6},{6,4},{8,10},{10,8},{12,14},{14,12},{16,18},{18,... | collective-permute-start | bytes 196616 | tf_op jit(solution)/shard_map/ppermute | solution.py:38

commit v5 on v4

--- a/solution.py
+++ b/solution.py
@@ -205,106 +205,121 @@
         pooled[i, :cols] = line
 
 
-def ends_kernel(above, below, weight, sums, down, sent, kept, first, pooled):
+def reduce_kernel(above, below, weight, sums, down, out, pooled):
     cols = above.shape[2]
     rows = sums.shape[0] // cols
-    half_cols = cols // 2
+    half_rows, half_cols = rows // 2, cols // 2
     top, bottom = halo_sums(above, below, weight, 0, rows)
     lines = []
-    for r in (0, 1, 2, rows - 2, rows - 1):
+    for r in range(rows):
         line = sums[r * cols : (r + 1) * cols]
         if r == 0:
             line = line + top
         if r == rows - 1:
             line = line + bottom
         lines.append(pool(line))
-    put_pooled(pooled, lines)
+    put_pooled(pooled, [*lines, jnp.zeros_like(lines[0])])
     dot = functools.partial(jnp.dot, preferred_element_type=F32)
-    flat = down[...].reshape(-1, down.shape[-1])
-    third = down.shape[1]
-    head = dot(down_taps(pooled, 0, 3, half_cols), flat).astype(BF16)
-    added = dot(down_taps(pooled, 0, 1, half_cols), down[2])
-    tail = dot(down_taps(pooled, 3, 2, half_cols), flat[: 2 * third])
-    first[...] = head
-    kept[0], kept[1] = added, tail
-    if sent.shape[0] == 2:
-        sent[0] = jnp.where(has_above(), head, tail.astype(BF16))
-        sent[1] = added.astype(BF16)
+    left = [down_taps(pooled, 2 * p, 3, half_cols) for p in range(half_rows)]
+    own = dot(jnp.concatenate(left, axis=0), down[...].reshape(-1, down.shape[-1]))
+    out[0, :half_rows] = own.astype(BF16).reshape(half_rows, half_cols, -1)
+    out[0, half_rows] = dot(down_taps(pooled, 0, 1, half_cols), down[2]).astype(BF16)
+
+
+def column_taps(flat, cols):
+    left, right = shifted_columns(flat, cols)
+    return jnp.concatenate([left, flat, right], axis=1)
+
+
+def coarse_sums(field, weight, a, sides):
+    _, count, cols, channels = field.shape
+    rows = count - 1
+    taps = column_taps(field.reshape(count * cols, channels), cols)
+    body, more = taps[: rows * cols], taps[rows * cols :]
+    zero = jnp.zeros_like(more)
+    tall = jnp.concatenate([jnp.where(has_above(), more, zero), body, zero], axis=0)
+    dot = functools.partial(jnp.dot, preferred_element_type=F32)
+    total = sum(dot(tall[b * cols : (b + rows) * cols], weight[a, b]) for b in range(3))
+    head, tail = body[:cols], body[(rows - 1) * cols :]
+    if sides == 1:
+        up = has_above()
+        first = jnp.concatenate([jnp.where(up, more, tail), jnp.where(up, head, zero)], axis=0)
+        ends = [dot(first, weight[a, 2 * lax.axis_index("rows")])]
+        second = [dot(jnp.where(up, more, zero), weight[a, 1])]
     else:
-        sent[0], sent[1], sent[2] = head, added.astype(BF16), tail.astype(BF16)
-
-
-def reduce_kernel(sums, first, down, out, pooled):
-    _, count, half_cols, _ = out.shape
-    cols = 2 * half_cols
-    put_pooled(pooled, [pool(sums[r * cols : (r + 1) * cols]) for r in range(2, 2 * count + 1)])
-    left = [down_taps(pooled, 2 * p, 3, half_cols) for p in range(count - 1)]
-    flat = down[...].reshape(-1, down.shape[-1])
-    rest = jnp.dot(jnp.concatenate(left, axis=0), flat, preferred_element_type=F32)
-    out[0, 0] = first[...]
-    out[0, 1:] = rest.astype(BF16).reshape(count - 1, half_cols, -1)
-
-
-def edge_rows_kernel(above, below, kept, out):
-    added, tail = kept[0], kept[1]
-    more = jnp.where(has_below(), below[1].astype(F32), 0.0)
-    out[0, 0] = (tail + more).astype(BF16)
-    upper = (above[0].astype(F32) + added).astype(BF16)
-    if out.shape[1] == 2:
-        out[0, 1] = jnp.where(has_above(), upper, below[0])
-    else:
-        out[0, 1], out[0, 2] = upper, below[0]
-
-
-def coarse_sum(main, edge, weight, a):
-    _, count, cols, channels = main.shape
-    rows = count + 1
-    zero = jnp.zeros((cols, channels), BF16)
-    flat = jnp.concatenate(
-        [
-            jnp.where(has_above(), edge[0, 1], zero),
-            main[0].reshape(count * cols, channels),
-            edge[0, 0],
-            jnp.where(has_below(), edge[0, edge.shape[1] - 1], zero),
-        ],
-        axis=0,
-    )
-    left, right = shifted_columns(flat, cols)
-    taps = jnp.concatenate([left, flat, right], axis=1)
-    total = None
-    for b in range(3):
-        part = jnp.dot(
-            taps[b * cols : (b + rows) * cols], weight[a, b], preferred_element_type=F32
+        first = jnp.concatenate([tail, zero], axis=0), jnp.concatenate([more, head], axis=0)
+        ends = [dot(first[0], weight[a, 0]), dot(first[1], weight[a, 2])]
+        second = [jnp.zeros((cols, weight.shape[-1]), F32), dot(more, weight[a, 1])]
+    ends = [
+        jnp.concatenate([end[:cols], end[cols:] + add], axis=0) for end, add in zip(ends, second)
+    ]
+    return total, ends
+
+
+def coarse_first_kernel(field, weight, body, ends):
+    total, parts = coarse_sums(field[...], weight, 2, ends.shape[0])
+    body[...] = total
+    for side, part in enumerate(parts):
+        ends[side] = part
+
+
+def coarse_next_kernel(field, weight, body_in, ends_in, body, ends):
+    cells = field[...]
+    cells = jnp.where(has_earlier(2), cells, jnp.zeros_like(cells))
+    total, parts = coarse_sums(cells, weight, 0, ends.shape[0])
+    body[...] = body_in[...] + total
+    for side, part in enumerate(parts):
+        ends[side] = ends_in[side] + part
+
+
+def middle(direct, relayed):
+    cells = jnp.where(lax.axis_index("tm") % 2 == 1, direct[...], relayed[...])
+    return jnp.where(has_earlier(1), cells, jnp.zeros_like(cells))
+
+
+def coarse_ends_kernel(direct, relayed, weight, ends, out):
+    _, parts = coarse_sums(middle(direct, relayed), weight, 1, ends.shape[0])
+    for side, part in enumerate(parts):
+        out[side] = (ends[side] + part).astype(BF16)
+
+
+def end_starts(rows, sides):
+    return [(rows - 2) * (1 - lax.axis_index("rows"))] if sides == 1 else [0, rows - 2]
+
+
+def coarse_body_kernel(direct, relayed, weight, body, out, ends, sums):
+    _, rows, cols, _ = out.shape
+    total, _ = coarse_sums(middle(direct, relayed), weight, 1, ends.shape[0])
+    sums[...] = body[...] + total
+    out[...] = silu(sums[...]).astype(BF16).reshape(out.shape)
+    for side, start in enumerate(end_starts(rows, ends.shape[0])):
+        ends[side] = sums[pl.ds(pl.multiple_of(start * cols, cols), 2 * cols), :]
+
+
+def finish_kernel(ends, added, _, out, lines, sem):
+    rows = out.shape[1]
+    copies = []
+    for side, start in enumerate(end_starts(rows, ends.shape[0])):
+        total = ends[side] + added[side].astype(F32)
+        lines[side] = silu(total).astype(BF16).reshape(lines.shape[1:])
+        copies.append(
+            pltpu.make_async_copy(lines.at[side], out.at[0, pl.ds(start, 2)], sem.at[side])
         )
-        total = part if total is None else total + part
-    return total
-
-
-def coarse_first_kernel(main, edge, weight, out):
-    out[...] = coarse_sum(main[...], edge[...], weight, 2)
-
-
-def coarse_next_kernel(main, edge, weight, total, out):
-    part = coarse_sum(main[...], edge[...], weight, 0)
-    out[...] = total[...] + jnp.where(has_earlier(2), part, 0.0)
-
-
-def coarse_last_kernel(direct, direct_rim, relayed, relayed_rim, weight, total, out):
-    odd = lax.axis_index("tm") % 2 == 1
-    field = jnp.where(odd, direct[...], relayed[...])
-    rim = jnp.where(odd, direct_rim[...], relayed_rim[...])
-    part = coarse_sum(field, rim, weight, 1)
-    total = total[...] + jnp.where(has_earlier(1), part, 0.0)
-    out[...] = silu(total).astype(BF16).reshape(out.shape)
-
-
-def call(kernel, out_shape, scratch, flops, args):
+        copies[-1].start()
+    for copy in copies:
+        copy.wait()
+
+
+def call(kernel, out_shape, scratch, flops, args, in_place=False):
     size = sum(a.size * a.dtype.itemsize for a in args)
+    vmem = pl.BlockSpec(memory_space=pltpu.VMEM)
+    last = pl.BlockSpec(memory_space=pl.ANY) if in_place else vmem
     return pl.pallas_call(
         kernel,
         out_shape=out_shape,
-        in_specs=[pl.BlockSpec(memory_space=pltpu.VMEM)] * len(args),
-        out_specs=jax.tree.map(lambda _: pl.BlockSpec(memory_space=pltpu.VMEM), out_shape),
+        in_specs=[vmem] * (len(args) - 1) + [last] if args else [],
+        out_specs=last if in_place else jax.tree.map(lambda _: vmem, out_shape),
+        input_output_aliases={len(args) - 1: 0} if in_place else {},
         scratch_shapes=scratch,
         cost_estimate=pl.CostEstimate(flops=flops, bytes_accessed=size, transcendentals=0),
         compiler_params=pltpu.CompilerParams(vmem_limit_bytes=20 * 1024 * 1024),
@@ -332,60 +347,53 @@
     )
     half_rows, half_cols = rows // 2, cols // 2
     shape = jax.ShapeDtypeStruct((1, half_rows, half_cols, wide), BF16)
-    two = strips == 2
     fine_sums = call(fine_rest_kernel, pair, [], flops, (earlier, conv_fine, own, halo))
     above_1, below_1, fine_sums = lax.optimization_barrier((above_1, below_1, fine_sums))
-    sent, kept, first = call(
-        ends_kernel,
-        (
-            jax.ShapeDtypeStruct((2 if two else 3, half_cols, wide), BF16),
-            jax.ShapeDtypeStruct((2, half_cols, wide), F32),
-            jax.ShapeDtypeStruct((half_cols, wide), BF16),
-        ),
-        [pltpu.VMEM((5, cols + 8, channels), F32)],
+    field = call(
+        reduce_kernel,
+        jax.ShapeDtypeStruct((1, half_rows + 1, half_cols, wide), BF16),
+        [pltpu.VMEM((rows + 1, cols + 8, channels), F32)],
         flops // 3,
         (above_1, below_1, conv_fine, fine_sums, conv_down),
     )
-    field = call(
-        reduce_kernel,
-        jax.ShapeDtypeStruct((1, half_rows - 1, half_cols, wide), BF16),
-        [pltpu.VMEM((rows - 3, cols + 8, channels), F32)],
-        flops // 3,
-        (fine_sums, first, conv_down),
-    )
+    sides = 1 if strips == 2 else 2
+    sums = jax.ShapeDtypeStruct((half_rows * half_cols, wide), F32)
+    pairs = jax.ShapeDtypeStruct((sides, 2 * half_cols, wide), F32)
+    flops = 2 * half_rows * half_cols * 9 * wide * wide
     field_2 = moved(field, 2, 0)
-    if two:
-        from_above = from_below = swapped(sent, 0)
-    else:
-        from_above, from_below = moved(sent[2:], 0, 1), moved(sent[:2], 0, -1)
-    rim = call(
-        edge_rows_kernel,
-        jax.ShapeDtypeStruct((1, 2 if two else 3, half_cols, wide), BF16),
-        [],
-        0,
-        (from_above, from_below, kept),
-    )
-    rim_2 = moved(rim, 2, 0)
-    sums = jax.ShapeDtypeStruct((half_rows * half_cols, wide), F32)
-    flops = 2 * half_rows * half_cols * 9 * wide * wide
-    total = call(coarse_first_kernel, sums, [], flops, (field, rim, conv_coarse))
     near = paired if times % 2 == 0 else functools.partial(ring, steps=1)
     direct = near(field)
-    direct_rim = near(rim)
-    field_2, rim_2, total, direct, direct_rim = lax.optimization_barrier(
-        (field_2, rim_2, total, direct, direct_rim)
-    )
-    if times % 2 == 0:
-        relayed, relayed_rim = paired(field_2), paired(rim_2)
+    body, ends = call(coarse_first_kernel, (sums, pairs), [], flops, (field, conv_coarse))
+    field_2, body, ends, direct = lax.optimization_barrier((field_2, body, ends, direct))
+    relayed = paired(field_2) if times % 2 == 0 else direct
+    body, ends = call(
+        coarse_next_kernel, (sums, pairs), [], flops, (field_2, conv_coarse, body, ends)
+    )
+    sent = call(
+        coarse_ends_kernel,
+        jax.ShapeDtypeStruct(pairs.shape, BF16),
+        [],
+        flops // 4,
+        (direct, relayed, conv_coarse, ends),
+    )
+    if sides == 1:
+        added = swapped(sent, 0)
     else:
-        relayed, relayed_rim = direct, direct_rim
-    total = call(coarse_next_kernel, sums, [], flops, (field_2, rim_2, conv_coarse, total))
+        added = jnp.concatenate([moved(sent[:1], 0, 1), moved(sent[1:], 0, -1)], axis=0)
+    out, end_sums = call(
+        coarse_body_kernel,
+        (shape, pairs),
+        [pltpu.VMEM(sums.shape, F32)],
+        flops,
+        (direct, relayed, conv_coarse, body),
+    )
     return call(
-        coarse_last_kernel,
+        finish_kernel,
         shape,
-        [],
-        flops,
-        (direct, direct_rim, relayed, relayed_rim, conv_coarse, total),
+        [pltpu.VMEM((sides, 2, half_cols, wide), BF16), pltpu.SemaphoreType.DMA((sides,))],
+        flops // 16,
+        (end_sums, added, out),
+        in_place=True,
     )
 
 

time: 27.2 us -> 28.6 us (1.051)
  the two profiles are of different devices: /device:TPU:0 before, /device:TPU:16 now
where the time goes in v5:
time: 28.6 us; the launch traced here: 28.4 us
  waiting for transfers between devices  12.1 us (42%)
  starting transfers between devices  7.83 us (27%)
  Pallas kernels  7.26 us (25%)
  local copies, waits for them, and re-layouts  1.04 us (4%)
    pallas_call x11, Pallas kernels, call(): pl.pallas_call(kernel, out_shape=out_shape, in_specs=[vmem] * (len(args)...  7.26 us
    ppermute x1, waiting for transfers between devices, moved(): return lax.ppermute(value, ('tm', 'rows'), pairs)  6.26 us
    ppermute x3, starting transfers between devices, swapped(): return lax.ppermute(value, ('tm', 'rows'), pairs)  5.26 us
    ppermute x1, waiting for transfers between devices, ring(): return lax.ppermute(value, 'tm', [(t, (t + steps) % tm) for t in range(tm)])  3.05 us
    ppermute x1, starting transfers between devices, moved(): return lax.ppermute(value, ('tm', 'rows'), pairs)  2.5 us
    ppermute x3, waiting for transfers between devices, swapped(): return lax.ppermute(value, ('tm', 'rows'), pairs)  2.01 us
    unnamed x8, local copies, waits for them, and re-layouts  1.04 us
    ppermute x2, waiting for transfers between devices, paired(): lax.ppermute(value, 'tm', [(t, t ^ 1) for t in range(lax.axis_size('tm'))])  0.8 us
  transfers between devices with their start and end apart: 7, of which 5 were waited for; matrix products, arithmetic and copies ran while one was open for 0% of the time, Pallas kernels for 19%

profile of v5, /device:TPU:16, one launch (start us, length us, event | category | flops | bytes accessed | tf_op | source)
XLA Modules:
  0.0 28.4 jit_solution(14179025878508503060)
XLA Ops:
  0.0 0.0 copy-start.3
  0.0 0.0 copy-start.1
  0.0 0.0 collective-permute-start.1
  0.0 1.0 %copy-done.3 = bf16[2,8,128,128]{3,2,1,0:T(8,128)(2,1)S(1)} copy-done((bf16[2,8,128,128]{3,2,1,0:T(8,128)(2,1)S(1)}, bf16[2,8,128,128]{3,2,1,0:T(8,128)(2,1)}, u32[]{:S(2)}) %copy-start.3) | copy-done | bytes 524312
  1.0 1.5 %collective-permute-start.2 = (bf16[2,1,128,128]{3,2,1,0:T(8,128)(2,1)S(1)}, bf16[2,1,128,128]{3,2,1,0:T(8,128)(2,1)S(1)}, u32[]{:S(2)}, u32[]{:S(2)}) collective-permute-start(bf16[2,1,128,128]{3,2,1,0:T(8,128)(2,1)S(1)} %shard_map.47), channel_id=1, source_target_pairs={{0,1},{1,0},{2,3},{3,2},{4,5},{5,4},{6,7},{7,6},{8,9},{9,8},{10,11... | collective-permute-start | bytes 196616 | tf_op jit(solution)/shard_map/ppermute | solution.py:34
  2.6 2.4 %collective-permute-start = (bf16[2,1,128,128]{3,2,1,0:T(8,128)(2,1)S(1)}, bf16[2,1,128,128]{3,2,1,0:T(8,128)(2,1)S(1)}, u32[]{:S(2)}, u32[]{:S(2)}) collective-permute-start(bf16[2,1,128,128]{3,2,1,0:T(8,128)(2,1)S(1)} %shard_map.47), channel_id=1, source_target_pairs={{0,3},{1,2},{2,5},{3,4},{4,7},{5,6},{6,9},{7,8},{8,11},{9,10},{10,... | collective-permute-start | bytes 196616 | tf_op jit(solution)/shard_map/ppermute | solution.py:34
  4.9 0.0 copy-done.1
  5.0 1.4 %shard_map.48.own = f32[1024,256]{1,0:T(8,128)S(1)} custom-call(bf16[2,8,128,128]{3,2,1,0:T(8,128)(2,1)S(1)} %copy-done.3, bf16[3,3,384,128]{3,2,1,0:T(8,128)(2,1)S(1)} %copy-done.1), custom_call_target="tpu_custom_call" | custom-call | flops 1207959552 | bytes 1409024 | tf_op jit(solution)/shard_map/pallas_call | solution.py:317
  6.4 0.0 copy-start.2
  6.4 0.0 collective-permute-done.2.above.below
  6.4 0.3 shard_map.49.halo
  6.7 0.0 copy-start
  6.7 3.1 %collective-permute-done.1.frames = bf16[2,8,128,128]{3,2,1,0:T(8,128)(2,1)S(1)} collective-permute-done((bf16[2,8,128,128]{3,2,1,0:T(8,128)(2,1)}, bf16[2,8,128,128]{3,2,1,0:T(8,128)(2,1)S(1)}, u32[]{:S(2)}, u32[]{:S(2)}) %collective-permute-start.1) | collective-permute-done | bytes 524320 | tf_op jit(solution)/shard_map/ppermute | solution.py:28
  9.7 1.4 %shard_map.50.sums = f32[1024,256]{1,0:T(8,128)S(1)} custom-call(bf16[2,8,128,128]{3,2,1,0:T(8,128)(2,1)S(1)} %collective-permute-done.1.frames, bf16[3,3,384,128]{3,2,1,0:T(8,128)(2,1)S(1)} %copy-done.1, f32[1024,256]{1,0:T(8,128)S(1)} %shard_map.48.own, f32[2,128,256]{2,1,0:T(8,128)S(1)} %shard_map.49.halo), custom_call_target="tpu_custom_call" | custom-call | flops 1207959552 | bytes 2719744 | tf_op jit(solution)/shard_map/pallas_call | solution.py:317
  11.1 0.2 collective-permute-done.above.below
  11.4 0.0 copy-done.2
  11.4 0.9 %shard_map.51.field = bf16[1,5,64,256]{3,2,1,0:T(8,128)(2,1)S(1)} custom-call(bf16[2,1,128,128]{3,2,1,0:T(8,128)(2,1)S(1)} %collective-permute-done.above.below, bf16[2,1,128,128]{3,2,1,0:T(8,128)(2,1)S(1)} %collective-permute-done.above.below, bf16[3,3,384,128]{3,2,1,0:T(8,128)(2,1)S(1)} %copy-done.1, f32[1024,256]{1,0:T(8,128)S(1)} %shard_map.50.sums, ...), custom_call_target="tpu_custom_call" | custom-call | flops 402653184 | bytes 2654208 | tf_op jit(solution)/shard_map/pallas_call | solution.py:317
  12.2 0.1 collective-permute-start.4
  12.3 2.5 %collective-permute-start.3 = (bf16[1,5,64,256]{3,2,1,0:T(8,128)(2,1)S(1)}, bf16[1,5,64,256]{3,2,1,0:T(8,128)(2,1)S(1)}, u32[]{:S(2)}, u32[]{:S(2)}) collective-permute-start(bf16[1,5,64,256]{3,2,1,0:T(8,128)(2,1)S(1)} %shard_map.51.field), channel_id=1, source_target_pairs={{0,4},{1,5},{2,6},{3,7},{4,8},{5,9},{6,10},{7,11},{8,12},{9,13},{1... | collective-permute-start | bytes 491528 | tf_op jit(solution)/shard_map/ppermute | solution.py:23
  14.8 0.0 copy-done
  14.8 0.6 %shard_map.52 = (f32[256,256]{1,0:T(8,128)S(1)}, f32[1,128,256]{2,1,0:T(8,128)S(1)}) custom-call(bf16[1,5,64,256]{3,2,1,0:T(8,128)(2,1)S(1)} %shard_map.51.field, bf16[3,3,768,256]{3,2,1,0:T(8,128)(2,1)S(1)} %copy-done), custom_call_target="tpu_custom_call" | custom-call | flops 301989888 | bytes 3702784 | tf_op jit(solution)/shard_map/pallas_call | solution.py:317
  15.4 0.0 collective-permute-done.4.direct
  15.4 6.3 %collective-permute-done.3.field = bf16[1,5,64,256]{3,2,1,0:T(8,128)(2,1)S(1)} collective-permute-done((bf16[1,5,64,256]{3,2,1,0:T(8,128)(2,1)S(1)}, bf16[1,5,64,256]{3,2,1,0:T(8,128)(2,1)S(1)}, u32[]{:S(2)}, u32[]{:S(2)}) %collective-permute-start.3) | collective-permute-done | bytes 163872 | tf_op jit(solution)/shard_map/ppermute | solution.py:23
  21.7 0.0 collective-permute-start.5
  21.7 0.6 %shard_map.53 = (f32[256,256]{1,0:T(8,128)S(1)}, f32[1,128,256]{2,1,0:T(8,128)S(1)}) custom-call(bf16[1,5,64,256]{3,2,1,0:T(8,128)(2,1)S(1)} %collective-permute-done.3.field, bf16[3,3,768,256]{3,2,1,0:T(8,128)(2,1)S(1)} %copy-done, f32[256,256]{1,0:T(8,128)S(1)} %get-tuple-element.25.body_in, f32[1,128,256]{2,1,0:T(8,128)S(1)} %get-tuple-element.26.ends_in), custom_call_target="tpu_custom_call" | custom-call | flops 301989888 | bytes 4096000 | tf_op jit(solution)/shard_map/pallas_call | solution.py:317
  22.3 0.8 %collective-permute-done.5.relayed = bf16[1,5,64,256]{3,2,1,0:T(8,128)(2,1)S(1)} collective-permute-done((bf16[1,5,64,256]{3,2,1,0:T(8,128)(2,1)S(1)}, bf16[1,5,64,256]{3,2,1,0:T(8,128)(2,1)S(1)}, u32[]{:S(2)}, u32[]{:S(2)}) %collective-permute-start.5) | collective-permute-done | bytes 163872 | tf_op jit(solution)/shard_map/ppermute | solution.py:38
  23.1 0.3 shard_map.55
  23.4 1.4 %collective-permute-start.6 = (bf16[1,128,256]{2,1,0:T(8,128)(2,1)S(1)}, bf16[1,128,256]{2,1,0:T(8,128)(2,1)S(1)}, u32[]{:S(2)}, u32[]{:S(2)}) collective-permute-start(bf16[1,128,256]{2,1,0:T(8,128)(2,1)S(1)} %shard_map.55), channel_id=1, source_target_pairs={{0,1},{1,0},{2,3},{3,2},{4,5},{5,4},{6,7},{7,6},{8,9},{9,8},{10,11... | collective-permute-start | bytes 196616 | tf_op jit(solution)/shard_map/ppermute | solution.py:34
  24.7 1.2 %shard_map.54 = (bf16[1,4,64,256]{3,2,1,0:T(8,128)(2,1)}, f32[1,128,256]{2,1,0:T(8,128)S(1)}) custom-call(bf16[1,5,64,256]{3,2,1,0:T(8,128)(2,1)S(1)} %collective-permute-done.4.direct, bf16[1,5,64,256]{3,2,1,0:T(8,128)(2,1)S(1)} %collective-permute-done.5.relayed, bf16[3,3,768,256]{3,2,1,0:T(8,128)(2,1)S(1)} %copy-done, f32[256,256]{1,0:T(8,128)S(1)} %get-tuple-element.27.body), custom_call_target="tpu_custom_call" | custom-call | flops 301989888 | bytes 4128768 | tf_op jit(solution)/shard_map/pallas_call | solution.py:317
  25.9 1.8 %collective-permute-done.6.added = bf16[1,128,256]{2,1,0:T(8,128)(2,1)S(1)} collective-permute-done((bf16[1,128,256]{2,1,0:T(8,128)(2,1)S(1)}, bf16[1,128,256]{2,1,0:T(8,128)(2,1)S(1)}, u32[]{:S(2)}, u32[]{:S(2)}) %collective-permute-start.6) | collective-permute-done | bytes 65568 | tf_op jit(solution)/shard_map/ppermute | solution.py:34
  27.7 0.7 %shard_map.56 = bf16[1,4,64,256]{3,2,1,0:T(8,128)(2,1)} custom-call(f32[1,128,256]{2,1,0:T(8,128)S(1)} %get-tuple-element.28.ends, bf16[1,128,256]{2,1,0:T(8,128)(2,1)S(1)} %collective-permute-done.6.added, bf16[1,4,64,256]{3,2,1,0:T(8,128)(2,1)} %get-tuple-element.30._), custom_call_target="tpu_custom_call", output_to_operand_aliasing={{}: (2, {})} | custom-call | flops 18874368 | bytes 327680 | tf_op jit(solution)/shard_map/pallas_call | solution.py:317
  (2 shorter events, 0.0 us)
Async XLA Ops:
  0.0 1.0 %copy-start.3 = (bf16[2,8,128,128]{3,2,1,0:T(8,128)(2,1)S(1)}, bf16[2,8,128,128]{3,2,1,0:T(8,128)(2,1)}, u32[]{:S(2)}) copy-start(bf16[2,8,128,128]{3,2,1,0:T(8,128)(2,1)} %frames.1) | copy-start | bytes 1572868
  0.0 4.9 %copy-start.1 = (bf16[3,3,384,128]{3,2,1,0:T(8,128)(2,1)S(1)}, bf16[3,3,384,128]{3,2,1,0:T(8,128)(2,1)}, u32[]{:S(2)}) copy-start(bf16[3,3,384,128]{3,2,1,0:T(8,128)(2,1)} %weight.11) | copy-start | bytes 2654212
  0.0 9.7 %collective-permute-start.1 = (bf16[2,8,128,128]{3,2,1,0:T(8,128)(2,1)}, bf16[2,8,128,128]{3,2,1,0:T(8,128)(2,1)S(1)}, u32[]{:S(2)}, u32[]{:S(2)}) collective-permute-start(bf16[2,8,128,128]{3,2,1,0:T(8,128)(2,1)} %frames.1), channel_id=1, source_target_pairs={{0,2},{2,4},{4,6},{6,8},{8,10},{10,12},{12,14},{14,16},{16,18},{18... | collective-permute-start | bytes 1572872 | tf_op jit(solution)/shard_map/ppermute | solution.py:28
  1.0 5.3 %collective-permute-start.2 = (bf16[2,1,128,128]{3,2,1,0:T(8,128)(2,1)S(1)}, bf16[2,1,128,128]{3,2,1,0:T(8,128)(2,1)S(1)}, u32[]{:S(2)}, u32[]{:S(2)}) collective-permute-start(bf16[2,1,128,128]{3,2,1,0:T(8,128)(2,1)S(1)} %shard_map.47), channel_id=1, source_target_pairs={{0,1},{1,0},{2,3},{3,2},{4,5},{5,4},{6,7},{7,6},{8,9},{9,8},{10,11... | collective-permute-start | bytes 196616 | tf_op jit(solution)/shard_map/ppermute | solution.py:34
  2.6 8.8 %collective-permute-start = (bf16[2,1,128,128]{3,2,1,0:T(8,128)(2,1)S(1)}, bf16[2,1,128,128]{3,2,1,0:T(8,128)(2,1)S(1)}, u32[]{:S(2)}, u32[]{:S(2)}) collective-permute-start(bf16[2,1,128,128]{3,2,1,0:T(8,128)(2,1)S(1)} %shard_map.47), channel_id=1, source_target_pairs={{0,3},{1,2},{2,5},{3,4},{4,7},{5,6},{6,9},{7,8},{8,11},{9,10},{10,... | collective-permute-start | bytes 196616 | tf_op jit(solution)/shard_map/ppermute | solution.py:34
  6.4 5.0 %copy-start.2 = (bf16[3,384,256]{2,1,0:T(8,128)(2,1)S(1)}, bf16[3,384,256]{2,1,0:T(8,128)(2,1)}, u32[]{:S(2)}) copy-start(bf16[3,384,256]{2,1,0:T(8,128)(2,1)} %down.1) | copy-start | bytes 1769476
  6.7 8.2 %copy-start = (bf16[3,3,768,256]{3,2,1,0:T(8,128)(2,1)S(1)}, bf16[3,3,768,256]{3,2,1,0:T(8,128)(2,1)}, u32[]{:S(2)}) copy-start(bf16[3,3,768,256]{3,2,1,0:T(8,128)(2,1)} %weight.15) | copy-start | bytes 10616836
  12.2 3.2 %collective-permute-start.4 = (bf16[1,5,64,256]{3,2,1,0:T(8,128)(2,1)S(1)}, bf16[1,5,64,256]{3,2,1,0:T(8,128)(2,1)S(1)}, u32[]{:S(2)}, u32[]{:S(2)}) collective-permute-start(bf16[1,5,64,256]{3,2,1,0:T(8,128)(2,1)S(1)} %shard_map.51.field), channel_id=1, source_target_pairs={{0,2},{2,0},{4,6},{6,4},{8,10},{10,8},{12,14},{14,12},{16,18},{18,... | collective-permute-start | bytes 491528 | tf_op jit(solution)/shard_map/ppermute | solution.py:38
  12.3 9.4 %collective-permute-start.3 = (bf16[1,5,64,256]{3,2,1,0:T(8,128)(2,1)S(1)}, bf16[1,5,64,256]{3,2,1,0:T(8,128)(2,1)S(1)}, u32[]{:S(2)}, u32[]{:S(2)}) collective-permute-start(bf16[1,5,64,256]{3,2,1,0:T(8,128)(2,1)S(1)} %shard_map.51.field), channel_id=1, source_target_pairs={{0,4},{1,5},{2,6},{3,7},{4,8},{5,9},{6,10},{7,11},{8,12},{9,13},{1... | collective-permute-start | bytes 491528 | tf_op jit(solution)/shard_map/ppermute | solution.py:23
  21.7 1.4 %collective-permute-start.5 = (bf16[1,5,64,256]{3,2,1,0:T(8,128)(2,1)S(1)}, bf16[1,5,64,256]{3,2,1,0:T(8,128)(2,1)S(1)}, u32[]{:S(2)}, u32[]{:S(2)}) collective-permute-start(bf16[1,5,64,256]{3,2,1,0:T(8,128)(2,1)S(1)} %collective-permute-done.3.field), channel_id=1, source_target_pairs={{0,2},{2,0},{4,6},{6,4},{8,10},{10,8},{12,14},{14,12},{16,18},{18,... | collective-permute-start | bytes 491528 | tf_op jit(solution)/shard_map/ppermute | solution.py:38
  23.4 4.3 %collective-permute-start.6 = (bf16[1,128,256]{2,1,0:T(8,128)(2,1)S(1)}, bf16[1,128,256]{2,1,0:T(8,128)(2,1)S(1)}, u32[]{:S(2)}, u32[]{:S(2)}) collective-permute-start(bf16[1,128,256]{2,1,0:T(8,128)(2,1)S(1)} %shard_map.55), channel_id=1, source_target_pairs={{0,1},{1,0},{2,3},{3,2},{4,5},{5,4},{6,7},{7,6},{8,9},{9,8},{10,11... | collective-permute-start | bytes 196616 | tf_op jit(solution)/shard_map/ppermute | solution.py:34

commit v6 on v5

--- a/solution.py
+++ b/solution.py
@@ -32,6 +32,16 @@
     tm = lax.axis_size("tm")
     pairs = [(t * 2 + r, (t + steps) * 2 + 1 - r) for t in range(tm - steps) for r in range(2)]
     return lax.ppermute(value, ("tm", "rows"), pairs)
+
+
+def by_parity(value, odd):
+    tm = lax.axis_size("tm")
+    if odd:
+        count = tm // 2
+        pairs = [(t, t if t % 2 == 0 else (t // 2 + 1) % count * 2 + 1) for t in range(tm)]
+    else:
+        pairs = [(t, t + 2) for t in range(0, tm - 2, 2)]
+    return lax.ppermute(value, "tm", pairs)
 
 
 def paired(value):
@@ -265,20 +275,20 @@
 
 def coarse_next_kernel(field, weight, body_in, ends_in, body, ends):
     cells = field[...]
-    cells = jnp.where(has_earlier(2), cells, jnp.zeros_like(cells))
-    total, parts = coarse_sums(cells, weight, 0, ends.shape[0])
+    cells = jnp.where(has_earlier(1), cells, jnp.zeros_like(cells))
+    total, parts = coarse_sums(cells, weight, 1, ends.shape[0])
     body[...] = body_in[...] + total
     for side, part in enumerate(parts):
         ends[side] = ends_in[side] + part
 
 
-def middle(direct, relayed):
-    cells = jnp.where(lax.axis_index("tm") % 2 == 1, direct[...], relayed[...])
-    return jnp.where(has_earlier(1), cells, jnp.zeros_like(cells))
-
-
-def coarse_ends_kernel(direct, relayed, weight, ends, out):
-    _, parts = coarse_sums(middle(direct, relayed), weight, 1, ends.shape[0])
+def second_earlier(odd_field, even_field):
+    cells = jnp.where(lax.axis_index("tm") % 2 == 1, odd_field[...], even_field[...])
+    return jnp.where(has_earlier(2), cells, jnp.zeros_like(cells))
+
+
+def coarse_ends_kernel(odd_field, even_field, weight, ends, out):
+    _, parts = coarse_sums(second_earlier(odd_field, even_field), weight, 0, ends.shape[0])
     for side, part in enumerate(parts):
         out[side] = (ends[side] + part).astype(BF16)
 
@@ -287,9 +297,9 @@
     return [(rows - 2) * (1 - lax.axis_index("rows"))] if sides == 1 else [0, rows - 2]
 
 
-def coarse_body_kernel(direct, relayed, weight, body, out, ends, sums):
+def coarse_body_kernel(odd_field, even_field, weight, body, out, ends, sums):
     _, rows, cols, _ = out.shape
-    total, _ = coarse_sums(middle(direct, relayed), weight, 1, ends.shape[0])
+    total, _ = coarse_sums(second_earlier(odd_field, even_field), weight, 0, ends.shape[0])
     sums[...] = body[...] + total
     out[...] = silu(sums[...]).astype(BF16).reshape(out.shape)
     for side, start in enumerate(end_starts(rows, ends.shape[0])):
@@ -360,21 +370,21 @@
     sums = jax.ShapeDtypeStruct((half_rows * half_cols, wide), F32)
     pairs = jax.ShapeDtypeStruct((sides, 2 * half_cols, wide), F32)
     flops = 2 * half_rows * half_cols * 9 * wide * wide
-    field_2 = moved(field, 2, 0)
-    near = paired if times % 2 == 0 else functools.partial(ring, steps=1)
-    direct = near(field)
+    odd_field = by_parity(field, True)
+    even_field = by_parity(field, False)
     body, ends = call(coarse_first_kernel, (sums, pairs), [], flops, (field, conv_coarse))
-    field_2, body, ends, direct = lax.optimization_barrier((field_2, body, ends, direct))
-    relayed = paired(field_2) if times % 2 == 0 else direct
+    odd_field, body, ends = lax.optimization_barrier((odd_field, body, ends))
+    field_1 = paired(odd_field) if times % 2 == 0 else ring(field, 1)
     body, ends = call(
-        coarse_next_kernel, (sums, pairs), [], flops, (field_2, conv_coarse, body, ends)
-    )
+        coarse_next_kernel, (sums, pairs), [], flops, (field_1, conv_coarse, body, ends)
+    )
+    even_field, body, ends = lax.optimization_barrier((even_field, body, ends))
     sent = call(
         coarse_ends_kernel,
         jax.ShapeDtypeStruct(pairs.shape, BF16),
         [],
         flops // 4,
-        (direct, relayed, conv_coarse, ends),
+        (odd_field, even_field, conv_coarse, ends),
     )
     if sides == 1:
         added = swapped(sent, 0)
@@ -385,7 +395,7 @@
         (shape, pairs),
         [pltpu.VMEM(sums.shape, F32)],
         flops,
-        (direct, relayed, conv_coarse, body),
+        (odd_field, even_field, conv_coarse, body),
     )
     return call(
         finish_kernel,

time: 28.6 us -> 30.9 us (1.080)
  starting transfers between devices: 7.83 us -> 12.5 us
  waiting for transfers between devices: 12.1 us -> 9.79 us
    ppermute x2 -> x1, starting transfers between devices: 0.07 us -> 3.78 us  [paired(): lax.ppermute(value, 'tm', [(t, t ^ 1) for t in range(lax.axis_size('tm'))])]
    ppermute x1 -> x2, waiting for transfers between devices: 6.26 us -> 4.94 us  [by_parity(): return lax.ppermute(value, 'tm', pairs)]
    ppermute x2 -> x1, waiting for transfers between devices: 0.8 us -> 0.01 us  [paired(): lax.ppermute(value, 'tm', [(t, t ^ 1) for t in range(lax.axis_size('tm'))])]
    ppermute x1 -> x2, starting transfers between devices: 2.5 us -> 3.22 us  [by_parity(): return lax.ppermute(value, 'tm', pairs)]
  transfers between devices with their start and end apart: 7 -> 7, of which waited for: 5 -> 4; matrix products, arithmetic and copies ran while one was open for 0% -> 0% of each run, Pallas kernels for 19% -> 18%
where the time goes in v6:
time: 30.9 us; the launch traced here: 30.7 us
  starting transfers between devices  12.5 us (40%)
  waiting for transfers between devices  9.79 us (32%)
  Pallas kernels  7.26 us (23%)
  local copies, waits for them, and re-layouts  1.04 us (3%)
    pallas_call x11, Pallas kernels, call(): pl.pallas_call(kernel, out_shape=out_shape, in_specs=[vmem] * (len(args)...  7.26 us
    ppermute x3, starting transfers between devices, swapped(): return lax.ppermute(value, ('tm', 'rows'), pairs)  5.47 us
    ppermute x2, waiting for transfers between devices, by_parity(): return lax.ppermute(value, 'tm', pairs)  4.94 us
    ppermute x1, starting transfers between devices, paired(): lax.ppermute(value, 'tm', [(t, t ^ 1) for t in range(lax.axis_size('tm'))])  3.78 us
    ppermute x2, starting transfers between devices, by_parity(): return lax.ppermute(value, 'tm', pairs)  3.22 us
    ppermute x1, waiting for transfers between devices, ring(): return lax.ppermute(value, 'tm', [(t, (t + steps) % tm) for t in range(tm)])  3.05 us
    ppermute x3, waiting for transfers between devices, swapped(): return lax.ppermute(value, ('tm', 'rows'), pairs)  1.79 us
    unnamed x8, local copies, waits for them, and re-layouts  1.04 us
  transfers between devices with their start and end apart: 7, of which 4 were waited for; matrix products, arithmetic and copies ran while one was open for 0% of the time, Pallas kernels for 18%

profile of v6, /device:TPU:16, one launch (start us, length us, event | category | flops | bytes accessed | tf_op | source)
XLA Modules:
  0.0 30.7 jit_solution(9196982534686848559)
XLA Ops:
  0.0 0.0 copy-start.3
  0.0 0.0 copy-start.1
  0.0 0.0 collective-permute-start.1
  0.0 1.0 %copy-done.3 = bf16[2,8,128,128]{3,2,1,0:T(8,128)(2,1)S(1)} copy-done((bf16[2,8,128,128]{3,2,1,0:T(8,128)(2,1)S(1)}, bf16[2,8,128,128]{3,2,1,0:T(8,128)(2,1)}, u32[]{:S(2)}) %copy-start.3) | copy-done | bytes 524312
  1.0 1.5 %collective-permute-start.2 = (bf16[2,1,128,128]{3,2,1,0:T(8,128)(2,1)S(1)}, bf16[2,1,128,128]{3,2,1,0:T(8,128)(2,1)S(1)}, u32[]{:S(2)}, u32[]{:S(2)}) collective-permute-start(bf16[2,1,128,128]{3,2,1,0:T(8,128)(2,1)S(1)} %shard_map.47), channel_id=1, source_target_pairs={{0,1},{1,0},{2,3},{3,2},{4,5},{5,4},{6,7},{7,6},{8,9},{9,8},{10,11... | collective-permute-start | bytes 196616 | tf_op jit(solution)/shard_map/ppermute | solution.py:34
  2.6 2.4 %collective-permute-start = (bf16[2,1,128,128]{3,2,1,0:T(8,128)(2,1)S(1)}, bf16[2,1,128,128]{3,2,1,0:T(8,128)(2,1)S(1)}, u32[]{:S(2)}, u32[]{:S(2)}) collective-permute-start(bf16[2,1,128,128]{3,2,1,0:T(8,128)(2,1)S(1)} %shard_map.47), channel_id=1, source_target_pairs={{0,3},{1,2},{2,5},{3,4},{4,7},{5,6},{6,9},{7,8},{8,11},{9,10},{10,... | collective-permute-start | bytes 196616 | tf_op jit(solution)/shard_map/ppermute | solution.py:34
  4.9 0.0 copy-done.1
  5.0 1.4 %shard_map.48.own = f32[1024,256]{1,0:T(8,128)S(1)} custom-call(bf16[2,8,128,128]{3,2,1,0:T(8,128)(2,1)S(1)} %copy-done.3, bf16[3,3,384,128]{3,2,1,0:T(8,128)(2,1)S(1)} %copy-done.1), custom_call_target="tpu_custom_call" | custom-call | flops 1207959552 | bytes 1409024 | tf_op jit(solution)/shard_map/pallas_call | solution.py:327
  6.4 0.0 copy-start.2
  6.4 0.0 collective-permute-done.2.above.below
  6.4 0.3 shard_map.49.halo
  6.7 0.0 copy-start
  6.7 3.1 %collective-permute-done.1.frames = bf16[2,8,128,128]{3,2,1,0:T(8,128)(2,1)S(1)} collective-permute-done((bf16[2,8,128,128]{3,2,1,0:T(8,128)(2,1)}, bf16[2,8,128,128]{3,2,1,0:T(8,128)(2,1)S(1)}, u32[]{:S(2)}, u32[]{:S(2)}) %collective-permute-start.1) | collective-permute-done | bytes 524320 | tf_op jit(solution)/shard_map/ppermute | solution.py:28
  9.7 1.4 %shard_map.50.sums = f32[1024,256]{1,0:T(8,128)S(1)} custom-call(bf16[2,8,128,128]{3,2,1,0:T(8,128)(2,1)S(1)} %collective-permute-done.1.frames, bf16[3,3,384,128]{3,2,1,0:T(8,128)(2,1)S(1)} %copy-done.1, f32[1024,256]{1,0:T(8,128)S(1)} %shard_map.48.own, f32[2,128,256]{2,1,0:T(8,128)S(1)} %shard_map.49.halo), custom_call_target="tpu_custom_call" | custom-call | flops 1207959552 | bytes 2719744 | tf_op jit(solution)/shard_map/pallas_call | solution.py:327
  11.1 0.2 collective-permute-done.above.below
  11.4 0.0 copy-done.2
  11.4 0.9 %shard_map.51.field = bf16[1,5,64,256]{3,2,1,0:T(8,128)(2,1)S(1)} custom-call(bf16[2,1,128,128]{3,2,1,0:T(8,128)(2,1)S(1)} %collective-permute-done.above.below, bf16[2,1,128,128]{3,2,1,0:T(8,128)(2,1)S(1)} %collective-permute-done.above.below, bf16[3,3,384,128]{3,2,1,0:T(8,128)(2,1)S(1)} %copy-done.1, f32[1024,256]{1,0:T(8,128)S(1)} %shard_map.50.sums, ...), custom_call_target="tpu_custom_call" | custom-call | flops 402653184 | bytes 2654208 | tf_op jit(solution)/shard_map/pallas_call | solution.py:327
  12.2 0.7 %collective-permute-start.3 = (bf16[1,5,64,256]{3,2,1,0:T(8,128)(2,1)S(1)}, bf16[1,5,64,256]{3,2,1,0:T(8,128)(2,1)S(1)}, u32[]{:S(2)}, u32[]{:S(2)}) collective-permute-start(bf16[1,5,64,256]{3,2,1,0:T(8,128)(2,1)S(1)} %shard_map.51.field), channel_id=1, source_target_pairs={{0,0},{2,6},{4,4},{6,10},{8,8},{10,14},{12,12},{14,18},{16,16},{18... | collective-permute-start | bytes 491528 | tf_op jit(solution)/shard_map/ppermute | solution.py:44
  12.9 0.0 copy-done
  12.9 0.6 %shard_map.52 = (f32[256,256]{1,0:T(8,128)S(1)}, f32[1,128,256]{2,1,0:T(8,128)S(1)}) custom-call(bf16[1,5,64,256]{3,2,1,0:T(8,128)(2,1)S(1)} %shard_map.51.field, bf16[3,3,768,256]{3,2,1,0:T(8,128)(2,1)S(1)} %copy-done), custom_call_target="tpu_custom_call" | custom-call | flops 301989888 | bytes 3702784 | tf_op jit(solution)/shard_map/pallas_call | solution.py:327
  13.5 0.0 collective-permute-done.3.odd_field
  13.5 3.8 %collective-permute-start.5 = (bf16[1,5,64,256]{3,2,1,0:T(8,128)(2,1)S(1)}, bf16[1,5,64,256]{3,2,1,0:T(8,128)(2,1)S(1)}, u32[]{:S(2)}, u32[]{:S(2)}) collective-permute-start(bf16[1,5,64,256]{3,2,1,0:T(8,128)(2,1)S(1)} %collective-permute-done.3.odd_field), channel_id=1, source_target_pairs={{0,2},{2,0},{4,6},{6,4},{8,10},{10,8},{12,14},{14,12},{16,18},{18,... | collective-permute-start | bytes 491528 | tf_op jit(solution)/shard_map/ppermute | solution.py:48
  17.3 2.5 %collective-permute-start.4 = (bf16[1,5,64,256]{3,2,1,0:T(8,128)(2,1)S(1)}, bf16[1,5,64,256]{3,2,1,0:T(8,128)(2,1)S(1)}, u32[]{:S(2)}, u32[]{:S(2)}) collective-permute-start(bf16[1,5,64,256]{3,2,1,0:T(8,128)(2,1)S(1)} %shard_map.51.field), channel_id=1, source_target_pairs={{0,4},{4,8},{8,12},{12,16},{16,20},{20,24},{24,28},{1,5},{5,9},{9,... | collective-permute-start | bytes 491528 | tf_op jit(solution)/shard_map/ppermute | solution.py:44
  19.9 0.0 collective-permute-done.5.field
  19.9 0.6 %shard_map.53 = (f32[256,256]{1,0:T(8,128)S(1)}, f32[1,128,256]{2,1,0:T(8,128)S(1)}) custom-call(bf16[1,5,64,256]{3,2,1,0:T(8,128)(2,1)S(1)} %collective-permute-done.5.field, bf16[3,3,768,256]{3,2,1,0:T(8,128)(2,1)S(1)} %copy-done, f32[256,256]{1,0:T(8,128)S(1)} %get-tuple-element.26.body_in, f32[1,128,256]{2,1,0:T(8,128)S(1)} %get-tuple-element.27.ends_in), custom_call_target="tpu_custom_call" | custom-call | flops 301989888 | bytes 4096000 | tf_op jit(solution)/shard_map/pallas_call | solution.py:327
  20.5 4.9 %collective-permute-done.4.even_field = bf16[1,5,64,256]{3,2,1,0:T(8,128)(2,1)S(1)} collective-permute-done((bf16[1,5,64,256]{3,2,1,0:T(8,128)(2,1)S(1)}, bf16[1,5,64,256]{3,2,1,0:T(8,128)(2,1)S(1)}, u32[]{:S(2)}, u32[]{:S(2)}) %collective-permute-start.4) | collective-permute-done | bytes 163872 | tf_op jit(solution)/shard_map/ppermute | solution.py:44
  25.4 0.3 shard_map.55
  25.7 1.6 %collective-permute-start.6 = (bf16[1,128,256]{2,1,0:T(8,128)(2,1)S(1)}, bf16[1,128,256]{2,1,0:T(8,128)(2,1)S(1)}, u32[]{:S(2)}, u32[]{:S(2)}) collective-permute-start(bf16[1,128,256]{2,1,0:T(8,128)(2,1)S(1)} %shard_map.55), channel_id=1, source_target_pairs={{0,1},{1,0},{2,3},{3,2},{4,5},{5,4},{6,7},{7,6},{8,9},{9,8},{10,11... | collective-permute-start | bytes 196616 | tf_op jit(solution)/shard_map/ppermute | solution.py:34
  27.3 1.2 %shard_map.54 = (bf16[1,4,64,256]{3,2,1,0:T(8,128)(2,1)}, f32[1,128,256]{2,1,0:T(8,128)S(1)}) custom-call(bf16[1,5,64,256]{3,2,1,0:T(8,128)(2,1)S(1)} %collective-permute-done.3.odd_field, bf16[1,5,64,256]{3,2,1,0:T(8,128)(2,1)S(1)} %collective-permute-done.4.even_field, bf16[3,3,768,256]{3,2,1,0:T(8,128)(2,1)S(1)} %copy-done, ...), custom_call_target="tpu_custom_call" | custom-call | flops 301989888 | bytes 4128768 | tf_op jit(solution)/shard_map/pallas_call | solution.py:327
  28.5 1.6 %collective-permute-done.6.added = bf16[1,128,256]{2,1,0:T(8,128)(2,1)S(1)} collective-permute-done((bf16[1,128,256]{2,1,0:T(8,128)(2,1)S(1)}, bf16[1,128,256]{2,1,0:T(8,128)(2,1)S(1)}, u32[]{:S(2)}, u32[]{:S(2)}) %collective-permute-start.6) | collective-permute-done | bytes 65568 | tf_op jit(solution)/shard_map/ppermute | solution.py:34
  30.0 0.7 %shard_map.56 = bf16[1,4,64,256]{3,2,1,0:T(8,128)(2,1)} custom-call(f32[1,128,256]{2,1,0:T(8,128)S(1)} %get-tuple-element.32.ends, bf16[1,128,256]{2,1,0:T(8,128)(2,1)S(1)} %collective-permute-done.6.added, bf16[1,4,64,256]{3,2,1,0:T(8,128)(2,1)} %get-tuple-element.34._), custom_call_target="tpu_custom_call", output_to_operand_aliasing={{}: (2, {})} | custom-call | flops 18874368 | bytes 327680 | tf_op jit(solution)/shard_map/pallas_call | solution.py:327
  (2 shorter events, 0.0 us)
Async XLA Ops:
  0.0 1.0 %copy-start.3 = (bf16[2,8,128,128]{3,2,1,0:T(8,128)(2,1)S(1)}, bf16[2,8,128,128]{3,2,1,0:T(8,128)(2,1)}, u32[]{:S(2)}) copy-start(bf16[2,8,128,128]{3,2,1,0:T(8,128)(2,1)} %frames.1) | copy-start | bytes 1572868
  0.0 4.9 %copy-start.1 = (bf16[3,3,384,128]{3,2,1,0:T(8,128)(2,1)S(1)}, bf16[3,3,384,128]{3,2,1,0:T(8,128)(2,1)}, u32[]{:S(2)}) copy-start(bf16[3,3,384,128]{3,2,1,0:T(8,128)(2,1)} %weight.11) | copy-start | bytes 2654212
  0.0 9.7 %collective-permute-start.1 = (bf16[2,8,128,128]{3,2,1,0:T(8,128)(2,1)}, bf16[2,8,128,128]{3,2,1,0:T(8,128)(2,1)S(1)}, u32[]{:S(2)}, u32[]{:S(2)}) collective-permute-start(bf16[2,8,128,128]{3,2,1,0:T(8,128)(2,1)} %frames.1), channel_id=1, source_target_pairs={{0,2},{2,4},{4,6},{6,8},{8,10},{10,12},{12,14},{14,16},{16,18},{18... | collective-permute-start | bytes 1572872 | tf_op jit(solution)/shard_map/ppermute | solution.py:28
  1.0 5.3 %collective-permute-start.2 = (bf16[2,1,128,128]{3,2,1,0:T(8,128)(2,1)S(1)}, bf16[2,1,128,128]{3,2,1,0:T(8,128)(2,1)S(1)}, u32[]{:S(2)}, u32[]{:S(2)}) collective-permute-start(bf16[2,1,128,128]{3,2,1,0:T(8,128)(2,1)S(1)} %shard_map.47), channel_id=1, source_target_pairs={{0,1},{1,0},{2,3},{3,2},{4,5},{5,4},{6,7},{7,6},{8,9},{9,8},{10,11... | collective-permute-start | bytes 196616 | tf_op jit(solution)/shard_map/ppermute | solution.py:34
  2.6 8.8 %collective-permute-start = (bf16[2,1,128,128]{3,2,1,0:T(8,128)(2,1)S(1)}, bf16[2,1,128,128]{3,2,1,0:T(8,128)(2,1)S(1)}, u32[]{:S(2)}, u32[]{:S(2)}) collective-permute-start(bf16[2,1,128,128]{3,2,1,0:T(8,128)(2,1)S(1)} %shard_map.47), channel_id=1, source_target_pairs={{0,3},{1,2},{2,5},{3,4},{4,7},{5,6},{6,9},{7,8},{8,11},{9,10},{10,... | collective-permute-start | bytes 196616 | tf_op jit(solution)/shard_map/ppermute | solution.py:34
  6.4 5.0 %copy-start.2 = (bf16[3,384,256]{2,1,0:T(8,128)(2,1)S(1)}, bf16[3,384,256]{2,1,0:T(8,128)(2,1)}, u32[]{:S(2)}) copy-start(bf16[3,384,256]{2,1,0:T(8,128)(2,1)} %down.1) | copy-start | bytes 1769476
  6.7 6.3 %copy-start = (bf16[3,3,768,256]{3,2,1,0:T(8,128)(2,1)S(1)}, bf16[3,3,768,256]{3,2,1,0:T(8,128)(2,1)}, u32[]{:S(2)}) copy-start(bf16[3,3,768,256]{3,2,1,0:T(8,128)(2,1)} %weight.15) | copy-start | bytes 10616836
  12.2 1.3 %collective-permute-start.3 = (bf16[1,5,64,256]{3,2,1,0:T(8,128)(2,1)S(1)}, bf16[1,5,64,256]{3,2,1,0:T(8,128)(2,1)S(1)}, u32[]{:S(2)}, u32[]{:S(2)}) collective-permute-start(bf16[1,5,64,256]{3,2,1,0:T(8,128)(2,1)S(1)} %shard_map.51.field), channel_id=1, source_target_pairs={{0,0},{2,6},{4,4},{6,10},{8,8},{10,14},{12,12},{14,18},{16,16},{18... | collective-permute-start | bytes 491528 | tf_op jit(solution)/shard_map/ppermute | solution.py:44
  13.5 6.3 %collective-permute-start.5 = (bf16[1,5,64,256]{3,2,1,0:T(8,128)(2,1)S(1)}, bf16[1,5,64,256]{3,2,1,0:T(8,128)(2,1)S(1)}, u32[]{:S(2)}, u32[]{:S(2)}) collective-permute-start(bf16[1,5,64,256]{3,2,1,0:T(8,128)(2,1)S(1)} %collective-permute-done.3.odd_field), channel_id=1, source_target_pairs={{0,2},{2,0},{4,6},{6,4},{8,10},{10,8},{12,14},{14,12},{16,18},{18,... | collective-permute-start | bytes 491528 | tf_op jit(solution)/shard_map/ppermute | solution.py:48
  17.3 8.1 %collective-permute-start.4 = (bf16[1,5,64,256]{3,2,1,0:T(8,128)(2,1)S(1)}, bf16[1,5,64,256]{3,2,1,0:T(8,128)(2,1)S(1)}, u32[]{:S(2)}, u32[]{:S(2)}) collective-permute-start(bf16[1,5,64,256]{3,2,1,0:T(8,128)(2,1)S(1)} %shard_map.51.field), channel_id=1, source_target_pairs={{0,4},{4,8},{8,12},{12,16},{16,20},{20,24},{24,28},{1,5},{5,9},{9,... | collective-permute-start | bytes 491528 | tf_op jit(solution)/shard_map/ppermute | solution.py:44
  25.7 4.3 %collective-permute-start.6 = (bf16[1,128,256]{2,1,0:T(8,128)(2,1)S(1)}, bf16[1,128,256]{2,1,0:T(8,128)(2,1)S(1)}, u32[]{:S(2)}, u32[]{:S(2)}) collective-permute-start(bf16[1,128,256]{2,1,0:T(8,128)(2,1)S(1)} %shard_map.55), channel_id=1, source_target_pairs={{0,1},{1,0},{2,3},{3,2},{4,5},{5,4},{6,7},{7,6},{8,9},{9,8},{10,11... | collective-permute-start | bytes 196616 | tf_op jit(solution)/shard_map/ppermute | solution.py:34

commit v7 on v6

--- a/solution.py
+++ b/solution.py
@@ -36,11 +36,9 @@
 
 def by_parity(value, odd):
     tm = lax.axis_size("tm")
+    pairs = [(t, t + 2) for t in range(odd, tm - 2, 2)]
     if odd:
-        count = tm // 2
-        pairs = [(t, t if t % 2 == 0 else (t // 2 + 1) % count * 2 + 1) for t in range(tm)]
-    else:
-        pairs = [(t, t + 2) for t in range(0, tm - 2, 2)]
+        pairs += [(t, t) for t in range(0, tm, 2)]
     return lax.ppermute(value, "tm", pairs)
 
 
@@ -370,8 +368,8 @@
     sums = jax.ShapeDtypeStruct((half_rows * half_cols, wide), F32)
     pairs = jax.ShapeDtypeStruct((sides, 2 * half_cols, wide), F32)
     flops = 2 * half_rows * half_cols * 9 * wide * wide
-    odd_field = by_parity(field, True)
-    even_field = by_parity(field, False)
+    odd_field = by_parity(field, 1)
+    even_field = by_parity(field, 0)
     body, ends = call(coarse_first_kernel, (sums, pairs), [], flops, (field, conv_coarse))
     odd_field, body, ends = lax.optimization_barrier((odd_field, body, ends))
     field_1 = paired(odd_field) if times % 2 == 0 else ring(field, 1)

time: 30.9 us -> 30.9 us (level)
  no operation moved by 1% of the time
where the time goes in v7:
time: 30.9 us; the launch traced here: 30.7 us
  starting transfers between devices  12.5 us (40%)
  waiting for transfers between devices  9.79 us (32%)
  Pallas kernels  7.26 us (23%)
  local copies, waits for them, and re-layouts  1.04 us (3%)
    pallas_call x11, Pallas kernels, call(): pl.pallas_call(kernel, out_shape=out_shape, in_specs=[vmem] * (len(args)...  7.26 us
    ppermute x3, starting transfers between devices, swapped(): return lax.ppermute(value, ('tm', 'rows'), pairs)  5.47 us
    ppermute x2, waiting for transfers between devices, by_parity(): return lax.ppermute(value, 'tm', pairs)  4.94 us
    ppermute x1, starting transfers between devices, paired(): lax.ppermute(value, 'tm', [(t, t ^ 1) for t in range(lax.axis_size('tm'))])  3.78 us
    ppermute x2, starting transfers between devices, by_parity(): return lax.ppermute(value, 'tm', pairs)  3.22 us
    ppermute x1, waiting for transfers between devices, ring(): return lax.ppermute(value, 'tm', [(t, (t + steps) % tm) for t in range(tm)])  3.05 us
    ppermute x3, waiting for transfers between devices, swapped(): return lax.ppermute(value, ('tm', 'rows'), pairs)  1.79 us
    unnamed x8, local copies, waits for them, and re-layouts  1.04 us
  transfers between devices with their start and end apart: 7, of which 4 were waited for; matrix products, arithmetic and copies ran while one was open for 0% of the time, Pallas kernels for 18%

profile of v7, /device:TPU:16, one launch (start us, length us, event | category | flops | bytes accessed | tf_op | source)
XLA Modules:
  0.0 30.7 jit_solution(1056846818139745340)
XLA Ops:
  0.0 0.0 copy-start.3
  0.0 0.0 copy-start.1
  0.0 0.0 collective-permute-start.1
  0.0 1.0 %copy-done.3 = bf16[2,8,128,128]{3,2,1,0:T(8,128)(2,1)S(1)} copy-done((bf16[2,8,128,128]{3,2,1,0:T(8,128)(2,1)S(1)}, bf16[2,8,128,128]{3,2,1,0:T(8,128)(2,1)}, u32[]{:S(2)}) %copy-start.3) | copy-done | bytes 524312
  1.0 1.5 %collective-permute-start.2 = (bf16[2,1,128,128]{3,2,1,0:T(8,128)(2,1)S(1)}, bf16[2,1,128,128]{3,2,1,0:T(8,128)(2,1)S(1)}, u32[]{:S(2)}, u32[]{:S(2)}) collective-permute-start(bf16[2,1,128,128]{3,2,1,0:T(8,128)(2,1)S(1)} %shard_map.47), channel_id=1, source_target_pairs={{0,1},{1,0},{2,3},{3,2},{4,5},{5,4},{6,7},{7,6},{8,9},{9,8},{10,11... | collective-permute-start | bytes 196616 | tf_op jit(solution)/shard_map/ppermute | solution.py:34
  2.6 2.4 %collective-permute-start = (bf16[2,1,128,128]{3,2,1,0:T(8,128)(2,1)S(1)}, bf16[2,1,128,128]{3,2,1,0:T(8,128)(2,1)S(1)}, u32[]{:S(2)}, u32[]{:S(2)}) collective-permute-start(bf16[2,1,128,128]{3,2,1,0:T(8,128)(2,1)S(1)} %shard_map.47), channel_id=1, source_target_pairs={{0,3},{1,2},{2,5},{3,4},{4,7},{5,6},{6,9},{7,8},{8,11},{9,10},{10,... | collective-permute-start | bytes 196616 | tf_op jit(solution)/shard_map/ppermute | solution.py:34
  4.9 0.0 copy-done.1
  5.0 1.4 %shard_map.48.own = f32[1024,256]{1,0:T(8,128)S(1)} custom-call(bf16[2,8,128,128]{3,2,1,0:T(8,128)(2,1)S(1)} %copy-done.3, bf16[3,3,384,128]{3,2,1,0:T(8,128)(2,1)S(1)} %copy-done.1), custom_call_target="tpu_custom_call" | custom-call | flops 1207959552 | bytes 1409024 | tf_op jit(solution)/shard_map/pallas_call | solution.py:325
  6.4 0.0 copy-start.2
  6.4 0.0 collective-permute-done.2.above.below
  6.4 0.3 shard_map.49.halo
  6.7 0.0 copy-start
  6.7 3.1 %collective-permute-done.1.frames = bf16[2,8,128,128]{3,2,1,0:T(8,128)(2,1)S(1)} collective-permute-done((bf16[2,8,128,128]{3,2,1,0:T(8,128)(2,1)}, bf16[2,8,128,128]{3,2,1,0:T(8,128)(2,1)S(1)}, u32[]{:S(2)}, u32[]{:S(2)}) %collective-permute-start.1) | collective-permute-done | bytes 524320 | tf_op jit(solution)/shard_map/ppermute | solution.py:28
  9.7 1.4 %shard_map.50.sums = f32[1024,256]{1,0:T(8,128)S(1)} custom-call(bf16[2,8,128,128]{3,2,1,0:T(8,128)(2,1)S(1)} %collective-permute-done.1.frames, bf16[3,3,384,128]{3,2,1,0:T(8,128)(2,1)S(1)} %copy-done.1, f32[1024,256]{1,0:T(8,128)S(1)} %shard_map.48.own, f32[2,128,256]{2,1,0:T(8,128)S(1)} %shard_map.49.halo), custom_call_target="tpu_custom_call" | custom-call | flops 1207959552 | bytes 2719744 | tf_op jit(solution)/shard_map/pallas_call | solution.py:325
  11.1 0.2 collective-permute-done.above.below
  11.4 0.0 copy-done.2
  11.4 0.9 %shard_map.51.field = bf16[1,5,64,256]{3,2,1,0:T(8,128)(2,1)S(1)} custom-call(bf16[2,1,128,128]{3,2,1,0:T(8,128)(2,1)S(1)} %collective-permute-done.above.below, bf16[2,1,128,128]{3,2,1,0:T(8,128)(2,1)S(1)} %collective-permute-done.above.below, bf16[3,3,384,128]{3,2,1,0:T(8,128)(2,1)S(1)} %copy-done.1, f32[1024,256]{1,0:T(8,128)S(1)} %shard_map.50.sums, ...), custom_call_target="tpu_custom_call" | custom-call | flops 402653184 | bytes 2654208 | tf_op jit(solution)/shard_map/pallas_call | solution.py:325
  12.2 0.7 %collective-permute-start.3 = (bf16[1,5,64,256]{3,2,1,0:T(8,128)(2,1)S(1)}, bf16[1,5,64,256]{3,2,1,0:T(8,128)(2,1)S(1)}, u32[]{:S(2)}, u32[]{:S(2)}) collective-permute-start(bf16[1,5,64,256]{3,2,1,0:T(8,128)(2,1)S(1)} %shard_map.51.field), channel_id=1, source_target_pairs={{2,6},{6,10},{10,14},{14,18},{18,22},{22,26},{26,30},{0,0},{4,4},{... | collective-permute-start | bytes 491528 | tf_op jit(solution)/shard_map/ppermute | solution.py:42
  12.9 0.0 copy-done
  12.9 0.6 %shard_map.52 = (f32[256,256]{1,0:T(8,128)S(1)}, f32[1,128,256]{2,1,0:T(8,128)S(1)}) custom-call(bf16[1,5,64,256]{3,2,1,0:T(8,128)(2,1)S(1)} %shard_map.51.field, bf16[3,3,768,256]{3,2,1,0:T(8,128)(2,1)S(1)} %copy-done), custom_call_target="tpu_custom_call" | custom-call | flops 301989888 | bytes 3702784 | tf_op jit(solution)/shard_map/pallas_call | solution.py:325
  13.5 0.0 collective-permute-done.3.odd_field
  13.5 3.8 %collective-permute-start.5 = (bf16[1,5,64,256]{3,2,1,0:T(8,128)(2,1)S(1)}, bf16[1,5,64,256]{3,2,1,0:T(8,128)(2,1)S(1)}, u32[]{:S(2)}, u32[]{:S(2)}) collective-permute-start(bf16[1,5,64,256]{3,2,1,0:T(8,128)(2,1)S(1)} %collective-permute-done.3.odd_field), channel_id=1, source_target_pairs={{0,2},{2,0},{4,6},{6,4},{8,10},{10,8},{12,14},{14,12},{16,18},{18,... | collective-permute-start | bytes 491528 | tf_op jit(solution)/shard_map/ppermute | solution.py:46
  17.3 2.5 %collective-permute-start.4 = (bf16[1,5,64,256]{3,2,1,0:T(8,128)(2,1)S(1)}, bf16[1,5,64,256]{3,2,1,0:T(8,128)(2,1)S(1)}, u32[]{:S(2)}, u32[]{:S(2)}) collective-permute-start(bf16[1,5,64,256]{3,2,1,0:T(8,128)(2,1)S(1)} %shard_map.51.field), channel_id=1, source_target_pairs={{0,4},{4,8},{8,12},{12,16},{16,20},{20,24},{24,28},{1,5},{5,9},{9,... | collective-permute-start | bytes 491528 | tf_op jit(solution)/shard_map/ppermute | solution.py:42
  19.9 0.0 collective-permute-done.5.field
  19.9 0.6 %shard_map.53 = (f32[256,256]{1,0:T(8,128)S(1)}, f32[1,128,256]{2,1,0:T(8,128)S(1)}) custom-call(bf16[1,5,64,256]{3,2,1,0:T(8,128)(2,1)S(1)} %collective-permute-done.5.field, bf16[3,3,768,256]{3,2,1,0:T(8,128)(2,1)S(1)} %copy-done, f32[256,256]{1,0:T(8,128)S(1)} %get-tuple-element.26.body_in, f32[1,128,256]{2,1,0:T(8,128)S(1)} %get-tuple-element.27.ends_in), custom_call_target="tpu_custom_call" | custom-call | flops 301989888 | bytes 4096000 | tf_op jit(solution)/shard_map/pallas_call | solution.py:325
  20.5 4.9 %collective-permute-done.4.even_field = bf16[1,5,64,256]{3,2,1,0:T(8,128)(2,1)S(1)} collective-permute-done((bf16[1,5,64,256]{3,2,1,0:T(8,128)(2,1)S(1)}, bf16[1,5,64,256]{3,2,1,0:T(8,128)(2,1)S(1)}, u32[]{:S(2)}, u32[]{:S(2)}) %collective-permute-start.4) | collective-permute-done | bytes 163872 | tf_op jit(solution)/shard_map/ppermute | solution.py:42
  25.4 0.3 shard_map.55
  25.7 1.6 %collective-permute-start.6 = (bf16[1,128,256]{2,1,0:T(8,128)(2,1)S(1)}, bf16[1,128,256]{2,1,0:T(8,128)(2,1)S(1)}, u32[]{:S(2)}, u32[]{:S(2)}) collective-permute-start(bf16[1,128,256]{2,1,0:T(8,128)(2,1)S(1)} %shard_map.55), channel_id=1, source_target_pairs={{0,1},{1,0},{2,3},{3,2},{4,5},{5,4},{6,7},{7,6},{8,9},{9,8},{10,11... | collective-permute-start | bytes 196616 | tf_op jit(solution)/shard_map/ppermute | solution.py:34
  27.3 1.2 %shard_map.54 = (bf16[1,4,64,256]{3,2,1,0:T(8,128)(2,1)}, f32[1,128,256]{2,1,0:T(8,128)S(1)}) custom-call(bf16[1,5,64,256]{3,2,1,0:T(8,128)(2,1)S(1)} %collective-permute-done.3.odd_field, bf16[1,5,64,256]{3,2,1,0:T(8,128)(2,1)S(1)} %collective-permute-done.4.even_field, bf16[3,3,768,256]{3,2,1,0:T(8,128)(2,1)S(1)} %copy-done, ...), custom_call_target="tpu_custom_call" | custom-call | flops 301989888 | bytes 4128768 | tf_op jit(solution)/shard_map/pallas_call | solution.py:325
  28.5 1.6 %collective-permute-done.6.added = bf16[1,128,256]{2,1,0:T(8,128)(2,1)S(1)} collective-permute-done((bf16[1,128,256]{2,1,0:T(8,128)(2,1)S(1)}, bf16[1,128,256]{2,1,0:T(8,128)(2,1)S(1)}, u32[]{:S(2)}, u32[]{:S(2)}) %collective-permute-start.6) | collective-permute-done | bytes 65568 | tf_op jit(solution)/shard_map/ppermute | solution.py:34
  30.0 0.7 %shard_map.56 = bf16[1,4,64,256]{3,2,1,0:T(8,128)(2,1)} custom-call(f32[1,128,256]{2,1,0:T(8,128)S(1)} %get-tuple-element.32.ends, bf16[1,128,256]{2,1,0:T(8,128)(2,1)S(1)} %collective-permute-done.6.added, bf16[1,4,64,256]{3,2,1,0:T(8,128)(2,1)} %get-tuple-element.34._), custom_call_target="tpu_custom_call", output_to_operand_aliasing={{}: (2, {})} | custom-call | flops 18874368 | bytes 327680 | tf_op jit(solution)/shard_map/pallas_call | solution.py:325
  (2 shorter events, 0.0 us)
Async XLA Ops:
  0.0 1.0 %copy-start.3 = (bf16[2,8,128,128]{3,2,1,0:T(8,128)(2,1)S(1)}, bf16[2,8,128,128]{3,2,1,0:T(8,128)(2,1)}, u32[]{:S(2)}) copy-start(bf16[2,8,128,128]{3,2,1,0:T(8,128)(2,1)} %frames.1) | copy-start | bytes 1572868
  0.0 4.9 %copy-start.1 = (bf16[3,3,384,128]{3,2,1,0:T(8,128)(2,1)S(1)}, bf16[3,3,384,128]{3,2,1,0:T(8,128)(2,1)}, u32[]{:S(2)}) copy-start(bf16[3,3,384,128]{3,2,1,0:T(8,128)(2,1)} %weight.11) | copy-start | bytes 2654212
  0.0 9.7 %collective-permute-start.1 = (bf16[2,8,128,128]{3,2,1,0:T(8,128)(2,1)}, bf16[2,8,128,128]{3,2,1,0:T(8,128)(2,1)S(1)}, u32[]{:S(2)}, u32[]{:S(2)}) collective-permute-start(bf16[2,8,128,128]{3,2,1,0:T(8,128)(2,1)} %frames.1), channel_id=1, source_target_pairs={{0,2},{2,4},{4,6},{6,8},{8,10},{10,12},{12,14},{14,16},{16,18},{18... | collective-permute-start | bytes 1572872 | tf_op jit(solution)/shard_map/ppermute | solution.py:28
  1.0 5.3 %collective-permute-start.2 = (bf16[2,1,128,128]{3,2,1,0:T(8,128)(2,1)S(1)}, bf16[2,1,128,128]{3,2,1,0:T(8,128)(2,1)S(1)}, u32[]{:S(2)}, u32[]{:S(2)}) collective-permute-start(bf16[2,1,128,128]{3,2,1,0:T(8,128)(2,1)S(1)} %shard_map.47), channel_id=1, source_target_pairs={{0,1},{1,0},{2,3},{3,2},{4,5},{5,4},{6,7},{7,6},{8,9},{9,8},{10,11... | collective-permute-start | bytes 196616 | tf_op jit(solution)/shard_map/ppermute | solution.py:34
  2.6 8.8 %collective-permute-start = (bf16[2,1,128,128]{3,2,1,0:T(8,128)(2,1)S(1)}, bf16[2,1,128,128]{3,2,1,0:T(8,128)(2,1)S(1)}, u32[]{:S(2)}, u32[]{:S(2)}) collective-permute-start(bf16[2,1,128,128]{3,2,1,0:T(8,128)(2,1)S(1)} %shard_map.47), channel_id=1, source_target_pairs={{0,3},{1,2},{2,5},{3,4},{4,7},{5,6},{6,9},{7,8},{8,11},{9,10},{10,... | collective-permute-start | bytes 196616 | tf_op jit(solution)/shard_map/ppermute | solution.py:34
  6.4 5.0 %copy-start.2 = (bf16[3,384,256]{2,1,0:T(8,128)(2,1)S(1)}, bf16[3,384,256]{2,1,0:T(8,128)(2,1)}, u32[]{:S(2)}) copy-start(bf16[3,384,256]{2,1,0:T(8,128)(2,1)} %down.1) | copy-start | bytes 1769476
  6.7 6.3 %copy-start = (bf16[3,3,768,256]{3,2,1,0:T(8,128)(2,1)S(1)}, bf16[3,3,768,256]{3,2,1,0:T(8,128)(2,1)}, u32[]{:S(2)}) copy-start(bf16[3,3,768,256]{3,2,1,0:T(8,128)(2,1)} %weight.15) | copy-start | bytes 10616836
  12.2 1.3 %collective-permute-start.3 = (bf16[1,5,64,256]{3,2,1,0:T(8,128)(2,1)S(1)}, bf16[1,5,64,256]{3,2,1,0:T(8,128)(2,1)S(1)}, u32[]{:S(2)}, u32[]{:S(2)}) collective-permute-start(bf16[1,5,64,256]{3,2,1,0:T(8,128)(2,1)S(1)} %shard_map.51.field), channel_id=1, source_target_pairs={{2,6},{6,10},{10,14},{14,18},{18,22},{22,26},{26,30},{0,0},{4,4},{... | collective-permute-start | bytes 491528 | tf_op jit(solution)/shard_map/ppermute | solution.py:42
  13.5 6.3 %collective-permute-start.5 = (bf16[1,5,64,256]{3,2,1,0:T(8,128)(2,1)S(1)}, bf16[1,5,64,256]{3,2,1,0:T(8,128)(2,1)S(1)}, u32[]{:S(2)}, u32[]{:S(2)}) collective-permute-start(bf16[1,5,64,256]{3,2,1,0:T(8,128)(2,1)S(1)} %collective-permute-done.3.odd_field), channel_id=1, source_target_pairs={{0,2},{2,0},{4,6},{6,4},{8,10},{10,8},{12,14},{14,12},{16,18},{18,... | collective-permute-start | bytes 491528 | tf_op jit(solution)/shard_map/ppermute | solution.py:46
  17.3 8.1 %collective-permute-start.4 = (bf16[1,5,64,256]{3,2,1,0:T(8,128)(2,1)S(1)}, bf16[1,5,64,256]{3,2,1,0:T(8,128)(2,1)S(1)}, u32[]{:S(2)}, u32[]{:S(2)}) collective-permute-start(bf16[1,5,64,256]{3,2,1,0:T(8,128)(2,1)S(1)} %shard_map.51.field), channel_id=1, source_target_pairs={{0,4},{4,8},{8,12},{12,16},{16,20},{20,24},{24,28},{1,5},{5,9},{9,... | collective-permute-start | bytes 491528 | tf_op jit(solution)/shard_map/ppermute | solution.py:42
  25.7 4.3 %collective-permute-start.6 = (bf16[1,128,256]{2,1,0:T(8,128)(2,1)S(1)}, bf16[1,128,256]{2,1,0:T(8,128)(2,1)S(1)}, u32[]{:S(2)}, u32[]{:S(2)}) collective-permute-start(bf16[1,128,256]{2,1,0:T(8,128)(2,1)S(1)} %shard_map.55), channel_id=1, source_target_pairs={{0,1},{1,0},{2,3},{3,2},{4,5},{5,4},{6,7},{7,6},{8,9},{9,8},{10,11... | collective-permute-start | bytes 196616 | tf_op jit(solution)/shard_map/ppermute | solution.py:34

commit v8 on v7

--- a/solution.py
+++ b/solution.py
@@ -137,6 +137,42 @@
     return sums[1] + column_shift(sums[0], cols, 1) + column_shift(sums[2], cols, -1)
 
 
+def previous_rows(row, outs, weight):
+    channels = weight.shape[-1]
+    cols = next(x for r in outs if (x := row(1, r)) is not None).shape[0]
+    zero = jnp.zeros((cols, channels), BF16)
+    none = jnp.zeros((channels, channels), BF16)
+
+    def cells(taps):
+        lines = [
+            jnp.concatenate([zero if (x := row(f, r - 1 + b)) is None else x for f, b in taps], axis=1)
+            for r in outs
+        ]
+        return jnp.concatenate(lines, axis=0)
+
+    def part(tap, b, e):
+        return weight[tap, b, e * channels : (e + 1) * channels]
+
+    def pair(left, right):
+        return jnp.concatenate([left, right], axis=1)
+
+    dot = functools.partial(jnp.dot, preferred_element_type=F32)
+    near = cells([(1, 0), (1, 1), (1, 2), (0, 2)])
+    sums = []
+    for e in range(3):
+        right = [pair(part(1, b, e), part(0, b, e)) for b in range(3)] + [pair(part(0, 2, e), none)]
+        sums.append(dot(near, jnp.concatenate(right, axis=0)))
+    far = cells([(0, 0), (0, 1)])
+    both = dot(far, jnp.concatenate([pair(part(0, b, 0), part(0, b, 1)) for b in range(2)], axis=0))
+    last = dot(far, jnp.concatenate([part(0, b, 2) for b in range(2)], axis=0))
+    old = (both[:, :channels], both[:, channels:], last)
+    first = [x[:, :channels] + y for x, y in zip(sums, old)]
+    second = [x[:, channels:] for x in sums]
+    return pair(*(
+        x[1] + column_shift(x[0], cols, 1) + column_shift(x[2], cols, -1) for x in (first, second)
+    ))
+
+
 def chunks_of(count):
     size = next(c for c in (4, 3, 2, 1) if count % c == 0)
     return [range(i, i + size) for i in range(0, count, size)]
@@ -153,6 +189,12 @@
 
 
 def halo_sums(above, below, weight, first_tap, rows):
+    if lax.axis_size("rows") == 2:
+        b = 2 * (1 - lax.axis_index("rows"))
+        added = fine_rows(lambda f, i: above[f, 0], [0], [b], weight, first_tap)
+        zero = jnp.zeros_like(added)
+        return jnp.where(has_above(), added, zero), jnp.where(has_above(), zero, added)
+
     def row(f, i):
         if i == -1:
             cells, have = above[f, 0], has_above()
@@ -181,7 +223,7 @@
         return frames[f, i] if 0 <= i < rows else None
 
     for outs in chunks_of(rows):
-        total = jnp.where(has_earlier(1), fine_rows(row, outs, range(3), weight, 0), 0.0)
+        total = jnp.where(has_earlier(1), previous_rows(row, outs, weight), 0.0)
         for i, r in enumerate(outs):
             line = total[i * cols : (i + 1) * cols] + own[r * cols : (r + 1) * cols]
             for k, halo_r in enumerate((0, rows - 1)):
@@ -196,13 +238,13 @@
     return ((fine[:, :channels] + fine[:, channels:]) * 0.5).astype(BF16).astype(F32)
 
 
-def down_taps(pooled, first, row_taps, half_cols):
-    pieces = [
-        pooled[first + i, pl.ds(e, half_cols, stride=2), :].astype(BF16)
-        for i in range(row_taps)
-        for e in range(3)
+def down_taps(pooled, half_cols):
+    return [
+        jnp.concatenate(
+            [pooled[i, pl.ds(e, half_cols, stride=2), :].astype(BF16) for e in range(3)], axis=1
+        )
+        for i in range(pooled.shape[0])
     ]
-    return jnp.concatenate(pieces, axis=1)
 
 
 def put_pooled(pooled, lines):
@@ -228,10 +270,11 @@
         lines.append(pool(line))
     put_pooled(pooled, [*lines, jnp.zeros_like(lines[0])])
     dot = functools.partial(jnp.dot, preferred_element_type=F32)
-    left = [down_taps(pooled, 2 * p, 3, half_cols) for p in range(half_rows)]
+    taps = down_taps(pooled, half_cols)
+    left = [jnp.concatenate(taps[2 * p : 2 * p + 3], axis=1) for p in range(half_rows)]
     own = dot(jnp.concatenate(left, axis=0), down[...].reshape(-1, down.shape[-1]))
     out[0, :half_rows] = own.astype(BF16).reshape(half_rows, half_cols, -1)
-    out[0, half_rows] = dot(down_taps(pooled, 0, 1, half_cols), down[2]).astype(BF16)
+    out[0, half_rows] = dot(taps[0], down[2]).astype(BF16)
 
 
 def column_taps(flat, cols):

time: 30.9 us -> 30.7 us (level)
  transfers between devices with their start and end apart: 7 -> 7, of which waited for: 4 -> 4; matrix products, arithmetic and copies ran while one was open for 0% -> 0% of each run, Pallas kernels for 18% -> 17%
where the time goes in v8:
time: 30.7 us; the launch traced here: 30.5 us
  starting transfers between devices  12.3 us (40%)
  waiting for transfers between devices  9.97 us (32%)
  Pallas kernels  7.01 us (23%)
  local copies, waits for them, and re-layouts  1.04 us (3%)
    pallas_call x11, Pallas kernels, call(): pl.pallas_call(kernel, out_shape=out_shape, in_specs=[vmem] * (len(args)...  7.01 us
    ppermute x3, starting transfers between devices, swapped(): return lax.ppermute(value, ('tm', 'rows'), pairs)  5.47 us
    ppermute x2, waiting for transfers between devices, by_parity(): return lax.ppermute(value, 'tm', pairs)  4.94 us
    ppermute x1, starting transfers between devices, paired(): lax.ppermute(value, 'tm', [(t, t ^ 1) for t in range(lax.axis_size('tm'))])  3.66 us
    ppermute x2, starting transfers between devices, by_parity(): return lax.ppermute(value, 'tm', pairs)  3.22 us
    ppermute x1, waiting for transfers between devices, ring(): return lax.ppermute(value, 'tm', [(t, (t + steps) % tm) for t in range(tm)])  3.1 us
    ppermute x3, waiting for transfers between devices, swapped(): return lax.ppermute(value, ('tm', 'rows'), pairs)  1.93 us
    unnamed x8, local copies, waits for them, and re-layouts  1.04 us
  transfers between devices with their start and end apart: 7, of which 4 were waited for; matrix products, arithmetic and copies ran while one was open for 0% of the time, Pallas kernels for 17%

profile of v8, /device:TPU:16, one launch (start us, length us, event | category | flops | bytes accessed | tf_op | source)
XLA Modules:
  0.0 30.5 jit_solution(8826728852662924377)
XLA Ops:
  0.0 0.0 copy-start.3
  0.0 0.0 copy-start.1
  0.0 0.0 collective-permute-start.1
  0.0 1.0 %copy-done.3 = bf16[2,8,128,128]{3,2,1,0:T(8,128)(2,1)S(1)} copy-done((bf16[2,8,128,128]{3,2,1,0:T(8,128)(2,1)S(1)}, bf16[2,8,128,128]{3,2,1,0:T(8,128)(2,1)}, u32[]{:S(2)}) %copy-start.3) | copy-done | bytes 524312
  1.0 1.5 %collective-permute-start.2 = (bf16[2,1,128,128]{3,2,1,0:T(8,128)(2,1)S(1)}, bf16[2,1,128,128]{3,2,1,0:T(8,128)(2,1)S(1)}, u32[]{:S(2)}, u32[]{:S(2)}) collective-permute-start(bf16[2,1,128,128]{3,2,1,0:T(8,128)(2,1)S(1)} %shard_map.47), channel_id=1, source_target_pairs={{0,1},{1,0},{2,3},{3,2},{4,5},{5,4},{6,7},{7,6},{8,9},{9,8},{10,11... | collective-permute-start | bytes 196616 | tf_op jit(solution)/shard_map/ppermute | solution.py:34
  2.6 2.4 %collective-permute-start = (bf16[2,1,128,128]{3,2,1,0:T(8,128)(2,1)S(1)}, bf16[2,1,128,128]{3,2,1,0:T(8,128)(2,1)S(1)}, u32[]{:S(2)}, u32[]{:S(2)}) collective-permute-start(bf16[2,1,128,128]{3,2,1,0:T(8,128)(2,1)S(1)} %shard_map.47), channel_id=1, source_target_pairs={{0,3},{1,2},{2,5},{3,4},{4,7},{5,6},{6,9},{7,8},{8,11},{9,10},{10,... | collective-permute-start | bytes 196616 | tf_op jit(solution)/shard_map/ppermute | solution.py:34
  4.9 0.0 copy-done.1
  5.0 1.4 %shard_map.48.own = f32[1024,256]{1,0:T(8,128)S(1)} custom-call(bf16[2,8,128,128]{3,2,1,0:T(8,128)(2,1)S(1)} %copy-done.3, bf16[3,3,384,128]{3,2,1,0:T(8,128)(2,1)S(1)} %copy-done.1), custom_call_target="tpu_custom_call" | custom-call | flops 1207959552 | bytes 1409024 | tf_op jit(solution)/shard_map/pallas_call | solution.py:368
  6.4 0.0 copy-start.2
  6.4 0.0 collective-permute-done.2.above.below
  6.4 0.2 shard_map.49.halo
  6.6 0.0 copy-start
  6.6 3.1 %collective-permute-done.1.frames = bf16[2,8,128,128]{3,2,1,0:T(8,128)(2,1)S(1)} collective-permute-done((bf16[2,8,128,128]{3,2,1,0:T(8,128)(2,1)}, bf16[2,8,128,128]{3,2,1,0:T(8,128)(2,1)S(1)}, u32[]{:S(2)}, u32[]{:S(2)}) %collective-permute-start.1) | collective-permute-done | bytes 524320 | tf_op jit(solution)/shard_map/ppermute | solution.py:28
  9.7 1.3 %shard_map.50.sums = f32[1024,256]{1,0:T(8,128)S(1)} custom-call(bf16[2,8,128,128]{3,2,1,0:T(8,128)(2,1)S(1)} %collective-permute-done.1.frames, bf16[3,3,384,128]{3,2,1,0:T(8,128)(2,1)S(1)} %copy-done.1, f32[1024,256]{1,0:T(8,128)S(1)} %shard_map.48.own, f32[2,128,256]{2,1,0:T(8,128)S(1)} %shard_map.49.halo), custom_call_target="tpu_custom_call" | custom-call | flops 1207959552 | bytes 2719744 | tf_op jit(solution)/shard_map/pallas_call | solution.py:368
  11.0 0.4 %collective-permute-done.above.below = bf16[2,1,128,128]{3,2,1,0:T(8,128)(2,1)S(1)} collective-permute-done((bf16[2,1,128,128]{3,2,1,0:T(8,128)(2,1)S(1)}, bf16[2,1,128,128]{3,2,1,0:T(8,128)(2,1)S(1)}, u32[]{:S(2)}, u32[]{:S(2)}) %collective-permute-start) | collective-permute-done | bytes 65568 | tf_op jit(solution)/shard_map/ppermute | solution.py:34
  11.4 0.0 copy-done.2
  11.4 0.8 %shard_map.51.field = bf16[1,5,64,256]{3,2,1,0:T(8,128)(2,1)S(1)} custom-call(bf16[2,1,128,128]{3,2,1,0:T(8,128)(2,1)S(1)} %collective-permute-done.above.below, bf16[2,1,128,128]{3,2,1,0:T(8,128)(2,1)S(1)} %collective-permute-done.above.below, bf16[3,3,384,128]{3,2,1,0:T(8,128)(2,1)S(1)} %copy-done.1, f32[1024,256]{1,0:T(8,128)S(1)} %shard_map.50.sums, ...), custom_call_target="tpu_custom_call" | custom-call | flops 402653184 | bytes 2654208 | tf_op jit(solution)/shard_map/pallas_call | solution.py:368
  12.2 0.7 %collective-permute-start.3 = (bf16[1,5,64,256]{3,2,1,0:T(8,128)(2,1)S(1)}, bf16[1,5,64,256]{3,2,1,0:T(8,128)(2,1)S(1)}, u32[]{:S(2)}, u32[]{:S(2)}) collective-permute-start(bf16[1,5,64,256]{3,2,1,0:T(8,128)(2,1)S(1)} %shard_map.51.field), channel_id=1, source_target_pairs={{2,6},{6,10},{10,14},{14,18},{18,22},{22,26},{26,30},{0,0},{4,4},{... | collective-permute-start | bytes 491528 | tf_op jit(solution)/shard_map/ppermute | solution.py:42
  12.8 0.0 copy-done
  12.9 0.6 %shard_map.52 = (f32[256,256]{1,0:T(8,128)S(1)}, f32[1,128,256]{2,1,0:T(8,128)S(1)}) custom-call(bf16[1,5,64,256]{3,2,1,0:T(8,128)(2,1)S(1)} %shard_map.51.field, bf16[3,3,768,256]{3,2,1,0:T(8,128)(2,1)S(1)} %copy-done), custom_call_target="tpu_custom_call" | custom-call | flops 301989888 | bytes 3702784 | tf_op jit(solution)/shard_map/pallas_call | solution.py:368
  13.5 0.0 collective-permute-done.3.odd_field
  13.5 3.7 %collective-permute-start.5 = (bf16[1,5,64,256]{3,2,1,0:T(8,128)(2,1)S(1)}, bf16[1,5,64,256]{3,2,1,0:T(8,128)(2,1)S(1)}, u32[]{:S(2)}, u32[]{:S(2)}) collective-permute-start(bf16[1,5,64,256]{3,2,1,0:T(8,128)(2,1)S(1)} %collective-permute-done.3.odd_field), channel_id=1, source_target_pairs={{0,2},{2,0},{4,6},{6,4},{8,10},{10,8},{12,14},{14,12},{16,18},{18,... | collective-permute-start | bytes 491528 | tf_op jit(solution)/shard_map/ppermute | solution.py:46
  17.1 2.5 %collective-permute-start.4 = (bf16[1,5,64,256]{3,2,1,0:T(8,128)(2,1)S(1)}, bf16[1,5,64,256]{3,2,1,0:T(8,128)(2,1)S(1)}, u32[]{:S(2)}, u32[]{:S(2)}) collective-permute-start(bf16[1,5,64,256]{3,2,1,0:T(8,128)(2,1)S(1)} %shard_map.51.field), channel_id=1, source_target_pairs={{0,4},{4,8},{8,12},{12,16},{16,20},{20,24},{24,28},{1,5},{5,9},{9,... | collective-permute-start | bytes 491528 | tf_op jit(solution)/shard_map/ppermute | solution.py:42
  19.7 0.0 collective-permute-done.5.field
  19.7 0.6 %shard_map.53 = (f32[256,256]{1,0:T(8,128)S(1)}, f32[1,128,256]{2,1,0:T(8,128)S(1)}) custom-call(bf16[1,5,64,256]{3,2,1,0:T(8,128)(2,1)S(1)} %collective-permute-done.5.field, bf16[3,3,768,256]{3,2,1,0:T(8,128)(2,1)S(1)} %copy-done, f32[256,256]{1,0:T(8,128)S(1)} %get-tuple-element.26.body_in, f32[1,128,256]{2,1,0:T(8,128)S(1)} %get-tuple-element.27.ends_in), custom_call_target="tpu_custom_call" | custom-call | flops 301989888 | bytes 4096000 | tf_op jit(solution)/shard_map/pallas_call | solution.py:368
  20.3 4.9 %collective-permute-done.4.even_field = bf16[1,5,64,256]{3,2,1,0:T(8,128)(2,1)S(1)} collective-permute-done((bf16[1,5,64,256]{3,2,1,0:T(8,128)(2,1)S(1)}, bf16[1,5,64,256]{3,2,1,0:T(8,128)(2,1)S(1)}, u32[]{:S(2)}, u32[]{:S(2)}) %collective-permute-start.4) | collective-permute-done | bytes 163872 | tf_op jit(solution)/shard_map/ppermute | solution.py:42
  25.2 0.3 shard_map.55
  25.5 1.6 %collective-permute-start.6 = (bf16[1,128,256]{2,1,0:T(8,128)(2,1)S(1)}, bf16[1,128,256]{2,1,0:T(8,128)(2,1)S(1)}, u32[]{:S(2)}, u32[]{:S(2)}) collective-permute-start(bf16[1,128,256]{2,1,0:T(8,128)(2,1)S(1)} %shard_map.55), channel_id=1, source_target_pairs={{0,1},{1,0},{2,3},{3,2},{4,5},{5,4},{6,7},{7,6},{8,9},{9,8},{10,11... | collective-permute-start | bytes 196616 | tf_op jit(solution)/shard_map/ppermute | solution.py:34
  27.1 1.2 %shard_map.54 = (bf16[1,4,64,256]{3,2,1,0:T(8,128)(2,1)}, f32[1,128,256]{2,1,0:T(8,128)S(1)}) custom-call(bf16[1,5,64,256]{3,2,1,0:T(8,128)(2,1)S(1)} %collective-permute-done.3.odd_field, bf16[1,5,64,256]{3,2,1,0:T(8,128)(2,1)S(1)} %collective-permute-done.4.even_field, bf16[3,3,768,256]{3,2,1,0:T(8,128)(2,1)S(1)} %copy-done, ...), custom_call_target="tpu_custom_call" | custom-call | flops 301989888 | bytes 4128768 | tf_op jit(solution)/shard_map/pallas_call | solution.py:368
  28.3 1.6 %collective-permute-done.6.added = bf16[1,128,256]{2,1,0:T(8,128)(2,1)S(1)} collective-permute-done((bf16[1,128,256]{2,1,0:T(8,128)(2,1)S(1)}, bf16[1,128,256]{2,1,0:T(8,128)(2,1)S(1)}, u32[]{:S(2)}, u32[]{:S(2)}) %collective-permute-start.6) | collective-permute-done | bytes 65568 | tf_op jit(solution)/shard_map/ppermute | solution.py:34
  29.8 0.7 %shard_map.56 = bf16[1,4,64,256]{3,2,1,0:T(8,128)(2,1)} custom-call(f32[1,128,256]{2,1,0:T(8,128)S(1)} %get-tuple-element.32.ends, bf16[1,128,256]{2,1,0:T(8,128)(2,1)S(1)} %collective-permute-done.6.added, bf16[1,4,64,256]{3,2,1,0:T(8,128)(2,1)} %get-tuple-element.34._), custom_call_target="tpu_custom_call", output_to_operand_aliasing={{}: (2, {})} | custom-call | flops 18874368 | bytes 327680 | tf_op jit(solution)/shard_map/pallas_call | solution.py:368
  (2 shorter events, 0.0 us)
Async XLA Ops:
  0.0 1.0 %copy-start.3 = (bf16[2,8,128,128]{3,2,1,0:T(8,128)(2,1)S(1)}, bf16[2,8,128,128]{3,2,1,0:T(8,128)(2,1)}, u32[]{:S(2)}) copy-start(bf16[2,8,128,128]{3,2,1,0:T(8,128)(2,1)} %frames.1) | copy-start | bytes 1572868
  0.0 4.9 %copy-start.1 = (bf16[3,3,384,128]{3,2,1,0:T(8,128)(2,1)S(1)}, bf16[3,3,384,128]{3,2,1,0:T(8,128)(2,1)}, u32[]{:S(2)}) copy-start(bf16[3,3,384,128]{3,2,1,0:T(8,128)(2,1)} %weight.11) | copy-start | bytes 2654212
  0.0 9.7 %collective-permute-start.1 = (bf16[2,8,128,128]{3,2,1,0:T(8,128)(2,1)}, bf16[2,8,128,128]{3,2,1,0:T(8,128)(2,1)S(1)}, u32[]{:S(2)}, u32[]{:S(2)}) collective-permute-start(bf16[2,8,128,128]{3,2,1,0:T(8,128)(2,1)} %frames.1), channel_id=1, source_target_pairs={{0,2},{2,4},{4,6},{6,8},{8,10},{10,12},{12,14},{14,16},{16,18},{18... | collective-permute-start | bytes 1572872 | tf_op jit(solution)/shard_map/ppermute | solution.py:28
  1.0 5.3 %collective-permute-start.2 = (bf16[2,1,128,128]{3,2,1,0:T(8,128)(2,1)S(1)}, bf16[2,1,128,128]{3,2,1,0:T(8,128)(2,1)S(1)}, u32[]{:S(2)}, u32[]{:S(2)}) collective-permute-start(bf16[2,1,128,128]{3,2,1,0:T(8,128)(2,1)S(1)} %shard_map.47), channel_id=1, source_target_pairs={{0,1},{1,0},{2,3},{3,2},{4,5},{5,4},{6,7},{7,6},{8,9},{9,8},{10,11... | collective-permute-start | bytes 196616 | tf_op jit(solution)/shard_map/ppermute | solution.py:34
  2.6 8.8 %collective-permute-start = (bf16[2,1,128,128]{3,2,1,0:T(8,128)(2,1)S(1)}, bf16[2,1,128,128]{3,2,1,0:T(8,128)(2,1)S(1)}, u32[]{:S(2)}, u32[]{:S(2)}) collective-permute-start(bf16[2,1,128,128]{3,2,1,0:T(8,128)(2,1)S(1)} %shard_map.47), channel_id=1, source_target_pairs={{0,3},{1,2},{2,5},{3,4},{4,7},{5,6},{6,9},{7,8},{8,11},{9,10},{10,... | collective-permute-start | bytes 196616 | tf_op jit(solution)/shard_map/ppermute | solution.py:34
  6.4 5.0 %copy-start.2 = (bf16[3,384,256]{2,1,0:T(8,128)(2,1)S(1)}, bf16[3,384,256]{2,1,0:T(8,128)(2,1)}, u32[]{:S(2)}) copy-start(bf16[3,384,256]{2,1,0:T(8,128)(2,1)} %down.1) | copy-start | bytes 1769476
  6.6 6.2 %copy-start = (bf16[3,3,768,256]{3,2,1,0:T(8,128)(2,1)S(1)}, bf16[3,3,768,256]{3,2,1,0:T(8,128)(2,1)}, u32[]{:S(2)}) copy-start(bf16[3,3,768,256]{3,2,1,0:T(8,128)(2,1)} %weight.15) | copy-start | bytes 10616836
  12.2 1.3 %collective-permute-start.3 = (bf16[1,5,64,256]{3,2,1,0:T(8,128)(2,1)S(1)}, bf16[1,5,64,256]{3,2,1,0:T(8,128)(2,1)S(1)}, u32[]{:S(2)}, u32[]{:S(2)}) collective-permute-start(bf16[1,5,64,256]{3,2,1,0:T(8,128)(2,1)S(1)} %shard_map.51.field), channel_id=1, source_target_pairs={{2,6},{6,10},{10,14},{14,18},{18,22},{22,26},{26,30},{0,0},{4,4},{... | collective-permute-start | bytes 491528 | tf_op jit(solution)/shard_map/ppermute | solution.py:42
  13.5 6.2 %collective-permute-start.5 = (bf16[1,5,64,256]{3,2,1,0:T(8,128)(2,1)S(1)}, bf16[1,5,64,256]{3,2,1,0:T(8,128)(2,1)S(1)}, u32[]{:S(2)}, u32[]{:S(2)}) collective-permute-start(bf16[1,5,64,256]{3,2,1,0:T(8,128)(2,1)S(1)} %collective-permute-done.3.odd_field), channel_id=1, source_target_pairs={{0,2},{2,0},{4,6},{6,4},{8,10},{10,8},{12,14},{14,12},{16,18},{18,... | collective-permute-start | bytes 491528 | tf_op jit(solution)/shard_map/ppermute | solution.py:46
  17.1 8.1 %collective-permute-start.4 = (bf16[1,5,64,256]{3,2,1,0:T(8,128)(2,1)S(1)}, bf16[1,5,64,256]{3,2,1,0:T(8,128)(2,1)S(1)}, u32[]{:S(2)}, u32[]{:S(2)}) collective-permute-start(bf16[1,5,64,256]{3,2,1,0:T(8,128)(2,1)S(1)} %shard_map.51.field), channel_id=1, source_target_pairs={{0,4},{4,8},{8,12},{12,16},{16,20},{20,24},{24,28},{1,5},{5,9},{9,... | collective-permute-start | bytes 491528 | tf_op jit(solution)/shard_map/ppermute | solution.py:42
  25.5 4.3 %collective-permute-start.6 = (bf16[1,128,256]{2,1,0:T(8,128)(2,1)S(1)}, bf16[1,128,256]{2,1,0:T(8,128)(2,1)S(1)}, u32[]{:S(2)}, u32[]{:S(2)}) collective-permute-start(bf16[1,128,256]{2,1,0:T(8,128)(2,1)S(1)} %shard_map.55), channel_id=1, source_target_pairs={{0,1},{1,0},{2,3},{3,2},{4,5},{5,4},{6,7},{7,6},{8,9},{9,8},{10,11... | collective-permute-start | bytes 196616 | tf_op jit(solution)/shard_map/ppermute | solution.py:34

commit v9 on v8

--- a/solution.py
+++ b/solution.py
@@ -34,12 +34,21 @@
     return lax.ppermute(value, ("tm", "rows"), pairs)
 
 
-def by_parity(value, odd):
+def odd_ahead(value):
     tm = lax.axis_size("tm")
-    pairs = [(t, t + 2) for t in range(odd, tm - 2, 2)]
-    if odd:
-        pairs += [(t, t) for t in range(0, tm, 2)]
+    pairs = [(t, t + 2) for t in range(1, tm - 2, 2)] + [(t, t) for t in range(0, tm, 2)]
     return lax.ppermute(value, "tm", pairs)
+
+
+def even_ahead(value):
+    tm, rows = lax.axis_size("tm"), lax.axis_size("rows")
+    pairs = [(t, r, t + 2, r) for t in range(0, tm - 2, 2) for r in range(rows)]
+    if tm % 4 == 0 and rows % 2 == 0:
+        for r in range(rows):
+            pairs += [(tm - 2, r, tm - 1, r), (3, r, 0, r)]
+            pairs += [(t, r, t - 4, r) for t in range(7, tm, 4)]
+            pairs += [(t, r, t, r ^ 1) for t in range(1, tm, 4)]
+    return lax.ppermute(value, ("tm", "rows"), [(t * rows + r, u * rows + q) for t, r, u, q in pairs])
 
 
 def paired(value):
@@ -411,8 +420,8 @@
     sums = jax.ShapeDtypeStruct((half_rows * half_cols, wide), F32)
     pairs = jax.ShapeDtypeStruct((sides, 2 * half_cols, wide), F32)
     flops = 2 * half_rows * half_cols * 9 * wide * wide
-    odd_field = by_parity(field, 1)
-    even_field = by_parity(field, 0)
+    odd_field = odd_ahead(field)
+    even_field = even_ahead(field)
     body, ends = call(coarse_first_kernel, (sums, pairs), [], flops, (field, conv_coarse))
     odd_field, body, ends = lax.optimization_barrier((odd_field, body, ends))
     field_1 = paired(odd_field) if times % 2 == 0 else ring(field, 1)

time: 30.7 us -> 28.8 us (0.938)
  starting transfers between devices: 12.3 us -> 10.5 us
    ppermute x2, starting transfers between devices: 3.22 us -> 1.32 us  [the longest x1 0.67 us: odd_ahead(): return lax.ppermute(value, 'tm', pairs)]
    ppermute x1, waiting for transfers between devices: 0.01 us -> 0.38 us  [paired(): lax.ppermute(value, 'tm', [(t, t ^ 1) for t in range(lax.axis_size('tm'))])]
    ppermute x2, waiting for transfers between devices: 4.94 us -> 4.6 us  [the longest x1 4.6 us: even_ahead(): lax.ppermute(value, ('tm', 'rows'), [(t * rows + r, u * rows + q) for t,...]
  transfers between devices with their start and end apart: 7 -> 7, of which waited for: 4 -> 5; matrix products, arithmetic and copies ran while one was open for 0% -> 0% of each run, Pallas kernels for 17% -> 18%
where the time goes in v9:
time: 28.8 us; the launch traced here: 28.6 us
  starting transfers between devices  10.5 us (36%)
  waiting for transfers between devices  10 us (35%)
  Pallas kernels  7 us (24%)
  local copies, waits for them, and re-layouts  1.04 us (4%)
    pallas_call x11, Pallas kernels, call(): pl.pallas_call(kernel, out_shape=out_shape, in_specs=[vmem] * (len(args)...  7 us
    ppermute x3, starting transfers between devices, swapped(): return lax.ppermute(value, ('tm', 'rows'), pairs)  5.48 us
    ppermute x1, waiting for transfers between devices, even_ahead(): lax.ppermute(value, ('tm', 'rows'), [(t * rows + r, u * rows + q) for t,...  4.6 us
    ppermute x1, starting transfers between devices, paired(): lax.ppermute(value, 'tm', [(t, t ^ 1) for t in range(lax.axis_size('tm'))])  3.66 us
    ppermute x1, waiting for transfers between devices, ring(): return lax.ppermute(value, 'tm', [(t, (t + steps) % tm) for t in range(tm)])  3.1 us
    ppermute x3, waiting for transfers between devices, swapped(): return lax.ppermute(value, ('tm', 'rows'), pairs)  1.92 us
    unnamed x8, local copies, waits for them, and re-layouts  1.04 us
    ppermute x1, starting transfers between devices, odd_ahead(): return lax.ppermute(value, 'tm', pairs)  0.67 us
  transfers between devices with their start and end apart: 7, of which 5 were waited for; matrix products, arithmetic and copies ran while one was open for 0% of the time, Pallas kernels for 18%

profile of v9, /device:TPU:16, one launch (start us, length us, event | category | flops | bytes accessed | tf_op | source)
XLA Modules:
  0.0 28.6 jit_solution(6017756211626067183)
XLA Ops:
  0.0 0.0 copy-start.3
  0.0 0.0 copy-start.1
  0.0 0.0 collective-permute-start.1
  0.0 1.0 %copy-done.3 = bf16[2,8,128,128]{3,2,1,0:T(8,128)(2,1)S(1)} copy-done((bf16[2,8,128,128]{3,2,1,0:T(8,128)(2,1)S(1)}, bf16[2,8,128,128]{3,2,1,0:T(8,128)(2,1)}, u32[]{:S(2)}) %copy-start.3) | copy-done | bytes 524312
  1.0 1.5 %collective-permute-start.2 = (bf16[2,1,128,128]{3,2,1,0:T(8,128)(2,1)S(1)}, bf16[2,1,128,128]{3,2,1,0:T(8,128)(2,1)S(1)}, u32[]{:S(2)}, u32[]{:S(2)}) collective-permute-start(bf16[2,1,128,128]{3,2,1,0:T(8,128)(2,1)S(1)} %shard_map.47), channel_id=1, source_target_pairs={{0,1},{1,0},{2,3},{3,2},{4,5},{5,4},{6,7},{7,6},{8,9},{9,8},{10,11... | collective-permute-start | bytes 196616 | tf_op jit(solution)/shard_map/ppermute | solution.py:34
  2.6 2.4 %collective-permute-start = (bf16[2,1,128,128]{3,2,1,0:T(8,128)(2,1)S(1)}, bf16[2,1,128,128]{3,2,1,0:T(8,128)(2,1)S(1)}, u32[]{:S(2)}, u32[]{:S(2)}) collective-permute-start(bf16[2,1,128,128]{3,2,1,0:T(8,128)(2,1)S(1)} %shard_map.47), channel_id=1, source_target_pairs={{0,3},{1,2},{2,5},{3,4},{4,7},{5,6},{6,9},{7,8},{8,11},{9,10},{10,... | collective-permute-start | bytes 196616 | tf_op jit(solution)/shard_map/ppermute | solution.py:34
  4.9 0.0 copy-done.1
  5.0 1.4 %shard_map.48.own = f32[1024,256]{1,0:T(8,128)S(1)} custom-call(bf16[2,8,128,128]{3,2,1,0:T(8,128)(2,1)S(1)} %copy-done.3, bf16[3,3,384,128]{3,2,1,0:T(8,128)(2,1)S(1)} %copy-done.1), custom_call_target="tpu_custom_call" | custom-call | flops 1207959552 | bytes 1409024 | tf_op jit(solution)/shard_map/pallas_call | solution.py:377
  6.4 0.0 copy-start.2
  6.4 0.0 collective-permute-done.2.above.below
  6.4 0.2 shard_map.49.halo
  6.6 0.0 copy-start
  6.6 3.1 %collective-permute-done.1.frames = bf16[2,8,128,128]{3,2,1,0:T(8,128)(2,1)S(1)} collective-permute-done((bf16[2,8,128,128]{3,2,1,0:T(8,128)(2,1)}, bf16[2,8,128,128]{3,2,1,0:T(8,128)(2,1)S(1)}, u32[]{:S(2)}, u32[]{:S(2)}) %collective-permute-start.1) | collective-permute-done | bytes 524320 | tf_op jit(solution)/shard_map/ppermute | solution.py:28
  9.7 1.3 %shard_map.50.sums = f32[1024,256]{1,0:T(8,128)S(1)} custom-call(bf16[2,8,128,128]{3,2,1,0:T(8,128)(2,1)S(1)} %collective-permute-done.1.frames, bf16[3,3,384,128]{3,2,1,0:T(8,128)(2,1)S(1)} %copy-done.1, f32[1024,256]{1,0:T(8,128)S(1)} %shard_map.48.own, f32[2,128,256]{2,1,0:T(8,128)S(1)} %shard_map.49.halo), custom_call_target="tpu_custom_call" | custom-call | flops 1207959552 | bytes 2719744 | tf_op jit(solution)/shard_map/pallas_call | solution.py:377
  11.0 0.4 %collective-permute-done.above.below = bf16[2,1,128,128]{3,2,1,0:T(8,128)(2,1)S(1)} collective-permute-done((bf16[2,1,128,128]{3,2,1,0:T(8,128)(2,1)S(1)}, bf16[2,1,128,128]{3,2,1,0:T(8,128)(2,1)S(1)}, u32[]{:S(2)}, u32[]{:S(2)}) %collective-permute-start) | collective-permute-done | bytes 65568 | tf_op jit(solution)/shard_map/ppermute | solution.py:34
  11.4 0.0 copy-done.2
  11.4 0.8 %shard_map.51.field = bf16[1,5,64,256]{3,2,1,0:T(8,128)(2,1)S(1)} custom-call(bf16[2,1,128,128]{3,2,1,0:T(8,128)(2,1)S(1)} %collective-permute-done.above.below, bf16[2,1,128,128]{3,2,1,0:T(8,128)(2,1)S(1)} %collective-permute-done.above.below, bf16[3,3,384,128]{3,2,1,0:T(8,128)(2,1)S(1)} %copy-done.1, f32[1024,256]{1,0:T(8,128)S(1)} %shard_map.50.sums, ...), custom_call_target="tpu_custom_call" | custom-call | flops 402653184 | bytes 2654208 | tf_op jit(solution)/shard_map/pallas_call | solution.py:377
  12.2 0.7 %collective-permute-start.3 = (bf16[1,5,64,256]{3,2,1,0:T(8,128)(2,1)S(1)}, bf16[1,5,64,256]{3,2,1,0:T(8,128)(2,1)S(1)}, u32[]{:S(2)}, u32[]{:S(2)}) collective-permute-start(bf16[1,5,64,256]{3,2,1,0:T(8,128)(2,1)S(1)} %shard_map.51.field), channel_id=1, source_target_pairs={{2,6},{6,10},{10,14},{14,18},{18,22},{22,26},{26,30},{0,0},{4,4},{... | collective-permute-start | bytes 491528 | tf_op jit(solution)/shard_map/ppermute | solution.py:40
  12.8 0.0 copy-done
  12.9 0.6 %shard_map.52 = (f32[256,256]{1,0:T(8,128)S(1)}, f32[1,128,256]{2,1,0:T(8,128)S(1)}) custom-call(bf16[1,5,64,256]{3,2,1,0:T(8,128)(2,1)S(1)} %shard_map.51.field, bf16[3,3,768,256]{3,2,1,0:T(8,128)(2,1)S(1)} %copy-done), custom_call_target="tpu_custom_call" | custom-call | flops 301989888 | bytes 3702784 | tf_op jit(solution)/shard_map/pallas_call | solution.py:377
  13.5 0.0 collective-permute-done.3.odd_field
  13.5 3.7 %collective-permute-start.5 = (bf16[1,5,64,256]{3,2,1,0:T(8,128)(2,1)S(1)}, bf16[1,5,64,256]{3,2,1,0:T(8,128)(2,1)S(1)}, u32[]{:S(2)}, u32[]{:S(2)}) collective-permute-start(bf16[1,5,64,256]{3,2,1,0:T(8,128)(2,1)S(1)} %collective-permute-done.3.odd_field), channel_id=1, source_target_pairs={{0,2},{2,0},{4,6},{6,4},{8,10},{10,8},{12,14},{14,12},{16,18},{18,... | collective-permute-start | bytes 491528 | tf_op jit(solution)/shard_map/ppermute | solution.py:55
  17.1 0.6 %collective-permute-start.4 = (bf16[1,5,64,256]{3,2,1,0:T(8,128)(2,1)S(1)}, bf16[1,5,64,256]{3,2,1,0:T(8,128)(2,1)S(1)}, u32[]{:S(2)}, u32[]{:S(2)}) collective-permute-start(bf16[1,5,64,256]{3,2,1,0:T(8,128)(2,1)S(1)} %shard_map.51.field), channel_id=1, source_target_pairs={{0,4},{1,5},{4,8},{5,9},{8,12},{9,13},{12,16},{13,17},{16,20},{17,... | collective-permute-start | bytes 491528 | tf_op jit(solution)/shard_map/ppermute | solution.py:51
  17.8 0.4 %collective-permute-done.5.field = bf16[1,5,64,256]{3,2,1,0:T(8,128)(2,1)S(1)} collective-permute-done((bf16[1,5,64,256]{3,2,1,0:T(8,128)(2,1)S(1)}, bf16[1,5,64,256]{3,2,1,0:T(8,128)(2,1)S(1)}, u32[]{:S(2)}, u32[]{:S(2)}) %collective-permute-start.5) | collective-permute-done | bytes 163872 | tf_op jit(solution)/shard_map/ppermute | solution.py:55
  18.2 0.6 %shard_map.53 = (f32[256,256]{1,0:T(8,128)S(1)}, f32[1,128,256]{2,1,0:T(8,128)S(1)}) custom-call(bf16[1,5,64,256]{3,2,1,0:T(8,128)(2,1)S(1)} %collective-permute-done.5.field, bf16[3,3,768,256]{3,2,1,0:T(8,128)(2,1)S(1)} %copy-done, f32[256,256]{1,0:T(8,128)S(1)} %get-tuple-element.26.body_in, f32[1,128,256]{2,1,0:T(8,128)S(1)} %get-tuple-element.27.ends_in), custom_call_target="tpu_custom_call" | custom-call | flops 301989888 | bytes 4096000 | tf_op jit(solution)/shard_map/pallas_call | solution.py:377
  18.7 4.6 %collective-permute-done.4.even_field = bf16[1,5,64,256]{3,2,1,0:T(8,128)(2,1)S(1)} collective-permute-done((bf16[1,5,64,256]{3,2,1,0:T(8,128)(2,1)S(1)}, bf16[1,5,64,256]{3,2,1,0:T(8,128)(2,1)S(1)}, u32[]{:S(2)}, u32[]{:S(2)}) %collective-permute-start.4) | collective-permute-done | bytes 163872 | tf_op jit(solution)/shard_map/ppermute | solution.py:51
  23.3 0.3 shard_map.55
  23.6 1.6 %collective-permute-start.6 = (bf16[1,128,256]{2,1,0:T(8,128)(2,1)S(1)}, bf16[1,128,256]{2,1,0:T(8,128)(2,1)S(1)}, u32[]{:S(2)}, u32[]{:S(2)}) collective-permute-start(bf16[1,128,256]{2,1,0:T(8,128)(2,1)S(1)} %shard_map.55), channel_id=1, source_target_pairs={{0,1},{1,0},{2,3},{3,2},{4,5},{5,4},{6,7},{7,6},{8,9},{9,8},{10,11... | collective-permute-start | bytes 196616 | tf_op jit(solution)/shard_map/ppermute | solution.py:34
  25.2 1.2 %shard_map.54 = (bf16[1,4,64,256]{3,2,1,0:T(8,128)(2,1)}, f32[1,128,256]{2,1,0:T(8,128)S(1)}) custom-call(bf16[1,5,64,256]{3,2,1,0:T(8,128)(2,1)S(1)} %collective-permute-done.3.odd_field, bf16[1,5,64,256]{3,2,1,0:T(8,128)(2,1)S(1)} %collective-permute-done.4.even_field, bf16[3,3,768,256]{3,2,1,0:T(8,128)(2,1)S(1)} %copy-done, ...), custom_call_target="tpu_custom_call" | custom-call | flops 301989888 | bytes 4128768 | tf_op jit(solution)/shard_map/pallas_call | solution.py:377
  26.4 1.6 %collective-permute-done.6.added = bf16[1,128,256]{2,1,0:T(8,128)(2,1)S(1)} collective-permute-done((bf16[1,128,256]{2,1,0:T(8,128)(2,1)S(1)}, bf16[1,128,256]{2,1,0:T(8,128)(2,1)S(1)}, u32[]{:S(2)}, u32[]{:S(2)}) %collective-permute-start.6) | collective-permute-done | bytes 65568 | tf_op jit(solution)/shard_map/ppermute | solution.py:34
  27.9 0.7 %shard_map.56 = bf16[1,4,64,256]{3,2,1,0:T(8,128)(2,1)} custom-call(f32[1,128,256]{2,1,0:T(8,128)S(1)} %get-tuple-element.32.ends, bf16[1,128,256]{2,1,0:T(8,128)(2,1)S(1)} %collective-permute-done.6.added, bf16[1,4,64,256]{3,2,1,0:T(8,128)(2,1)} %get-tuple-element.34._), custom_call_target="tpu_custom_call", output_to_operand_aliasing={{}: (2, {})} | custom-call | flops 18874368 | bytes 327680 | tf_op jit(solution)/shard_map/pallas_call | solution.py:377
  (2 shorter events, 0.0 us)
Async XLA Ops:
  0.0 1.0 %copy-start.3 = (bf16[2,8,128,128]{3,2,1,0:T(8,128)(2,1)S(1)}, bf16[2,8,128,128]{3,2,1,0:T(8,128)(2,1)}, u32[]{:S(2)}) copy-start(bf16[2,8,128,128]{3,2,1,0:T(8,128)(2,1)} %frames.1) | copy-start | bytes 1572868
  0.0 4.9 %copy-start.1 = (bf16[3,3,384,128]{3,2,1,0:T(8,128)(2,1)S(1)}, bf16[3,3,384,128]{3,2,1,0:T(8,128)(2,1)}, u32[]{:S(2)}) copy-start(bf16[3,3,384,128]{3,2,1,0:T(8,128)(2,1)} %weight.11) | copy-start | bytes 2654212
  0.0 9.7 %collective-permute-start.1 = (bf16[2,8,128,128]{3,2,1,0:T(8,128)(2,1)}, bf16[2,8,128,128]{3,2,1,0:T(8,128)(2,1)S(1)}, u32[]{:S(2)}, u32[]{:S(2)}) collective-permute-start(bf16[2,8,128,128]{3,2,1,0:T(8,128)(2,1)} %frames.1), channel_id=1, source_target_pairs={{0,2},{2,4},{4,6},{6,8},{8,10},{10,12},{12,14},{14,16},{16,18},{18... | collective-permute-start | bytes 1572872 | tf_op jit(solution)/shard_map/ppermute | solution.py:28
  1.0 5.3 %collective-permute-start.2 = (bf16[2,1,128,128]{3,2,1,0:T(8,128)(2,1)S(1)}, bf16[2,1,128,128]{3,2,1,0:T(8,128)(2,1)S(1)}, u32[]{:S(2)}, u32[]{:S(2)}) collective-permute-start(bf16[2,1,128,128]{3,2,1,0:T(8,128)(2,1)S(1)} %shard_map.47), channel_id=1, source_target_pairs={{0,1},{1,0},{2,3},{3,2},{4,5},{5,4},{6,7},{7,6},{8,9},{9,8},{10,11... | collective-permute-start | bytes 196616 | tf_op jit(solution)/shard_map/ppermute | solution.py:34
  2.6 8.8 %collective-permute-start = (bf16[2,1,128,128]{3,2,1,0:T(8,128)(2,1)S(1)}, bf16[2,1,128,128]{3,2,1,0:T(8,128)(2,1)S(1)}, u32[]{:S(2)}, u32[]{:S(2)}) collective-permute-start(bf16[2,1,128,128]{3,2,1,0:T(8,128)(2,1)S(1)} %shard_map.47), channel_id=1, source_target_pairs={{0,3},{1,2},{2,5},{3,4},{4,7},{5,6},{6,9},{7,8},{8,11},{9,10},{10,... | collective-permute-start | bytes 196616 | tf_op jit(solution)/shard_map/ppermute | solution.py:34
  6.4 5.0 %copy-start.2 = (bf16[3,384,256]{2,1,0:T(8,128)(2,1)S(1)}, bf16[3,384,256]{2,1,0:T(8,128)(2,1)}, u32[]{:S(2)}) copy-start(bf16[3,384,256]{2,1,0:T(8,128)(2,1)} %down.1) | copy-start | bytes 1769476
  6.6 6.2 %copy-start = (bf16[3,3,768,256]{3,2,1,0:T(8,128)(2,1)S(1)}, bf16[3,3,768,256]{3,2,1,0:T(8,128)(2,1)}, u32[]{:S(2)}) copy-start(bf16[3,3,768,256]{3,2,1,0:T(8,128)(2,1)} %weight.15) | copy-start | bytes 10616836
  12.2 1.3 %collective-permute-start.3 = (bf16[1,5,64,256]{3,2,1,0:T(8,128)(2,1)S(1)}, bf16[1,5,64,256]{3,2,1,0:T(8,128)(2,1)S(1)}, u32[]{:S(2)}, u32[]{:S(2)}) collective-permute-start(bf16[1,5,64,256]{3,2,1,0:T(8,128)(2,1)S(1)} %shard_map.51.field), channel_id=1, source_target_pairs={{2,6},{6,10},{10,14},{14,18},{18,22},{22,26},{26,30},{0,0},{4,4},{... | collective-permute-start | bytes 491528 | tf_op jit(solution)/shard_map/ppermute | solution.py:40
  13.5 4.7 %collective-permute-start.5 = (bf16[1,5,64,256]{3,2,1,0:T(8,128)(2,1)S(1)}, bf16[1,5,64,256]{3,2,1,0:T(8,128)(2,1)S(1)}, u32[]{:S(2)}, u32[]{:S(2)}) collective-permute-start(bf16[1,5,64,256]{3,2,1,0:T(8,128)(2,1)S(1)} %collective-permute-done.3.odd_field), channel_id=1, source_target_pairs={{0,2},{2,0},{4,6},{6,4},{8,10},{10,8},{12,14},{14,12},{16,18},{18,... | collective-permute-start | bytes 491528 | tf_op jit(solution)/shard_map/ppermute | solution.py:55
  17.1 6.2 %collective-permute-start.4 = (bf16[1,5,64,256]{3,2,1,0:T(8,128)(2,1)S(1)}, bf16[1,5,64,256]{3,2,1,0:T(8,128)(2,1)S(1)}, u32[]{:S(2)}, u32[]{:S(2)}) collective-permute-start(bf16[1,5,64,256]{3,2,1,0:T(8,128)(2,1)S(1)} %shard_map.51.field), channel_id=1, source_target_pairs={{0,4},{1,5},{4,8},{5,9},{8,12},{9,13},{12,16},{13,17},{16,20},{17,... | collective-permute-start | bytes 491528 | tf_op jit(solution)/shard_map/ppermute | solution.py:51
  23.6 4.3 %collective-permute-start.6 = (bf16[1,128,256]{2,1,0:T(8,128)(2,1)S(1)}, bf16[1,128,256]{2,1,0:T(8,128)(2,1)S(1)}, u32[]{:S(2)}, u32[]{:S(2)}) collective-permute-start(bf16[1,128,256]{2,1,0:T(8,128)(2,1)S(1)} %shard_map.55), channel_id=1, source_target_pairs={{0,1},{1,0},{2,3},{3,2},{4,5},{5,4},{6,7},{7,6},{8,9},{9,8},{10,11... | collective-permute-start | bytes 196616 | tf_op jit(solution)/shard_map/ppermute | solution.py:34

commit v10 on v9

--- a/solution.py
+++ b/solution.py
@@ -45,9 +45,9 @@
     pairs = [(t, r, t + 2, r) for t in range(0, tm - 2, 2) for r in range(rows)]
     if tm % 4 == 0 and rows % 2 == 0:
         for r in range(rows):
-            pairs += [(tm - 2, r, tm - 1, r), (3, r, 0, r)]
-            pairs += [(t, r, t - 4, r) for t in range(7, tm, 4)]
-            pairs += [(t, r, t, r ^ 1) for t in range(1, tm, 4)]
+            pairs += [(tm - 2, r, tm - 1, r), (tm - 1, r, tm - 3, r), (1, r, 0, r)]
+            pairs += [(t, r, t - 4, r) for t in range(5, tm, 4)]
+            pairs += [(t, r, t, r ^ 1) for t in range(3, tm - 1, 4)]
     return lax.ppermute(value, ("tm", "rows"), [(t * rows + r, u * rows + q) for t, r, u, q in pairs])
 
 

time: 28.8 us -> 28.8 us (level)
  no operation moved by 1% of the time
where the time goes in v10:
time: 28.8 us; the launch traced here: 28.6 us
  starting transfers between devices  10.5 us (36%)
  waiting for transfers between devices  10 us (35%)
  Pallas kernels  7 us (24%)
  local copies, waits for them, and re-layouts  1.04 us (4%)
    pallas_call x11, Pallas kernels, call(): pl.pallas_call(kernel, out_shape=out_shape, in_specs=[vmem] * (len(args)...  7 us
    ppermute x3, starting transfers between devices, swapped(): return lax.ppermute(value, ('tm', 'rows'), pairs)  5.48 us
    ppermute x1, waiting for transfers between devices, even_ahead(): lax.ppermute(value, ('tm', 'rows'), [(t * rows + r, u * rows + q) for t,...  4.6 us
    ppermute x1, starting transfers between devices, paired(): lax.ppermute(value, 'tm', [(t, t ^ 1) for t in range(lax.axis_size('tm'))])  3.66 us
    ppermute x1, waiting for transfers between devices, ring(): return lax.ppermute(value, 'tm', [(t, (t + steps) % tm) for t in range(tm)])  3.1 us
    ppermute x3, waiting for transfers between devices, swapped(): return lax.ppermute(value, ('tm', 'rows'), pairs)  1.92 us
    unnamed x8, local copies, waits for them, and re-layouts  1.04 us
    ppermute x1, starting transfers between devices, odd_ahead(): return lax.ppermute(value, 'tm', pairs)  0.67 us
  transfers between devices with their start and end apart: 7, of which 5 were waited for; matrix products, arithmetic and copies ran while one was open for 0% of the time, Pallas kernels for 18%

profile of v10, /device:TPU:16, one launch (start us, length us, event | category | flops | bytes accessed | tf_op | source)
XLA Modules:
  0.0 28.6 jit_solution(13540218497211269834)
XLA Ops:
  0.0 0.0 copy-start.3
  0.0 0.0 copy-start.1
  0.0 0.0 collective-permute-start.1
  0.0 1.0 %copy-done.3 = bf16[2,8,128,128]{3,2,1,0:T(8,128)(2,1)S(1)} copy-done((bf16[2,8,128,128]{3,2,1,0:T(8,128)(2,1)S(1)}, bf16[2,8,128,128]{3,2,1,0:T(8,128)(2,1)}, u32[]{:S(2)}) %copy-start.3) | copy-done | bytes 524312
  1.0 1.5 %collective-permute-start.2 = (bf16[2,1,128,128]{3,2,1,0:T(8,128)(2,1)S(1)}, bf16[2,1,128,128]{3,2,1,0:T(8,128)(2,1)S(1)}, u32[]{:S(2)}, u32[]{:S(2)}) collective-permute-start(bf16[2,1,128,128]{3,2,1,0:T(8,128)(2,1)S(1)} %shard_map.47), channel_id=1, source_target_pairs={{0,1},{1,0},{2,3},{3,2},{4,5},{5,4},{6,7},{7,6},{8,9},{9,8},{10,11... | collective-permute-start | bytes 196616 | tf_op jit(solution)/shard_map/ppermute | solution.py:34
  2.6 2.4 %collective-permute-start = (bf16[2,1,128,128]{3,2,1,0:T(8,128)(2,1)S(1)}, bf16[2,1,128,128]{3,2,1,0:T(8,128)(2,1)S(1)}, u32[]{:S(2)}, u32[]{:S(2)}) collective-permute-start(bf16[2,1,128,128]{3,2,1,0:T(8,128)(2,1)S(1)} %shard_map.47), channel_id=1, source_target_pairs={{0,3},{1,2},{2,5},{3,4},{4,7},{5,6},{6,9},{7,8},{8,11},{9,10},{10,... | collective-permute-start | bytes 196616 | tf_op jit(solution)/shard_map/ppermute | solution.py:34
  4.9 0.0 copy-done.1
  5.0 1.4 %shard_map.48.own = f32[1024,256]{1,0:T(8,128)S(1)} custom-call(bf16[2,8,128,128]{3,2,1,0:T(8,128)(2,1)S(1)} %copy-done.3, bf16[3,3,384,128]{3,2,1,0:T(8,128)(2,1)S(1)} %copy-done.1), custom_call_target="tpu_custom_call" | custom-call | flops 1207959552 | bytes 1409024 | tf_op jit(solution)/shard_map/pallas_call | solution.py:377
  6.4 0.0 copy-start.2
  6.4 0.0 collective-permute-done.2.above.below
  6.4 0.2 shard_map.49.halo
  6.6 0.0 copy-start
  6.6 3.1 %collective-permute-done.1.frames = bf16[2,8,128,128]{3,2,1,0:T(8,128)(2,1)S(1)} collective-permute-done((bf16[2,8,128,128]{3,2,1,0:T(8,128)(2,1)}, bf16[2,8,128,128]{3,2,1,0:T(8,128)(2,1)S(1)}, u32[]{:S(2)}, u32[]{:S(2)}) %collective-permute-start.1) | collective-permute-done | bytes 524320 | tf_op jit(solution)/shard_map/ppermute | solution.py:28
  9.7 1.3 %shard_map.50.sums = f32[1024,256]{1,0:T(8,128)S(1)} custom-call(bf16[2,8,128,128]{3,2,1,0:T(8,128)(2,1)S(1)} %collective-permute-done.1.frames, bf16[3,3,384,128]{3,2,1,0:T(8,128)(2,1)S(1)} %copy-done.1, f32[1024,256]{1,0:T(8,128)S(1)} %shard_map.48.own, f32[2,128,256]{2,1,0:T(8,128)S(1)} %shard_map.49.halo), custom_call_target="tpu_custom_call" | custom-call | flops 1207959552 | bytes 2719744 | tf_op jit(solution)/shard_map/pallas_call | solution.py:377
  11.0 0.4 %collective-permute-done.above.below = bf16[2,1,128,128]{3,2,1,0:T(8,128)(2,1)S(1)} collective-permute-done((bf16[2,1,128,128]{3,2,1,0:T(8,128)(2,1)S(1)}, bf16[2,1,128,128]{3,2,1,0:T(8,128)(2,1)S(1)}, u32[]{:S(2)}, u32[]{:S(2)}) %collective-permute-start) | collective-permute-done | bytes 65568 | tf_op jit(solution)/shard_map/ppermute | solution.py:34
  11.4 0.0 copy-done.2
  11.4 0.8 %shard_map.51.field = bf16[1,5,64,256]{3,2,1,0:T(8,128)(2,1)S(1)} custom-call(bf16[2,1,128,128]{3,2,1,0:T(8,128)(2,1)S(1)} %collective-permute-done.above.below, bf16[2,1,128,128]{3,2,1,0:T(8,128)(2,1)S(1)} %collective-permute-done.above.below, bf16[3,3,384,128]{3,2,1,0:T(8,128)(2,1)S(1)} %copy-done.1, f32[1024,256]{1,0:T(8,128)S(1)} %shard_map.50.sums, ...), custom_call_target="tpu_custom_call" | custom-call | flops 402653184 | bytes 2654208 | tf_op jit(solution)/shard_map/pallas_call | solution.py:377
  12.2 0.7 %collective-permute-start.3 = (bf16[1,5,64,256]{3,2,1,0:T(8,128)(2,1)S(1)}, bf16[1,5,64,256]{3,2,1,0:T(8,128)(2,1)S(1)}, u32[]{:S(2)}, u32[]{:S(2)}) collective-permute-start(bf16[1,5,64,256]{3,2,1,0:T(8,128)(2,1)S(1)} %shard_map.51.field), channel_id=1, source_target_pairs={{2,6},{6,10},{10,14},{14,18},{18,22},{22,26},{26,30},{0,0},{4,4},{... | collective-permute-start | bytes 491528 | tf_op jit(solution)/shard_map/ppermute | solution.py:40
  12.8 0.0 copy-done
  12.9 0.6 %shard_map.52 = (f32[256,256]{1,0:T(8,128)S(1)}, f32[1,128,256]{2,1,0:T(8,128)S(1)}) custom-call(bf16[1,5,64,256]{3,2,1,0:T(8,128)(2,1)S(1)} %shard_map.51.field, bf16[3,3,768,256]{3,2,1,0:T(8,128)(2,1)S(1)} %copy-done), custom_call_target="tpu_custom_call" | custom-call | flops 301989888 | bytes 3702784 | tf_op jit(solution)/shard_map/pallas_call | solution.py:377
  13.5 0.0 collective-permute-done.3.odd_field
  13.5 3.7 %collective-permute-start.5 = (bf16[1,5,64,256]{3,2,1,0:T(8,128)(2,1)S(1)}, bf16[1,5,64,256]{3,2,1,0:T(8,128)(2,1)S(1)}, u32[]{:S(2)}, u32[]{:S(2)}) collective-permute-start(bf16[1,5,64,256]{3,2,1,0:T(8,128)(2,1)S(1)} %collective-permute-done.3.odd_field), channel_id=1, source_target_pairs={{0,2},{2,0},{4,6},{6,4},{8,10},{10,8},{12,14},{14,12},{16,18},{18,... | collective-permute-start | bytes 491528 | tf_op jit(solution)/shard_map/ppermute | solution.py:55
  17.1 0.6 %collective-permute-start.4 = (bf16[1,5,64,256]{3,2,1,0:T(8,128)(2,1)S(1)}, bf16[1,5,64,256]{3,2,1,0:T(8,128)(2,1)S(1)}, u32[]{:S(2)}, u32[]{:S(2)}) collective-permute-start(bf16[1,5,64,256]{3,2,1,0:T(8,128)(2,1)S(1)} %shard_map.51.field), channel_id=1, source_target_pairs={{0,4},{1,5},{4,8},{5,9},{8,12},{9,13},{12,16},{13,17},{16,20},{17,... | collective-permute-start | bytes 491528 | tf_op jit(solution)/shard_map/ppermute | solution.py:51
  17.8 0.4 %collective-permute-done.5.field = bf16[1,5,64,256]{3,2,1,0:T(8,128)(2,1)S(1)} collective-permute-done((bf16[1,5,64,256]{3,2,1,0:T(8,128)(2,1)S(1)}, bf16[1,5,64,256]{3,2,1,0:T(8,128)(2,1)S(1)}, u32[]{:S(2)}, u32[]{:S(2)}) %collective-permute-start.5) | collective-permute-done | bytes 163872 | tf_op jit(solution)/shard_map/ppermute | solution.py:55
  18.2 0.6 %shard_map.53 = (f32[256,256]{1,0:T(8,128)S(1)}, f32[1,128,256]{2,1,0:T(8,128)S(1)}) custom-call(bf16[1,5,64,256]{3,2,1,0:T(8,128)(2,1)S(1)} %collective-permute-done.5.field, bf16[3,3,768,256]{3,2,1,0:T(8,128)(2,1)S(1)} %copy-done, f32[256,256]{1,0:T(8,128)S(1)} %get-tuple-element.26.body_in, f32[1,128,256]{2,1,0:T(8,128)S(1)} %get-tuple-element.27.ends_in), custom_call_target="tpu_custom_call" | custom-call | flops 301989888 | bytes 4096000 | tf_op jit(solution)/shard_map/pallas_call | solution.py:377
  18.7 4.6 %collective-permute-done.4.even_field = bf16[1,5,64,256]{3,2,1,0:T(8,128)(2,1)S(1)} collective-permute-done((bf16[1,5,64,256]{3,2,1,0:T(8,128)(2,1)S(1)}, bf16[1,5,64,256]{3,2,1,0:T(8,128)(2,1)S(1)}, u32[]{:S(2)}, u32[]{:S(2)}) %collective-permute-start.4) | collective-permute-done | bytes 163872 | tf_op jit(solution)/shard_map/ppermute | solution.py:51
  23.3 0.3 shard_map.55
  23.6 1.6 %collective-permute-start.6 = (bf16[1,128,256]{2,1,0:T(8,128)(2,1)S(1)}, bf16[1,128,256]{2,1,0:T(8,128)(2,1)S(1)}, u32[]{:S(2)}, u32[]{:S(2)}) collective-permute-start(bf16[1,128,256]{2,1,0:T(8,128)(2,1)S(1)} %shard_map.55), channel_id=1, source_target_pairs={{0,1},{1,0},{2,3},{3,2},{4,5},{5,4},{6,7},{7,6},{8,9},{9,8},{10,11... | collective-permute-start | bytes 196616 | tf_op jit(solution)/shard_map/ppermute | solution.py:34
  25.2 1.2 %shard_map.54 = (bf16[1,4,64,256]{3,2,1,0:T(8,128)(2,1)}, f32[1,128,256]{2,1,0:T(8,128)S(1)}) custom-call(bf16[1,5,64,256]{3,2,1,0:T(8,128)(2,1)S(1)} %collective-permute-done.3.odd_field, bf16[1,5,64,256]{3,2,1,0:T(8,128)(2,1)S(1)} %collective-permute-done.4.even_field, bf16[3,3,768,256]{3,2,1,0:T(8,128)(2,1)S(1)} %copy-done, ...), custom_call_target="tpu_custom_call" | custom-call | flops 301989888 | bytes 4128768 | tf_op jit(solution)/shard_map/pallas_call | solution.py:377
  26.4 1.6 %collective-permute-done.6.added = bf16[1,128,256]{2,1,0:T(8,128)(2,1)S(1)} collective-permute-done((bf16[1,128,256]{2,1,0:T(8,128)(2,1)S(1)}, bf16[1,128,256]{2,1,0:T(8,128)(2,1)S(1)}, u32[]{:S(2)}, u32[]{:S(2)}) %collective-permute-start.6) | collective-permute-done | bytes 65568 | tf_op jit(solution)/shard_map/ppermute | solution.py:34
  27.9 0.7 %shard_map.56 = bf16[1,4,64,256]{3,2,1,0:T(8,128)(2,1)} custom-call(f32[1,128,256]{2,1,0:T(8,128)S(1)} %get-tuple-element.32.ends, bf16[1,128,256]{2,1,0:T(8,128)(2,1)S(1)} %collective-permute-done.6.added, bf16[1,4,64,256]{3,2,1,0:T(8,128)(2,1)} %get-tuple-element.34._), custom_call_target="tpu_custom_call", output_to_operand_aliasing={{}: (2, {})} | custom-call | flops 18874368 | bytes 327680 | tf_op jit(solution)/shard_map/pallas_call | solution.py:377
  (2 shorter events, 0.0 us)
Async XLA Ops:
  0.0 1.0 %copy-start.3 = (bf16[2,8,128,128]{3,2,1,0:T(8,128)(2,1)S(1)}, bf16[2,8,128,128]{3,2,1,0:T(8,128)(2,1)}, u32[]{:S(2)}) copy-start(bf16[2,8,128,128]{3,2,1,0:T(8,128)(2,1)} %frames.1) | copy-start | bytes 1572868
  0.0 4.9 %copy-start.1 = (bf16[3,3,384,128]{3,2,1,0:T(8,128)(2,1)S(1)}, bf16[3,3,384,128]{3,2,1,0:T(8,128)(2,1)}, u32[]{:S(2)}) copy-start(bf16[3,3,384,128]{3,2,1,0:T(8,128)(2,1)} %weight.11) | copy-start | bytes 2654212
  0.0 9.7 %collective-permute-start.1 = (bf16[2,8,128,128]{3,2,1,0:T(8,128)(2,1)}, bf16[2,8,128,128]{3,2,1,0:T(8,128)(2,1)S(1)}, u32[]{:S(2)}, u32[]{:S(2)}) collective-permute-start(bf16[2,8,128,128]{3,2,1,0:T(8,128)(2,1)} %frames.1), channel_id=1, source_target_pairs={{0,2},{2,4},{4,6},{6,8},{8,10},{10,12},{12,14},{14,16},{16,18},{18... | collective-permute-start | bytes 1572872 | tf_op jit(solution)/shard_map/ppermute | solution.py:28
  1.0 5.3 %collective-permute-start.2 = (bf16[2,1,128,128]{3,2,1,0:T(8,128)(2,1)S(1)}, bf16[2,1,128,128]{3,2,1,0:T(8,128)(2,1)S(1)}, u32[]{:S(2)}, u32[]{:S(2)}) collective-permute-start(bf16[2,1,128,128]{3,2,1,0:T(8,128)(2,1)S(1)} %shard_map.47), channel_id=1, source_target_pairs={{0,1},{1,0},{2,3},{3,2},{4,5},{5,4},{6,7},{7,6},{8,9},{9,8},{10,11... | collective-permute-start | bytes 196616 | tf_op jit(solution)/shard_map/ppermute | solution.py:34
  2.6 8.8 %collective-permute-start = (bf16[2,1,128,128]{3,2,1,0:T(8,128)(2,1)S(1)}, bf16[2,1,128,128]{3,2,1,0:T(8,128)(2,1)S(1)}, u32[]{:S(2)}, u32[]{:S(2)}) collective-permute-start(bf16[2,1,128,128]{3,2,1,0:T(8,128)(2,1)S(1)} %shard_map.47), channel_id=1, source_target_pairs={{0,3},{1,2},{2,5},{3,4},{4,7},{5,6},{6,9},{7,8},{8,11},{9,10},{10,... | collective-permute-start | bytes 196616 | tf_op jit(solution)/shard_map/ppermute | solution.py:34
  6.4 5.0 %copy-start.2 = (bf16[3,384,256]{2,1,0:T(8,128)(2,1)S(1)}, bf16[3,384,256]{2,1,0:T(8,128)(2,1)}, u32[]{:S(2)}) copy-start(bf16[3,384,256]{2,1,0:T(8,128)(2,1)} %down.1) | copy-start | bytes 1769476
  6.6 6.2 %copy-start = (bf16[3,3,768,256]{3,2,1,0:T(8,128)(2,1)S(1)}, bf16[3,3,768,256]{3,2,1,0:T(8,128)(2,1)}, u32[]{:S(2)}) copy-start(bf16[3,3,768,256]{3,2,1,0:T(8,128)(2,1)} %weight.15) | copy-start | bytes 10616836
  12.2 1.3 %collective-permute-start.3 = (bf16[1,5,64,256]{3,2,1,0:T(8,128)(2,1)S(1)}, bf16[1,5,64,256]{3,2,1,0:T(8,128)(2,1)S(1)}, u32[]{:S(2)}, u32[]{:S(2)}) collective-permute-start(bf16[1,5,64,256]{3,2,1,0:T(8,128)(2,1)S(1)} %shard_map.51.field), channel_id=1, source_target_pairs={{2,6},{6,10},{10,14},{14,18},{18,22},{22,26},{26,30},{0,0},{4,4},{... | collective-permute-start | bytes 491528 | tf_op jit(solution)/shard_map/ppermute | solution.py:40
  13.5 4.7 %collective-permute-start.5 = (bf16[1,5,64,256]{3,2,1,0:T(8,128)(2,1)S(1)}, bf16[1,5,64,256]{3,2,1,0:T(8,128)(2,1)S(1)}, u32[]{:S(2)}, u32[]{:S(2)}) collective-permute-start(bf16[1,5,64,256]{3,2,1,0:T(8,128)(2,1)S(1)} %collective-permute-done.3.odd_field), channel_id=1, source_target_pairs={{0,2},{2,0},{4,6},{6,4},{8,10},{10,8},{12,14},{14,12},{16,18},{18,... | collective-permute-start | bytes 491528 | tf_op jit(solution)/shard_map/ppermute | solution.py:55
  17.1 6.2 %collective-permute-start.4 = (bf16[1,5,64,256]{3,2,1,0:T(8,128)(2,1)S(1)}, bf16[1,5,64,256]{3,2,1,0:T(8,128)(2,1)S(1)}, u32[]{:S(2)}, u32[]{:S(2)}) collective-permute-start(bf16[1,5,64,256]{3,2,1,0:T(8,128)(2,1)S(1)} %shard_map.51.field), channel_id=1, source_target_pairs={{0,4},{1,5},{4,8},{5,9},{8,12},{9,13},{12,16},{13,17},{16,20},{17,... | collective-permute-start | bytes 491528 | tf_op jit(solution)/shard_map/ppermute | solution.py:51
  23.6 4.3 %collective-permute-start.6 = (bf16[1,128,256]{2,1,0:T(8,128)(2,1)S(1)}, bf16[1,128,256]{2,1,0:T(8,128)(2,1)S(1)}, u32[]{:S(2)}, u32[]{:S(2)}) collective-permute-start(bf16[1,128,256]{2,1,0:T(8,128)(2,1)S(1)} %shard_map.55), channel_id=1, source_target_pairs={{0,1},{1,0},{2,3},{3,2},{4,5},{5,4},{6,7},{7,6},{8,9},{9,8},{10,11... | collective-permute-start | bytes 196616 | tf_op jit(solution)/shard_map/ppermute | solution.py:34

commit v11 on v10

--- a/solution.py
+++ b/solution.py
@@ -82,13 +82,13 @@
     if lax.axis_size("rows") == 2:
         sent = call(
             edge_kernel,
-            jax.ShapeDtypeStruct((frames.shape[0], 1, *frames.shape[2:]), BF16),
+            jax.ShapeDtypeStruct((frames.shape[0], 2, *frames.shape[2:]), BF16),
             [],
             0,
             (pace, frames),
         )
         return [(both, both) for both in (swapped(sent, 0), swapped(sent, 1))]
-    head, tail = frames[:, :1], frames[:, rows - 1 :]
+    head, tail = frames[:, :2], frames[:, rows - 1 :]
     return [(moved(tail, steps, 1), moved(head, steps, -1)) for steps in (0, 1)]
 
 
@@ -193,32 +193,36 @@
     def row(f, i):
         return frames[f, i] if 0 <= i < rows else None
 
-    for outs in chunks_of(rows):
+    for outs in chunks_of(rows + 1):
         out[outs[0] * cols : (outs[-1] + 1) * cols] = fine_rows(row, outs, range(3), weight, 2)
 
 
-def halo_sums(above, below, weight, first_tap, rows):
-    if lax.axis_size("rows") == 2:
-        b = 2 * (1 - lax.axis_index("rows"))
-        added = fine_rows(lambda f, i: above[f, 0], [0], [b], weight, first_tap)
-        zero = jnp.zeros_like(added)
-        return jnp.where(has_above(), added, zero), jnp.where(has_above(), zero, added)
-
+def halo_row(above, below, rows):
     def row(f, i):
         if i == -1:
-            cells, have = above[f, 0], has_above()
+            cells, have = above[f, above.shape[1] - 1], has_above()
+        elif i >= rows:
+            cells, have = below[f, i - rows], has_below()
         else:
-            cells, have = below[f, 0], has_below()
+            return None
         return jnp.where(have, cells, jnp.zeros_like(cells))
 
-    return (
-        fine_rows(row, [0], [0], weight, first_tap),
-        fine_rows(row, [rows - 1], [2], weight, first_tap),
+    return row
+
+
+def halo_sum(above, below, weight, first_tap, rows):
+    row = halo_row(above, below, rows)
+    return jnp.concatenate(
+        [
+            fine_rows(row, [0], [0], weight, first_tap),
+            fine_rows(row, [rows - 1, rows], [1, 2], weight, first_tap),
+        ],
+        axis=0,
     )
 
 
 def fine_halo_kernel(above, below, weight, out, *, rows):
-    out[0], out[1] = halo_sums(above, below, weight, 2, rows)
+    out[...] = halo_sum(above, below, weight, 2, rows)
 
 
 def silu(v):
@@ -231,13 +235,13 @@
     def row(f, i):
         return frames[f, i] if 0 <= i < rows else None
 
-    for outs in chunks_of(rows):
+    for outs in chunks_of(rows + 1):
         total = jnp.where(has_earlier(1), previous_rows(row, outs, weight), 0.0)
         for i, r in enumerate(outs):
             line = total[i * cols : (i + 1) * cols] + own[r * cols : (r + 1) * cols]
-            for k, halo_r in enumerate((0, rows - 1)):
+            for k, halo_r in enumerate((0, rows - 1, rows)):
                 if r == halo_r:
-                    line = line + halo[k]
+                    line = line + halo[k * cols : (k + 1) * cols]
             out[r * cols : (r + 1) * cols] = line
 
 
@@ -266,24 +270,26 @@
 
 def reduce_kernel(above, below, weight, sums, down, out, pooled):
     cols = above.shape[2]
-    rows = sums.shape[0] // cols
+    rows = sums.shape[0] // cols - 1
     half_rows, half_cols = rows // 2, cols // 2
-    top, bottom = halo_sums(above, below, weight, 0, rows)
+    added = halo_sum(above, below, weight, 0, rows)
     lines = []
-    for r in range(rows):
+    for r in range(rows + 1):
         line = sums[r * cols : (r + 1) * cols]
-        if r == 0:
-            line = line + top
-        if r == rows - 1:
-            line = line + bottom
-        lines.append(pool(line))
-    put_pooled(pooled, [*lines, jnp.zeros_like(lines[0])])
-    dot = functools.partial(jnp.dot, preferred_element_type=F32)
+        for k, halo_r in enumerate((0, rows - 1, rows)):
+            if r == halo_r:
+                line = line + added[k * cols : (k + 1) * cols]
+        line = pool(line)
+        lines.append(jnp.where(has_below(), line, 0.0) if r == rows else line)
+    put_pooled(pooled, lines)
     taps = down_taps(pooled, half_cols)
     left = [jnp.concatenate(taps[2 * p : 2 * p + 3], axis=1) for p in range(half_rows)]
-    own = dot(jnp.concatenate(left, axis=0), down[...].reshape(-1, down.shape[-1]))
-    out[0, :half_rows] = own.astype(BF16).reshape(half_rows, half_cols, -1)
-    out[0, half_rows] = dot(taps[0], down[2]).astype(BF16)
+    own = jnp.dot(
+        jnp.concatenate(left, axis=0),
+        down[...].reshape(-1, down.shape[-1]),
+        preferred_element_type=F32,
+    )
+    out[0] = own.astype(BF16).reshape(half_rows, half_cols, -1)
 
 
 def column_taps(flat, cols):
@@ -292,28 +298,16 @@
 
 
 def coarse_sums(field, weight, a, sides):
-    _, count, cols, channels = field.shape
-    rows = count - 1
-    taps = column_taps(field.reshape(count * cols, channels), cols)
-    body, more = taps[: rows * cols], taps[rows * cols :]
-    zero = jnp.zeros_like(more)
-    tall = jnp.concatenate([jnp.where(has_above(), more, zero), body, zero], axis=0)
+    _, rows, cols, channels = field.shape
+    body = column_taps(field.reshape(rows * cols, channels), cols)
+    zero = jnp.zeros_like(body[:cols])
+    tall = jnp.concatenate([zero, body, zero], axis=0)
     dot = functools.partial(jnp.dot, preferred_element_type=F32)
     total = sum(dot(tall[b * cols : (b + rows) * cols], weight[a, b]) for b in range(3))
     head, tail = body[:cols], body[(rows - 1) * cols :]
     if sides == 1:
-        up = has_above()
-        first = jnp.concatenate([jnp.where(up, more, tail), jnp.where(up, head, zero)], axis=0)
-        ends = [dot(first, weight[a, 2 * lax.axis_index("rows")])]
-        second = [dot(jnp.where(up, more, zero), weight[a, 1])]
-    else:
-        first = jnp.concatenate([tail, zero], axis=0), jnp.concatenate([more, head], axis=0)
-        ends = [dot(first[0], weight[a, 0]), dot(first[1], weight[a, 2])]
-        second = [jnp.zeros((cols, weight.shape[-1]), F32), dot(more, weight[a, 1])]
-    ends = [
-        jnp.concatenate([end[:cols], end[cols:] + add], axis=0) for end, add in zip(ends, second)
-    ]
-    return total, ends
+        return total, [dot(jnp.where(has_above(), head, tail), weight[a, 2 * lax.axis_index("rows")])]
+    return total, [dot(tail, weight[a, 0]), dot(head, weight[a, 2])]
 
 
 def coarse_first_kernel(field, weight, body, ends):
@@ -344,7 +338,7 @@
 
 
 def end_starts(rows, sides):
-    return [(rows - 2) * (1 - lax.axis_index("rows"))] if sides == 1 else [0, rows - 2]
+    return [(rows - 1) * (1 - lax.axis_index("rows"))] if sides == 1 else [0, rows - 1]
 
 
 def coarse_body_kernel(odd_field, even_field, weight, body, out, ends, sums):
@@ -353,7 +347,7 @@
     sums[...] = body[...] + total
     out[...] = silu(sums[...]).astype(BF16).reshape(out.shape)
     for side, start in enumerate(end_starts(rows, ends.shape[0])):
-        ends[side] = sums[pl.ds(pl.multiple_of(start * cols, cols), 2 * cols), :]
+        ends[side] = sums[pl.ds(pl.multiple_of(start * cols, cols), cols), :]
 
 
 def finish_kernel(ends, added, _, out, lines, sem):
@@ -361,9 +355,9 @@
     copies = []
     for side, start in enumerate(end_starts(rows, ends.shape[0])):
         total = ends[side] + added[side].astype(F32)
-        lines[side] = silu(total).astype(BF16).reshape(lines.shape[1:])
+        lines[side] = silu(total).astype(BF16)
         copies.append(
-            pltpu.make_async_copy(lines.at[side], out.at[0, pl.ds(start, 2)], sem.at[side])
+            pltpu.make_async_copy(lines.at[side], out.at[0, start], sem.at[side])
         )
         copies[-1].start()
     for copy in copies:
@@ -394,13 +388,13 @@
 
     earlier = ring(frames, 1)
     (above, below), (above_1, below_1) = frame_rims(pace, frames)
-    size = rows * cols
+    size = (rows + 1) * cols
     pair = jax.ShapeDtypeStruct((size, 2 * channels), F32)
     flops = 2 * size * 18 * channels * 2 * channels
     own = call(fine_own_kernel, pair, [], flops, (frames, conv_fine))
     halo = call(
         functools.partial(fine_halo_kernel, rows=rows),
-        jax.ShapeDtypeStruct((2, cols, 2 * channels), F32),
+        jax.ShapeDtypeStruct((3 * cols, 2 * channels), F32),
         [],
         flops // 3,
         (above, below, conv_fine),
@@ -411,14 +405,14 @@
     above_1, below_1, fine_sums = lax.optimization_barrier((above_1, below_1, fine_sums))
     field = call(
         reduce_kernel,
-        jax.ShapeDtypeStruct((1, half_rows + 1, half_cols, wide), BF16),
+        shape,
         [pltpu.VMEM((rows + 1, cols + 8, channels), F32)],
         flops // 3,
         (above_1, below_1, conv_fine, fine_sums, conv_down),
     )
     sides = 1 if strips == 2 else 2
     sums = jax.ShapeDtypeStruct((half_rows * half_cols, wide), F32)
-    pairs = jax.ShapeDtypeStruct((sides, 2 * half_cols, wide), F32)
+    pairs = jax.ShapeDtypeStruct((sides, half_cols, wide), F32)
     flops = 2 * half_rows * half_cols * 9 * wide * wide
     odd_field = odd_ahead(field)
     even_field = even_ahead(field)
@@ -450,7 +444,7 @@
     return call(
         finish_kernel,
         shape,
-        [pltpu.VMEM((sides, 2, half_cols, wide), BF16), pltpu.SemaphoreType.DMA((sides,))],
+        [pltpu.VMEM((sides, half_cols, wide), BF16), pltpu.SemaphoreType.DMA((sides,))],
         flops // 16,
         (end_sums, added, out),
         in_place=True,

time: 28.8 us -> 28.2 us (0.979)
  starting transfers between devices: 10.5 us -> 9.68 us
  Pallas kernels: 7 us -> 7.53 us
  waiting for transfers between devices: 10 us -> 9.62 us
    ppermute x1, waiting for transfers between devices: 3.1 us -> 2.17 us  [ring(): return lax.ppermute(value, 'tm', [(t, (t + steps) % tm) for t in range(tm)])]
    ppermute x3, waiting for transfers between devices: 1.92 us -> 2.76 us  [swapped(): return lax.ppermute(value, ('tm', 'rows'), pairs)]
    ppermute x1, starting transfers between devices: 3.66 us -> 2.88 us  [paired(): lax.ppermute(value, 'tm', [(t, t ^ 1) for t in range(lax.axis_size('tm'))])]
    pallas_call x11, Pallas kernels: 7 us -> 7.53 us  [call(): pl.pallas_call(kernel, out_shape=out_shape, in_specs=[vmem] * (len(args)...]
  transfers between devices with their start and end apart: 7 -> 7, of which waited for: 5 -> 6; matrix products, arithmetic and copies ran while one was open for 0% -> 0% of each run, Pallas kernels for 18% -> 20%
where the time goes in v11:
time: 28.2 us; the launch traced here: 28 us
  starting transfers between devices  9.68 us (34%)
  waiting for transfers between devices  9.62 us (34%)
  Pallas kernels  7.53 us (27%)
  local copies, waits for them, and re-layouts  1.03 us (4%)
    pallas_call x11, Pallas kernels, call(): pl.pallas_call(kernel, out_shape=out_shape, in_specs=[vmem] * (len(args)...  7.53 us
    ppermute x3, starting transfers between devices, swapped(): return lax.ppermute(value, ('tm', 'rows'), pairs)  5.48 us
    ppermute x1, waiting for transfers between devices, even_ahead(): lax.ppermute(value, ('tm', 'rows'), [(t * rows + r, u * rows + q) for t,...  4.35 us
    ppermute x1, starting transfers between devices, paired(): lax.ppermute(value, 'tm', [(t, t ^ 1) for t in range(lax.axis_size('tm'))])  2.88 us
    ppermute x3, waiting for transfers between devices, swapped(): return lax.ppermute(value, ('tm', 'rows'), pairs)  2.76 us
    ppermute x1, waiting for transfers between devices, ring(): return lax.ppermute(value, 'tm', [(t, (t + steps) % tm) for t in range(tm)])  2.17 us
    unnamed x8, local copies, waits for them, and re-layouts  1.03 us
    ppermute x1, starting transfers between devices, odd_ahead(): return lax.ppermute(value, 'tm', pairs)  0.67 us
  transfers between devices with their start and end apart: 7, of which 6 were waited for; matrix products, arithmetic and copies ran while one was open for 0% of the time, Pallas kernels for 20%

profile of v11, /device:TPU:16, one launch (start us, length us, event | category | flops | bytes accessed | tf_op | source)
XLA Modules:
  0.0 28.0 jit_solution(10347758427677723178)
XLA Ops:
  0.0 0.0 copy-start.3
  0.0 0.0 copy-start.1
  0.0 0.0 collective-permute-start.1
  0.0 1.0 %copy-done.3 = bf16[2,8,128,128]{3,2,1,0:T(8,128)(2,1)S(1)} copy-done((bf16[2,8,128,128]{3,2,1,0:T(8,128)(2,1)S(1)}, bf16[2,8,128,128]{3,2,1,0:T(8,128)(2,1)}, u32[]{:S(2)}) %copy-start.3) | copy-done | bytes 524312
  1.1 1.6 %collective-permute-start.2 = (bf16[2,2,128,128]{3,2,1,0:T(8,128)(2,1)S(1)}, bf16[2,2,128,128]{3,2,1,0:T(8,128)(2,1)S(1)}, u32[]{:S(2)}, u32[]{:S(2)}) collective-permute-start(bf16[2,2,128,128]{3,2,1,0:T(8,128)(2,1)S(1)} %shard_map.47), channel_id=1, source_target_pairs={{0,1},{1,0},{2,3},{3,2},{4,5},{5,4},{6,7},{7,6},{8,9},{9,8},{10,11... | collective-permute-start | bytes 393224 | tf_op jit(solution)/shard_map/ppermute | solution.py:34
  2.6 2.3 %collective-permute-start = (bf16[2,2,128,128]{3,2,1,0:T(8,128)(2,1)S(1)}, bf16[2,2,128,128]{3,2,1,0:T(8,128)(2,1)S(1)}, u32[]{:S(2)}, u32[]{:S(2)}) collective-permute-start(bf16[2,2,128,128]{3,2,1,0:T(8,128)(2,1)S(1)} %shard_map.47), channel_id=1, source_target_pairs={{0,3},{1,2},{2,5},{3,4},{4,7},{5,6},{6,9},{7,8},{8,11},{9,10},{10,... | collective-permute-start | bytes 393224 | tf_op jit(solution)/shard_map/ppermute | solution.py:34
  5.0 0.0 copy-done.1
  5.0 1.5 %shard_map.48.own = f32[1152,256]{1,0:T(8,128)S(1)} custom-call(bf16[2,8,128,128]{3,2,1,0:T(8,128)(2,1)S(1)} %copy-done.3, bf16[3,3,384,128]{3,2,1,0:T(8,128)(2,1)S(1)} %copy-done.1), custom_call_target="tpu_custom_call" | custom-call | flops 1358954496 | bytes 1409024 | tf_op jit(solution)/shard_map/pallas_call | solution.py:371
  6.5 0.6 %collective-permute-done.2.above.below = bf16[2,2,128,128]{3,2,1,0:T(8,128)(2,1)S(1)} collective-permute-done((bf16[2,2,128,128]{3,2,1,0:T(8,128)(2,1)S(1)}, bf16[2,2,128,128]{3,2,1,0:T(8,128)(2,1)S(1)}, u32[]{:S(2)}, u32[]{:S(2)}) %collective-permute-start.2) | collective-permute-done | bytes 131104 | tf_op jit(solution)/shard_map/ppermute | solution.py:34
  7.1 0.4 %shard_map.49.halo = f32[384,256]{1,0:T(8,128)S(1)} custom-call(bf16[2,2,128,128]{3,2,1,0:T(8,128)(2,1)S(1)} %collective-permute-done.2.above.below, bf16[2,2,128,128]{3,2,1,0:T(8,128)(2,1)S(1)} %collective-permute-done.2.above.below, bf16[3,3,384,128]{3,2,1,0:T(8,128)(2,1)S(1)} %copy-done.1), custom_call_target="tpu_custom_call" | custom-call | flops 452984832 | bytes 1146880 | tf_op jit(solution)/shard_map/pallas_call | solution.py:371
  7.5 0.0 copy-start.2
  7.5 2.2 %collective-permute-done.1.frames = bf16[2,8,128,128]{3,2,1,0:T(8,128)(2,1)S(1)} collective-permute-done((bf16[2,8,128,128]{3,2,1,0:T(8,128)(2,1)}, bf16[2,8,128,128]{3,2,1,0:T(8,128)(2,1)S(1)}, u32[]{:S(2)}, u32[]{:S(2)}) %collective-permute-start.1) | collective-permute-done | bytes 524320 | tf_op jit(solution)/shard_map/ppermute | solution.py:28
  9.7 0.0 copy-start
  9.7 1.4 %shard_map.50.sums = f32[1152,256]{1,0:T(8,128)S(1)} custom-call(bf16[2,8,128,128]{3,2,1,0:T(8,128)(2,1)S(1)} %collective-permute-done.1.frames, bf16[3,3,384,128]{3,2,1,0:T(8,128)(2,1)S(1)} %copy-done.1, f32[1152,256]{1,0:T(8,128)S(1)} %shard_map.48.own, f32[384,256]{1,0:T(8,128)S(1)} %shard_map.49.halo), custom_call_target="tpu_custom_call" | custom-call | flops 1358954496 | bytes 2981888 | tf_op jit(solution)/shard_map/pallas_call | solution.py:371
  11.1 1.0 %collective-permute-done.above.below = bf16[2,2,128,128]{3,2,1,0:T(8,128)(2,1)S(1)} collective-permute-done((bf16[2,2,128,128]{3,2,1,0:T(8,128)(2,1)S(1)}, bf16[2,2,128,128]{3,2,1,0:T(8,128)(2,1)S(1)}, u32[]{:S(2)}, u32[]{:S(2)}) %collective-permute-start) | collective-permute-done | bytes 131104 | tf_op jit(solution)/shard_map/ppermute | solution.py:34
  12.1 0.0 copy-done.2
  12.1 1.1 %shard_map.51.field = bf16[1,4,64,256]{3,2,1,0:T(8,128)(2,1)S(1)} custom-call(bf16[2,2,128,128]{3,2,1,0:T(8,128)(2,1)S(1)} %collective-permute-done.above.below, bf16[2,2,128,128]{3,2,1,0:T(8,128)(2,1)S(1)} %collective-permute-done.above.below, bf16[3,3,384,128]{3,2,1,0:T(8,128)(2,1)S(1)} %copy-done.1, f32[1152,256]{1,0:T(8,128)S(1)} %shard_map.50.sums, ...), custom_call_target="tpu_custom_call" | custom-call | flops 452984832 | bytes 2916352 | tf_op jit(solution)/shard_map/pallas_call | solution.py:371
  13.2 0.7 %collective-permute-start.3 = (bf16[1,4,64,256]{3,2,1,0:T(8,128)(2,1)S(1)}, bf16[1,4,64,256]{3,2,1,0:T(8,128)(2,1)S(1)}, u32[]{:S(2)}, u32[]{:S(2)}) collective-permute-start(bf16[1,4,64,256]{3,2,1,0:T(8,128)(2,1)S(1)} %shard_map.51.field), channel_id=1, source_target_pairs={{2,6},{6,10},{10,14},{14,18},{18,22},{22,26},{26,30},{0,0},{4,4},{... | collective-permute-start | bytes 393224 | tf_op jit(solution)/shard_map/ppermute | solution.py:40
  13.9 0.0 copy-done
  13.9 0.5 %shard_map.52 = (f32[256,256]{1,0:T(8,128)S(1)}, f32[1,64,256]{2,1,0:T(8,128)S(1)}) custom-call(bf16[1,4,64,256]{3,2,1,0:T(8,128)(2,1)S(1)} %shard_map.51.field, bf16[3,3,768,256]{3,2,1,0:T(8,128)(2,1)S(1)} %copy-done), custom_call_target="tpu_custom_call" | custom-call | flops 301989888 | bytes 3670016 | tf_op jit(solution)/shard_map/pallas_call | solution.py:371
  14.4 0.0 collective-permute-done.3.odd_field
  14.4 2.9 %collective-permute-start.5 = (bf16[1,4,64,256]{3,2,1,0:T(8,128)(2,1)S(1)}, bf16[1,4,64,256]{3,2,1,0:T(8,128)(2,1)S(1)}, u32[]{:S(2)}, u32[]{:S(2)}) collective-permute-start(bf16[1,4,64,256]{3,2,1,0:T(8,128)(2,1)S(1)} %collective-permute-done.3.odd_field), channel_id=1, source_target_pairs={{0,2},{2,0},{4,6},{6,4},{8,10},{10,8},{12,14},{14,12},{16,18},{18,... | collective-permute-start | bytes 393224 | tf_op jit(solution)/shard_map/ppermute | solution.py:55
  17.3 0.6 %collective-permute-start.4 = (bf16[1,4,64,256]{3,2,1,0:T(8,128)(2,1)S(1)}, bf16[1,4,64,256]{3,2,1,0:T(8,128)(2,1)S(1)}, u32[]{:S(2)}, u32[]{:S(2)}) collective-permute-start(bf16[1,4,64,256]{3,2,1,0:T(8,128)(2,1)S(1)} %shard_map.51.field), channel_id=1, source_target_pairs={{0,4},{1,5},{4,8},{5,9},{8,12},{9,13},{12,16},{13,17},{16,20},{17,... | collective-permute-start | bytes 393224 | tf_op jit(solution)/shard_map/ppermute | solution.py:51
  17.9 0.3 %collective-permute-done.5.field = bf16[1,4,64,256]{3,2,1,0:T(8,128)(2,1)S(1)} collective-permute-done((bf16[1,4,64,256]{3,2,1,0:T(8,128)(2,1)S(1)}, bf16[1,4,64,256]{3,2,1,0:T(8,128)(2,1)S(1)}, u32[]{:S(2)}, u32[]{:S(2)}) %collective-permute-start.5) | collective-permute-done | bytes 131104 | tf_op jit(solution)/shard_map/ppermute | solution.py:55
  18.3 0.5 %shard_map.53 = (f32[256,256]{1,0:T(8,128)S(1)}, f32[1,64,256]{2,1,0:T(8,128)S(1)}) custom-call(bf16[1,4,64,256]{3,2,1,0:T(8,128)(2,1)S(1)} %collective-permute-done.5.field, bf16[3,3,768,256]{3,2,1,0:T(8,128)(2,1)S(1)} %copy-done, f32[256,256]{1,0:T(8,128)S(1)} %get-tuple-element.26.body_in, f32[1,64,256]{2,1,0:T(8,128)S(1)} %get-tuple-element.27.ends_in), custom_call_target="tpu_custom_call" | custom-call | flops 301989888 | bytes 3997696 | tf_op jit(solution)/shard_map/pallas_call | solution.py:371
  18.8 4.4 %collective-permute-done.4.even_field = bf16[1,4,64,256]{3,2,1,0:T(8,128)(2,1)S(1)} collective-permute-done((bf16[1,4,64,256]{3,2,1,0:T(8,128)(2,1)S(1)}, bf16[1,4,64,256]{3,2,1,0:T(8,128)(2,1)S(1)}, u32[]{:S(2)}, u32[]{:S(2)}) %collective-permute-start.4) | collective-permute-done | bytes 131104 | tf_op jit(solution)/shard_map/ppermute | solution.py:51
  23.2 0.2 shard_map.55
  23.3 1.6 %collective-permute-start.6 = (bf16[1,64,256]{2,1,0:T(8,128)(2,1)S(1)}, bf16[1,64,256]{2,1,0:T(8,128)(2,1)S(1)}, u32[]{:S(2)}, u32[]{:S(2)}) collective-permute-start(bf16[1,64,256]{2,1,0:T(8,128)(2,1)S(1)} %shard_map.55), channel_id=1, source_target_pairs={{0,1},{1,0},{2,3},{3,2},{4,5},{5,4},{6,7},{7,6},{8,9},{9,8},{10,11... | collective-permute-start | bytes 98312 | tf_op jit(solution)/shard_map/ppermute | solution.py:34
  24.9 1.2 %shard_map.54 = (bf16[1,4,64,256]{3,2,1,0:T(8,128)(2,1)}, f32[1,64,256]{2,1,0:T(8,128)S(1)}) custom-call(bf16[1,4,64,256]{3,2,1,0:T(8,128)(2,1)S(1)} %collective-permute-done.3.odd_field, bf16[1,4,64,256]{3,2,1,0:T(8,128)(2,1)S(1)} %collective-permute-done.4.even_field, bf16[3,3,768,256]{3,2,1,0:T(8,128)(2,1)S(1)} %copy-done, ...), custom_call_target="tpu_custom_call" | custom-call | flops 301989888 | bytes 4063232 | tf_op jit(solution)/shard_map/pallas_call | solution.py:371
  26.1 1.2 %collective-permute-done.6.added = bf16[1,64,256]{2,1,0:T(8,128)(2,1)S(1)} collective-permute-done((bf16[1,64,256]{2,1,0:T(8,128)(2,1)S(1)}, bf16[1,64,256]{2,1,0:T(8,128)(2,1)S(1)}, u32[]{:S(2)}, u32[]{:S(2)}) %collective-permute-start.6) | collective-permute-done | bytes 32800 | tf_op jit(solution)/shard_map/ppermute | solution.py:34
  27.3 0.7 %shard_map.56 = bf16[1,4,64,256]{3,2,1,0:T(8,128)(2,1)} custom-call(f32[1,64,256]{2,1,0:T(8,128)S(1)} %get-tuple-element.32.ends, bf16[1,64,256]{2,1,0:T(8,128)(2,1)S(1)} %collective-permute-done.6.added, bf16[1,4,64,256]{3,2,1,0:T(8,128)(2,1)} %get-tuple-element.34._), custom_call_target="tpu_custom_call", output_to_operand_aliasing={{}: (2, {})} | custom-call | flops 18874368 | bytes 229376 | tf_op jit(solution)/shard_map/pallas_call | solution.py:371
  (2 shorter events, 0.0 us)
Async XLA Ops:
  0.0 1.0 %copy-start.3 = (bf16[2,8,128,128]{3,2,1,0:T(8,128)(2,1)S(1)}, bf16[2,8,128,128]{3,2,1,0:T(8,128)(2,1)}, u32[]{:S(2)}) copy-start(bf16[2,8,128,128]{3,2,1,0:T(8,128)(2,1)} %frames.1) | copy-start | bytes 1572868
  0.0 4.9 %copy-start.1 = (bf16[3,3,384,128]{3,2,1,0:T(8,128)(2,1)S(1)}, bf16[3,3,384,128]{3,2,1,0:T(8,128)(2,1)}, u32[]{:S(2)}) copy-start(bf16[3,3,384,128]{3,2,1,0:T(8,128)(2,1)} %weight.11) | copy-start | bytes 2654212
  0.0 9.7 %collective-permute-start.1 = (bf16[2,8,128,128]{3,2,1,0:T(8,128)(2,1)}, bf16[2,8,128,128]{3,2,1,0:T(8,128)(2,1)S(1)}, u32[]{:S(2)}, u32[]{:S(2)}) collective-permute-start(bf16[2,8,128,128]{3,2,1,0:T(8,128)(2,1)} %frames.1), channel_id=1, source_target_pairs={{0,2},{2,4},{4,6},{6,8},{8,10},{10,12},{12,14},{14,16},{16,18},{18... | collective-permute-start | bytes 1572872 | tf_op jit(solution)/shard_map/ppermute | solution.py:28
  1.1 6.0 %collective-permute-start.2 = (bf16[2,2,128,128]{3,2,1,0:T(8,128)(2,1)S(1)}, bf16[2,2,128,128]{3,2,1,0:T(8,128)(2,1)S(1)}, u32[]{:S(2)}, u32[]{:S(2)}) collective-permute-start(bf16[2,2,128,128]{3,2,1,0:T(8,128)(2,1)S(1)} %shard_map.47), channel_id=1, source_target_pairs={{0,1},{1,0},{2,3},{3,2},{4,5},{5,4},{6,7},{7,6},{8,9},{9,8},{10,11... | collective-permute-start | bytes 393224 | tf_op jit(solution)/shard_map/ppermute | solution.py:34
  2.6 9.4 %collective-permute-start = (bf16[2,2,128,128]{3,2,1,0:T(8,128)(2,1)S(1)}, bf16[2,2,128,128]{3,2,1,0:T(8,128)(2,1)S(1)}, u32[]{:S(2)}, u32[]{:S(2)}) collective-permute-start(bf16[2,2,128,128]{3,2,1,0:T(8,128)(2,1)S(1)} %shard_map.47), channel_id=1, source_target_pairs={{0,3},{1,2},{2,5},{3,4},{4,7},{5,6},{6,9},{7,8},{8,11},{9,10},{10,... | collective-permute-start | bytes 393224 | tf_op jit(solution)/shard_map/ppermute | solution.py:34
  7.5 4.5 %copy-start.2 = (bf16[3,384,256]{2,1,0:T(8,128)(2,1)S(1)}, bf16[3,384,256]{2,1,0:T(8,128)(2,1)}, u32[]{:S(2)}) copy-start(bf16[3,384,256]{2,1,0:T(8,128)(2,1)} %down.1) | copy-start | bytes 1769476
  9.7 4.1 %copy-start = (bf16[3,3,768,256]{3,2,1,0:T(8,128)(2,1)S(1)}, bf16[3,3,768,256]{3,2,1,0:T(8,128)(2,1)}, u32[]{:S(2)}) copy-start(bf16[3,3,768,256]{3,2,1,0:T(8,128)(2,1)} %weight.15) | copy-start | bytes 10616836
  13.2 1.2 %collective-permute-start.3 = (bf16[1,4,64,256]{3,2,1,0:T(8,128)(2,1)S(1)}, bf16[1,4,64,256]{3,2,1,0:T(8,128)(2,1)S(1)}, u32[]{:S(2)}, u32[]{:S(2)}) collective-permute-start(bf16[1,4,64,256]{3,2,1,0:T(8,128)(2,1)S(1)} %shard_map.51.field), channel_id=1, source_target_pairs={{2,6},{6,10},{10,14},{14,18},{18,22},{22,26},{26,30},{0,0},{4,4},{... | collective-permute-start | bytes 393224 | tf_op jit(solution)/shard_map/ppermute | solution.py:40
  14.4 3.9 %collective-permute-start.5 = (bf16[1,4,64,256]{3,2,1,0:T(8,128)(2,1)S(1)}, bf16[1,4,64,256]{3,2,1,0:T(8,128)(2,1)S(1)}, u32[]{:S(2)}, u32[]{:S(2)}) collective-permute-start(bf16[1,4,64,256]{3,2,1,0:T(8,128)(2,1)S(1)} %collective-permute-done.3.odd_field), channel_id=1, source_target_pairs={{0,2},{2,0},{4,6},{6,4},{8,10},{10,8},{12,14},{14,12},{16,18},{18,... | collective-permute-start | bytes 393224 | tf_op jit(solution)/shard_map/ppermute | solution.py:55
  17.3 5.9 %collective-permute-start.4 = (bf16[1,4,64,256]{3,2,1,0:T(8,128)(2,1)S(1)}, bf16[1,4,64,256]{3,2,1,0:T(8,128)(2,1)S(1)}, u32[]{:S(2)}, u32[]{:S(2)}) collective-permute-start(bf16[1,4,64,256]{3,2,1,0:T(8,128)(2,1)S(1)} %shard_map.51.field), channel_id=1, source_target_pairs={{0,4},{1,5},{4,8},{5,9},{8,12},{9,13},{12,16},{13,17},{16,20},{17,... | collective-permute-start | bytes 393224 | tf_op jit(solution)/shard_map/ppermute | solution.py:51
  23.3 4.0 %collective-permute-start.6 = (bf16[1,64,256]{2,1,0:T(8,128)(2,1)S(1)}, bf16[1,64,256]{2,1,0:T(8,128)(2,1)S(1)}, u32[]{:S(2)}, u32[]{:S(2)}) collective-permute-start(bf16[1,64,256]{2,1,0:T(8,128)(2,1)S(1)} %shard_map.55), channel_id=1, source_target_pairs={{0,1},{1,0},{2,3},{3,2},{4,5},{5,4},{6,7},{7,6},{8,9},{9,8},{10,11... | collective-permute-start | bytes 98312 | tf_op jit(solution)/shard_map/ppermute | solution.py:34

commit v12 on v11

--- a/solution.py
+++ b/solution.py
@@ -268,28 +268,38 @@
         pooled[i, :cols] = line
 
 
-def reduce_kernel(above, below, weight, sums, down, out, pooled):
+def reduced_rows(lines, firsts, half_cols, down, pooled):
+    put_pooled(pooled, lines)
+    taps = down_taps(pooled, half_cols)
+    left = [jnp.concatenate(taps[i : i + 3], axis=1) for i in firsts]
+    right = down[...].reshape(-1, down.shape[-1])
+    rows = jnp.dot(jnp.concatenate(left, axis=0), right, preferred_element_type=F32)
+    return rows.astype(BF16).reshape(len(firsts), half_cols, -1)
+
+
+def inner_kernel(sums, down, out, pooled):
+    count, half_cols, _ = out.shape
+    cols = 2 * half_cols
+    lines = [pool(sums[r * cols : (r + 1) * cols]) for r in range(2, 2 * count + 3)]
+    out[...] = reduced_rows(lines, range(0, 2 * count, 2), half_cols, down, pooled)
+
+
+def reduce_kernel(above, below, weight, sums, inner, down, out, pooled):
     cols = above.shape[2]
     rows = sums.shape[0] // cols - 1
-    half_rows, half_cols = rows // 2, cols // 2
     added = halo_sum(above, below, weight, 0, rows)
     lines = []
-    for r in range(rows + 1):
+    for r in (0, 1, 2, rows - 2, rows - 1, rows):
         line = sums[r * cols : (r + 1) * cols]
         for k, halo_r in enumerate((0, rows - 1, rows)):
             if r == halo_r:
                 line = line + added[k * cols : (k + 1) * cols]
         line = pool(line)
         lines.append(jnp.where(has_below(), line, 0.0) if r == rows else line)
-    put_pooled(pooled, lines)
-    taps = down_taps(pooled, half_cols)
-    left = [jnp.concatenate(taps[2 * p : 2 * p + 3], axis=1) for p in range(half_rows)]
-    own = jnp.dot(
-        jnp.concatenate(left, axis=0),
-        down[...].reshape(-1, down.shape[-1]),
-        preferred_element_type=F32,
-    )
-    out[0] = own.astype(BF16).reshape(half_rows, half_cols, -1)
+    ends = reduced_rows(lines, (0, 3), cols // 2, down, pooled)
+    out[0, 0] = ends[0]
+    out[0, 1 : rows // 2 - 1] = inner[...]
+    out[0, rows // 2 - 1] = ends[1]
 
 
 def column_taps(flat, cols):
@@ -402,13 +412,22 @@
     half_rows, half_cols = rows // 2, cols // 2
     shape = jax.ShapeDtypeStruct((1, half_rows, half_cols, wide), BF16)
     fine_sums = call(fine_rest_kernel, pair, [], flops, (earlier, conv_fine, own, halo))
-    above_1, below_1, fine_sums = lax.optimization_barrier((above_1, below_1, fine_sums))
+    inner = call(
+        inner_kernel,
+        jax.ShapeDtypeStruct((half_rows - 2, half_cols, wide), BF16),
+        [pltpu.VMEM((rows - 3, cols + 8, channels), F32)],
+        flops // 4,
+        (fine_sums, conv_down),
+    )
+    above_1, below_1, fine_sums, inner = lax.optimization_barrier(
+        (above_1, below_1, fine_sums, inner)
+    )
     field = call(
         reduce_kernel,
         shape,
-        [pltpu.VMEM((rows + 1, cols + 8, channels), F32)],
+        [pltpu.VMEM((6, cols + 8, channels), F32)],
         flops // 3,
-        (above_1, below_1, conv_fine, fine_sums, conv_down),
+        (above_1, below_1, conv_fine, fine_sums, inner, conv_down),
     )
     sides = 1 if strips == 2 else 2
     sums = jax.ShapeDtypeStruct((half_rows * half_cols, wide), F32)

time: 28.2 us -> 28.3 us (level)
  waiting for transfers between devices: 9.62 us -> 9.19 us
  starting transfers between devices: 9.68 us -> 10.1 us
    ppermute x3, waiting for transfers between devices: 2.76 us -> 2.32 us  [swapped(): return lax.ppermute(value, ('tm', 'rows'), pairs)]
    ppermute x1, starting transfers between devices: 2.88 us -> 3.3 us  [paired(): lax.ppermute(value, 'tm', [(t, t ^ 1) for t in range(lax.axis_size('tm'))])]
    pallas_call x11 -> x12, Pallas kernels: 7.53 us -> 7.66 us  [call(): pl.pallas_call(kernel, out_shape=out_shape, in_specs=[vmem] * (len(args)...]
  transfers between devices with their start and end apart: 7 -> 7, of which waited for: 6 -> 6; matrix products, arithmetic and copies ran while one was open for 0% -> 0% of each run, Pallas kernels for 20% -> 21%
where the time goes in v12:
time: 28.3 us; the launch traced here: 28.1 us
  starting transfers between devices  10.1 us (36%)
  waiting for transfers between devices  9.19 us (32%)
  Pallas kernels  7.66 us (27%)
  local copies, waits for them, and re-layouts  1.04 us (4%)
    pallas_call x12, Pallas kernels, call(): pl.pallas_call(kernel, out_shape=out_shape, in_specs=[vmem] * (len(args)...  7.66 us
    ppermute x3, starting transfers between devices, swapped(): return lax.ppermute(value, ('tm', 'rows'), pairs)  5.48 us
    ppermute x1, waiting for transfers between devices, even_ahead(): lax.ppermute(value, ('tm', 'rows'), [(t * rows + r, u * rows + q) for t,...  4.36 us
    ppermute x1, starting transfers between devices, paired(): lax.ppermute(value, 'tm', [(t, t ^ 1) for t in range(lax.axis_size('tm'))])  3.3 us
    ppermute x3, waiting for transfers between devices, swapped(): return lax.ppermute(value, ('tm', 'rows'), pairs)  2.32 us
    ppermute x1, waiting for transfers between devices, ring(): return lax.ppermute(value, 'tm', [(t, (t + steps) % tm) for t in range(tm)])  2.17 us
    unnamed x8, local copies, waits for them, and re-layouts  1.04 us
    ppermute x1, starting transfers between devices, odd_ahead(): return lax.ppermute(value, 'tm', pairs)  0.67 us
  transfers between devices with their start and end apart: 7, of which 6 were waited for; matrix products, arithmetic and copies ran while one was open for 0% of the time, Pallas kernels for 21%

profile of v12, /device:TPU:16, one launch (start us, length us, event | category | flops | bytes accessed | tf_op | source)
XLA Modules:
  0.0 28.1 jit_solution(17651950456625591698)
XLA Ops:
  0.0 0.0 copy-start.3
  0.0 0.0 copy-start.2
  0.0 0.0 collective-permute-start.1
  0.0 1.0 %copy-done.3 = bf16[2,8,128,128]{3,2,1,0:T(8,128)(2,1)S(1)} copy-done((bf16[2,8,128,128]{3,2,1,0:T(8,128)(2,1)S(1)}, bf16[2,8,128,128]{3,2,1,0:T(8,128)(2,1)}, u32[]{:S(2)}) %copy-start.3) | copy-done | bytes 524312
  1.1 1.6 %collective-permute-start.2 = (bf16[2,2,128,128]{3,2,1,0:T(8,128)(2,1)S(1)}, bf16[2,2,128,128]{3,2,1,0:T(8,128)(2,1)S(1)}, u32[]{:S(2)}, u32[]{:S(2)}) collective-permute-start(bf16[2,2,128,128]{3,2,1,0:T(8,128)(2,1)S(1)} %shard_map.47), channel_id=1, source_target_pairs={{0,1},{1,0},{2,3},{3,2},{4,5},{5,4},{6,7},{7,6},{8,9},{9,8},{10,11... | collective-permute-start | bytes 393224 | tf_op jit(solution)/shard_map/ppermute | solution.py:34
  2.6 2.3 %collective-permute-start = (bf16[2,2,128,128]{3,2,1,0:T(8,128)(2,1)S(1)}, bf16[2,2,128,128]{3,2,1,0:T(8,128)(2,1)S(1)}, u32[]{:S(2)}, u32[]{:S(2)}) collective-permute-start(bf16[2,2,128,128]{3,2,1,0:T(8,128)(2,1)S(1)} %shard_map.47), channel_id=1, source_target_pairs={{0,3},{1,2},{2,5},{3,4},{4,7},{5,6},{6,9},{7,8},{8,11},{9,10},{10,... | collective-permute-start | bytes 393224 | tf_op jit(solution)/shard_map/ppermute | solution.py:34
  5.0 0.0 copy-done.2
  5.0 1.5 %shard_map.48.own = f32[1152,256]{1,0:T(8,128)S(1)} custom-call(bf16[2,8,128,128]{3,2,1,0:T(8,128)(2,1)S(1)} %copy-done.3, bf16[3,3,384,128]{3,2,1,0:T(8,128)(2,1)S(1)} %copy-done.2), custom_call_target="tpu_custom_call" | custom-call | flops 1358954496 | bytes 1409024 | tf_op jit(solution)/shard_map/pallas_call | solution.py:381
  6.5 0.6 %collective-permute-done.2.above.below = bf16[2,2,128,128]{3,2,1,0:T(8,128)(2,1)S(1)} collective-permute-done((bf16[2,2,128,128]{3,2,1,0:T(8,128)(2,1)S(1)}, bf16[2,2,128,128]{3,2,1,0:T(8,128)(2,1)S(1)}, u32[]{:S(2)}, u32[]{:S(2)}) %collective-permute-start.2) | collective-permute-done | bytes 131104 | tf_op jit(solution)/shard_map/ppermute | solution.py:34
  7.1 0.4 %shard_map.49.halo = f32[384,256]{1,0:T(8,128)S(1)} custom-call(bf16[2,2,128,128]{3,2,1,0:T(8,128)(2,1)S(1)} %collective-permute-done.2.above.below, bf16[2,2,128,128]{3,2,1,0:T(8,128)(2,1)S(1)} %collective-permute-done.2.above.below, bf16[3,3,384,128]{3,2,1,0:T(8,128)(2,1)S(1)} %copy-done.2), custom_call_target="tpu_custom_call" | custom-call | flops 452984832 | bytes 1146880 | tf_op jit(solution)/shard_map/pallas_call | solution.py:381
  7.5 0.0 copy-start.1
  7.5 2.2 %collective-permute-done.1.frames = bf16[2,8,128,128]{3,2,1,0:T(8,128)(2,1)S(1)} collective-permute-done((bf16[2,8,128,128]{3,2,1,0:T(8,128)(2,1)}, bf16[2,8,128,128]{3,2,1,0:T(8,128)(2,1)S(1)}, u32[]{:S(2)}, u32[]{:S(2)}) %collective-permute-start.1) | collective-permute-done | bytes 524320 | tf_op jit(solution)/shard_map/ppermute | solution.py:28
  9.7 1.4 %shard_map.50.sums = f32[1152,256]{1,0:T(8,128)S(1)} custom-call(bf16[2,8,128,128]{3,2,1,0:T(8,128)(2,1)S(1)} %collective-permute-done.1.frames, bf16[3,3,384,128]{3,2,1,0:T(8,128)(2,1)S(1)} %copy-done.2, f32[1152,256]{1,0:T(8,128)S(1)} %shard_map.48.own, f32[384,256]{1,0:T(8,128)S(1)} %shard_map.49.halo), custom_call_target="tpu_custom_call" | custom-call | flops 1358954496 | bytes 2981888 | tf_op jit(solution)/shard_map/pallas_call | solution.py:381
  11.1 0.0 copy-done.1
  11.1 0.0 copy-start
  11.2 0.4 %shard_map.51.inner = bf16[2,64,256]{2,1,0:T(8,128)(2,1)S(1)} custom-call(f32[1152,256]{1,0:T(8,128)S(1)} %shard_map.50.sums, bf16[3,384,256]{2,1,0:T(8,128)(2,1)S(1)} %copy-done.1), custom_call_target="tpu_custom_call" | custom-call | flops 339738624 | bytes 1769472 | tf_op jit(solution)/shard_map/pallas_call | solution.py:381
  11.6 0.5 %collective-permute-done.above.below = bf16[2,2,128,128]{3,2,1,0:T(8,128)(2,1)S(1)} collective-permute-done((bf16[2,2,128,128]{3,2,1,0:T(8,128)(2,1)S(1)}, bf16[2,2,128,128]{3,2,1,0:T(8,128)(2,1)S(1)}, u32[]{:S(2)}, u32[]{:S(2)}) %collective-permute-start) | collective-permute-done | bytes 131104 | tf_op jit(solution)/shard_map/ppermute | solution.py:34
  12.1 0.8 %shard_map.52.field = bf16[1,4,64,256]{3,2,1,0:T(8,128)(2,1)S(1)} custom-call(bf16[2,2,128,128]{3,2,1,0:T(8,128)(2,1)S(1)} %collective-permute-done.above.below, bf16[2,2,128,128]{3,2,1,0:T(8,128)(2,1)S(1)} %collective-permute-done.above.below, bf16[3,3,384,128]{3,2,1,0:T(8,128)(2,1)S(1)} %copy-done.2, f32[1152,256]{1,0:T(8,128)S(1)} %shard_map.50.sums, ...), custom_call_target="tpu_custom_call" | custom-call | flops 452984832 | bytes 2981888 | tf_op jit(solution)/shard_map/pallas_call | solution.py:381
  12.9 0.7 %collective-permute-start.3 = (bf16[1,4,64,256]{3,2,1,0:T(8,128)(2,1)S(1)}, bf16[1,4,64,256]{3,2,1,0:T(8,128)(2,1)S(1)}, u32[]{:S(2)}, u32[]{:S(2)}) collective-permute-start(bf16[1,4,64,256]{3,2,1,0:T(8,128)(2,1)S(1)} %shard_map.52.field), channel_id=1, source_target_pairs={{2,6},{6,10},{10,14},{14,18},{18,22},{22,26},{26,30},{0,0},{4,4},{... | collective-permute-start | bytes 393224 | tf_op jit(solution)/shard_map/ppermute | solution.py:40
  13.6 0.0 copy-done
  13.6 0.5 %shard_map.53 = (f32[256,256]{1,0:T(8,128)S(1)}, f32[1,64,256]{2,1,0:T(8,128)S(1)}) custom-call(bf16[1,4,64,256]{3,2,1,0:T(8,128)(2,1)S(1)} %shard_map.52.field, bf16[3,3,768,256]{3,2,1,0:T(8,128)(2,1)S(1)} %copy-done), custom_call_target="tpu_custom_call" | custom-call | flops 301989888 | bytes 3670016 | tf_op jit(solution)/shard_map/pallas_call | solution.py:381
  14.1 0.0 collective-permute-done.3.odd_field
  14.1 3.3 %collective-permute-start.5 = (bf16[1,4,64,256]{3,2,1,0:T(8,128)(2,1)S(1)}, bf16[1,4,64,256]{3,2,1,0:T(8,128)(2,1)S(1)}, u32[]{:S(2)}, u32[]{:S(2)}) collective-permute-start(bf16[1,4,64,256]{3,2,1,0:T(8,128)(2,1)S(1)} %collective-permute-done.3.odd_field), channel_id=1, source_target_pairs={{0,2},{2,0},{4,6},{6,4},{8,10},{10,8},{12,14},{14,12},{16,18},{18,... | collective-permute-start | bytes 393224 | tf_op jit(solution)/shard_map/ppermute | solution.py:55
  17.4 0.6 %collective-permute-start.4 = (bf16[1,4,64,256]{3,2,1,0:T(8,128)(2,1)S(1)}, bf16[1,4,64,256]{3,2,1,0:T(8,128)(2,1)S(1)}, u32[]{:S(2)}, u32[]{:S(2)}) collective-permute-start(bf16[1,4,64,256]{3,2,1,0:T(8,128)(2,1)S(1)} %shard_map.52.field), channel_id=1, source_target_pairs={{0,4},{1,5},{4,8},{5,9},{8,12},{9,13},{12,16},{13,17},{16,20},{17,... | collective-permute-start | bytes 393224 | tf_op jit(solution)/shard_map/ppermute | solution.py:51
  18.1 0.3 %collective-permute-done.5.field = bf16[1,4,64,256]{3,2,1,0:T(8,128)(2,1)S(1)} collective-permute-done((bf16[1,4,64,256]{3,2,1,0:T(8,128)(2,1)S(1)}, bf16[1,4,64,256]{3,2,1,0:T(8,128)(2,1)S(1)}, u32[]{:S(2)}, u32[]{:S(2)}) %collective-permute-start.5) | collective-permute-done | bytes 131104 | tf_op jit(solution)/shard_map/ppermute | solution.py:55
  18.4 0.5 %shard_map.54 = (f32[256,256]{1,0:T(8,128)S(1)}, f32[1,64,256]{2,1,0:T(8,128)S(1)}) custom-call(bf16[1,4,64,256]{3,2,1,0:T(8,128)(2,1)S(1)} %collective-permute-done.5.field, bf16[3,3,768,256]{3,2,1,0:T(8,128)(2,1)S(1)} %copy-done, f32[256,256]{1,0:T(8,128)S(1)} %get-tuple-element.28.body_in, f32[1,64,256]{2,1,0:T(8,128)S(1)} %get-tuple-element.29.ends_in), custom_call_target="tpu_custom_call" | custom-call | flops 301989888 | bytes 3997696 | tf_op jit(solution)/shard_map/pallas_call | solution.py:381
  18.9 4.4 %collective-permute-done.4.even_field = bf16[1,4,64,256]{3,2,1,0:T(8,128)(2,1)S(1)} collective-permute-done((bf16[1,4,64,256]{3,2,1,0:T(8,128)(2,1)S(1)}, bf16[1,4,64,256]{3,2,1,0:T(8,128)(2,1)S(1)}, u32[]{:S(2)}, u32[]{:S(2)}) %collective-permute-start.4) | collective-permute-done | bytes 131104 | tf_op jit(solution)/shard_map/ppermute | solution.py:51
  23.3 0.2 shard_map.56
  23.5 1.6 %collective-permute-start.6 = (bf16[1,64,256]{2,1,0:T(8,128)(2,1)S(1)}, bf16[1,64,256]{2,1,0:T(8,128)(2,1)S(1)}, u32[]{:S(2)}, u32[]{:S(2)}) collective-permute-start(bf16[1,64,256]{2,1,0:T(8,128)(2,1)S(1)} %shard_map.56), channel_id=1, source_target_pairs={{0,1},{1,0},{2,3},{3,2},{4,5},{5,4},{6,7},{7,6},{8,9},{9,8},{10,11... | collective-permute-start | bytes 98312 | tf_op jit(solution)/shard_map/ppermute | solution.py:34
  25.1 1.2 %shard_map.55 = (bf16[1,4,64,256]{3,2,1,0:T(8,128)(2,1)}, f32[1,64,256]{2,1,0:T(8,128)S(1)}) custom-call(bf16[1,4,64,256]{3,2,1,0:T(8,128)(2,1)S(1)} %collective-permute-done.3.odd_field, bf16[1,4,64,256]{3,2,1,0:T(8,128)(2,1)S(1)} %collective-permute-done.4.even_field, bf16[3,3,768,256]{3,2,1,0:T(8,128)(2,1)S(1)} %copy-done, ...), custom_call_target="tpu_custom_call" | custom-call | flops 301989888 | bytes 4063232 | tf_op jit(solution)/shard_map/pallas_call | solution.py:381
  26.2 1.2 %collective-permute-done.6.added = bf16[1,64,256]{2,1,0:T(8,128)(2,1)S(1)} collective-permute-done((bf16[1,64,256]{2,1,0:T(8,128)(2,1)S(1)}, bf16[1,64,256]{2,1,0:T(8,128)(2,1)S(1)}, u32[]{:S(2)}, u32[]{:S(2)}) %collective-permute-start.6) | collective-permute-done | bytes 32800 | tf_op jit(solution)/shard_map/ppermute | solution.py:34
  27.5 0.7 %shard_map.57 = bf16[1,4,64,256]{3,2,1,0:T(8,128)(2,1)} custom-call(f32[1,64,256]{2,1,0:T(8,128)S(1)} %get-tuple-element.34.ends, bf16[1,64,256]{2,1,0:T(8,128)(2,1)S(1)} %collective-permute-done.6.added, bf16[1,4,64,256]{3,2,1,0:T(8,128)(2,1)} %get-tuple-element.36._), custom_call_target="tpu_custom_call", output_to_operand_aliasing={{}: (2, {})} | custom-call | flops 18874368 | bytes 229376 | tf_op jit(solution)/shard_map/pallas_call | solution.py:381
  (2 shorter events, 0.0 us)
Async XLA Ops:
  0.0 1.0 %copy-start.3 = (bf16[2,8,128,128]{3,2,1,0:T(8,128)(2,1)S(1)}, bf16[2,8,128,128]{3,2,1,0:T(8,128)(2,1)}, u32[]{:S(2)}) copy-start(bf16[2,8,128,128]{3,2,1,0:T(8,128)(2,1)} %frames.1) | copy-start | bytes 1572868
  0.0 4.9 %copy-start.2 = (bf16[3,3,384,128]{3,2,1,0:T(8,128)(2,1)S(1)}, bf16[3,3,384,128]{3,2,1,0:T(8,128)(2,1)}, u32[]{:S(2)}) copy-start(bf16[3,3,384,128]{3,2,1,0:T(8,128)(2,1)} %weight.11) | copy-start | bytes 2654212
  0.0 9.7 %collective-permute-start.1 = (bf16[2,8,128,128]{3,2,1,0:T(8,128)(2,1)}, bf16[2,8,128,128]{3,2,1,0:T(8,128)(2,1)S(1)}, u32[]{:S(2)}, u32[]{:S(2)}) collective-permute-start(bf16[2,8,128,128]{3,2,1,0:T(8,128)(2,1)} %frames.1), channel_id=1, source_target_pairs={{0,2},{2,4},{4,6},{6,8},{8,10},{10,12},{12,14},{14,16},{16,18},{18... | collective-permute-start | bytes 1572872 | tf_op jit(solution)/shard_map/ppermute | solution.py:28
  1.1 6.0 %collective-permute-start.2 = (bf16[2,2,128,128]{3,2,1,0:T(8,128)(2,1)S(1)}, bf16[2,2,128,128]{3,2,1,0:T(8,128)(2,1)S(1)}, u32[]{:S(2)}, u32[]{:S(2)}) collective-permute-start(bf16[2,2,128,128]{3,2,1,0:T(8,128)(2,1)S(1)} %shard_map.47), channel_id=1, source_target_pairs={{0,1},{1,0},{2,3},{3,2},{4,5},{5,4},{6,7},{7,6},{8,9},{9,8},{10,11... | collective-permute-start | bytes 393224 | tf_op jit(solution)/shard_map/ppermute | solution.py:34
  2.6 9.4 %collective-permute-start = (bf16[2,2,128,128]{3,2,1,0:T(8,128)(2,1)S(1)}, bf16[2,2,128,128]{3,2,1,0:T(8,128)(2,1)S(1)}, u32[]{:S(2)}, u32[]{:S(2)}) collective-permute-start(bf16[2,2,128,128]{3,2,1,0:T(8,128)(2,1)S(1)} %shard_map.47), channel_id=1, source_target_pairs={{0,3},{1,2},{2,5},{3,4},{4,7},{5,6},{6,9},{7,8},{8,11},{9,10},{10,... | collective-permute-start | bytes 393224 | tf_op jit(solution)/shard_map/ppermute | solution.py:34
  7.5 3.6 %copy-start.1 = (bf16[3,384,256]{2,1,0:T(8,128)(2,1)S(1)}, bf16[3,384,256]{2,1,0:T(8,128)(2,1)}, u32[]{:S(2)}) copy-start(bf16[3,384,256]{2,1,0:T(8,128)(2,1)} %down.3) | copy-start | bytes 1769476
  11.1 2.4 %copy-start = (bf16[3,3,768,256]{3,2,1,0:T(8,128)(2,1)S(1)}, bf16[3,3,768,256]{3,2,1,0:T(8,128)(2,1)}, u32[]{:S(2)}) copy-start(bf16[3,3,768,256]{3,2,1,0:T(8,128)(2,1)} %weight.15) | copy-start | bytes 10616836
  12.9 1.2 %collective-permute-start.3 = (bf16[1,4,64,256]{3,2,1,0:T(8,128)(2,1)S(1)}, bf16[1,4,64,256]{3,2,1,0:T(8,128)(2,1)S(1)}, u32[]{:S(2)}, u32[]{:S(2)}) collective-permute-start(bf16[1,4,64,256]{3,2,1,0:T(8,128)(2,1)S(1)} %shard_map.52.field), channel_id=1, source_target_pairs={{2,6},{6,10},{10,14},{14,18},{18,22},{22,26},{26,30},{0,0},{4,4},{... | collective-permute-start | bytes 393224 | tf_op jit(solution)/shard_map/ppermute | solution.py:40
  14.1 4.3 %collective-permute-start.5 = (bf16[1,4,64,256]{3,2,1,0:T(8,128)(2,1)S(1)}, bf16[1,4,64,256]{3,2,1,0:T(8,128)(2,1)S(1)}, u32[]{:S(2)}, u32[]{:S(2)}) collective-permute-start(bf16[1,4,64,256]{3,2,1,0:T(8,128)(2,1)S(1)} %collective-permute-done.3.odd_field), channel_id=1, source_target_pairs={{0,2},{2,0},{4,6},{6,4},{8,10},{10,8},{12,14},{14,12},{16,18},{18,... | collective-permute-start | bytes 393224 | tf_op jit(solution)/shard_map/ppermute | solution.py:55
  17.4 5.9 %collective-permute-start.4 = (bf16[1,4,64,256]{3,2,1,0:T(8,128)(2,1)S(1)}, bf16[1,4,64,256]{3,2,1,0:T(8,128)(2,1)S(1)}, u32[]{:S(2)}, u32[]{:S(2)}) collective-permute-start(bf16[1,4,64,256]{3,2,1,0:T(8,128)(2,1)S(1)} %shard_map.52.field), channel_id=1, source_target_pairs={{0,4},{1,5},{4,8},{5,9},{8,12},{9,13},{12,16},{13,17},{16,20},{17,... | collective-permute-start | bytes 393224 | tf_op jit(solution)/shard_map/ppermute | solution.py:51
  23.5 4.0 %collective-permute-start.6 = (bf16[1,64,256]{2,1,0:T(8,128)(2,1)S(1)}, bf16[1,64,256]{2,1,0:T(8,128)(2,1)S(1)}, u32[]{:S(2)}, u32[]{:S(2)}) collective-permute-start(bf16[1,64,256]{2,1,0:T(8,128)(2,1)S(1)} %shard_map.56), channel_id=1, source_target_pairs={{0,1},{1,0},{2,3},{3,2},{4,5},{5,4},{6,7},{7,6},{8,9},{9,8},{10,11... | collective-permute-start | bytes 98312 | tf_op jit(solution)/shard_map/ppermute | solution.py:34
